TPU v7x, 32 devices: a whole 2x2x4 slice. The times are simulated.
32 devices in a mesh: groups: 2 (over y), tm: 4 (over z), space: 2 (over x), chan: 2 (over core).
Axes of the slice: x: 2, y: 2, z: 4, core: 2. Of those that a mesh axis runs over, the one named last changes fastest.
Arguments:
- frames: bfloat16 [32, 64, 64, 256], P(('groups', 'tm'), 'chan', 'space'), parts along dimension 0, may hold values from -6 to 6
- conv_taps: float32 [64, 9], P('chan'), may hold values from -2 to 2
- pooling: float32 [64, 256], P('space'), may hold values from -0.0625 to 0.0625
- gain_matrix: float32 [256, 128], P(None, ('space', 'chan')), may hold values from -0.5 to 0.5
- transition: float32 [256, 256], replicated, as said below
- update_map: float32 [256, 256], replicated, as said below
- quiet_root: float32 [256, 256], replicated, as said below
- observed_root: float32 [256, 256], replicated, as said below
- init_mean: float32 [512], P('groups'), parts along dimension 0, may hold values from -6 to 6
- init_root: float32 [512, 256], P('groups'), parts along dimension 0, as said below
- observed: int32 [32], P(('groups', 'tm')), parts along dimension 0, may hold values 0 or 1
Outputs:
- filtered_means: float32 [32, 256], P(('groups', 'tm')), parts along dimension 0
- block_roots: float32 [8, 256, 256], P(('groups', 'tm')), parts along dimension 0
- tap_gradient: float32 [8, 64, 9], P(('groups', 'tm'), 'chan'), parts along dimension 0
There are 2 independent parts, one for each index of `groups`. A program takes and returns all parts, laid end to end along the dimension named above; an argument that names none is the same for every part. Nothing has to cross between parts.
Inputs may be any that keep to these rules, and one draw needn't show every extreme that they name: transition and update_map are upper triangular, with the same diagonal entries where these exceed 0.8. transition is upper triangular. `quiet_root`: upper triangular with a positive diagonal. `observed_root`: upper triangular with a positive diagonal. `init_root`: upper triangular with a positive diagonal.
All inputs are finite; a program needn't handle non-finite values. No bound on the sum of `observed` on one device may be relied on, other than what follows from the above.
Results may differ from a plain program's by a relative error of at most 0.0003.
Values may be sent and summed in bfloat16 or wider, within the bound.
No kernel may reach another device: no remote copies, remote signals or barrier semaphores. Data moves between devices by JAX's collectives and lax.ppermute only.
A program may use at most 64 MiB of HBM per device.

v0:
```python
import jax
import jax.numpy as jnp
from jax import lax
from jax.sharding import PartitionSpec as P

DILATION_STEP = 2


precise = lax.Precision.HIGHEST


def extended(block, sides, width):
    for axis, dim in sides:
        count = lax.axis_size(axis)
        forward = [(i, i + 1) for i in range(count - 1)]
        backward = [(target, source) for source, target in forward]
        low = lax.ppermute(
            lax.slice_in_dim(block, block.shape[dim] - width, None, axis=dim), axis, forward
        )
        high = lax.ppermute(lax.slice_in_dim(block, 0, width, axis=dim), axis, backward)
        block = jnp.concatenate([low, block, high], axis=dim)
    return block


def prefix(value, axis, join, neutral):
    count, mine = (lax.axis_size(axis), lax.axis_index(axis))
    pieces = jax.tree.map(lambda part: lax.all_gather(part, axis), value)
    running = jax.tree.map(
        lambda part, zero: jnp.full_like(part, 0) + jnp.asarray(zero, part.dtype), value, neutral
    )

    def turn(position, running):
        longer = join(running, jax.tree.map(lambda part: part[position], pieces))
        return jax.tree.map(lambda new, old: jnp.where(position < mine, new, old), longer, running)

    return lax.fori_loop(0, count - 1, turn, running)


def gram_of(root_matrix):
    return jnp.dot(
        root_matrix.T, root_matrix, precision=precise, preferred_element_type=jnp.float32
    )


def merge_elements(earlier, later):
    first_map, first_shift, first_gram = earlier
    second_map, second_shift, second_gram = later
    joined_map = jnp.dot(
        second_map, first_map, precision=precise, preferred_element_type=jnp.float32
    )
    joined_shift = (
        jnp.dot(second_map, first_shift, precision=precise, preferred_element_type=jnp.float32)
        + second_shift
    )
    carried = jnp.dot(second_map, first_gram, precision=precise, preferred_element_type=jnp.float32)
    joined_gram = (
        jnp.dot(carried, second_map.T, precision=precise, preferred_element_type=jnp.float32)
        + second_gram
    )
    return (joined_map, joined_shift, joined_gram)


def local(
    frames,
    conv_taps,
    pooling,
    gain_matrix,
    transition,
    update_map,
    quiet_root,
    observed_root,
    init_mean,
    init_root,
    observed,
):
    step_count, channels, row_tiles, column_list = frames.shape
    width_state = transition.shape[0]
    extended_frame = extended(frames, (("space", 2),), DILATION_STEP)
    extended_frame = jnp.pad(
        extended_frame, ((0, 0), (0, 0), (0, 0), (DILATION_STEP, DILATION_STEP))
    ).astype(jnp.float32)
    window_views = [
        extended_frame[
            :,
            :,
            left_element * DILATION_STEP : left_element * DILATION_STEP + row_tiles,
            right_element * DILATION_STEP : right_element * DILATION_STEP + column_list,
        ]
        for left_element in range(3)
        for right_element in range(3)
    ]
    response = jnp.zeros(frames.shape, jnp.float32)
    for k in range(9):
        response = response + conv_taps[:, k][None, :, None, None] * window_views[k]
    weights = observed.astype(jnp.float32)
    tile_sums = jnp.einsum("tchw,hw->tc", response, pooling, precision=precise)
    gain_part = (
        jnp.dot(tile_sums, gain_matrix.T, precision=precise, preferred_element_type=jnp.float32)
        * weights[:, None]
    )
    shifts = lax.psum(gain_part, ("space", "chan"))
    scaling = weights / (row_tiles * lax.axis_size("space") * column_list)
    grad_local = jnp.stack(
        [
            jnp.sum(response * window_views[k] * scaling[:, None, None, None], axis=(0, 2, 3))
            for k in range(9)
        ],
        axis=1,
    )
    tap_gradient = lax.psum(grad_local, "space")[None]
    is_seen = observed > 0
    step_maps = jnp.where(is_seen[:, None, None], update_map[None], transition[None])
    observed_gram = gram_of(observed_root)
    quiet_gram = gram_of(quiet_root)
    step_grams = jnp.where(is_seen[:, None, None], observed_gram[None], quiet_gram[None])
    unit_matrix = jnp.eye(width_state, dtype=jnp.float32)
    block_map, block_shift, block_gram = (step_maps[0], shifts[0], step_grams[0])
    for j in range(1, step_count):
        block_map, block_shift, block_gram = merge_elements(
            (block_map, block_shift, block_gram), (step_maps[j], shifts[j], step_grams[j])
        )
    identity = (
        unit_matrix,
        jnp.zeros((width_state,), jnp.float32),
        jnp.zeros((width_state, width_state), jnp.float32),
    )
    before = prefix((block_map, block_shift, block_gram), "tm", merge_elements, identity)
    state = merge_elements((unit_matrix, init_mean, gram_of(init_root)), before)
    mean_now = state[1]
    mean_list = []
    for j in range(step_count):
        mean_now = (
            jnp.dot(step_maps[j], mean_now, precision=precise, preferred_element_type=jnp.float32)
            + shifts[j]
        )
        mean_list.append(mean_now)
    filtered_means = jnp.stack(mean_list, axis=0)
    final_state = merge_elements(state, (block_map, block_shift, block_gram))
    block_roots = jnp.linalg.cholesky(final_state[2]).T[None]
    return (filtered_means, block_roots, tap_gradient)


def solution(mesh):
    return jax.shard_map(
        local,
        mesh=mesh,
        in_specs=(
            P(("groups", "tm"), "chan", "space", None),
            P("chan", None),
            P("space", None),
            P(None, ("space", "chan")),
            P(),
            P(),
            P(),
            P(),
            P("groups"),
            P("groups", None),
            P(("groups", "tm")),
        ),
        out_specs=(
            P(("groups", "tm"), None),
            P(("groups", "tm"), None, None),
            P(("groups", "tm"), "chan", None),
        ),
        check_vma=False,
    )
```

profile of v0, /device:TPU:0, one launch (start us, length us, event | category | flops | bytes accessed | tf_op | source)
XLA Modules:
  0.0 149.7 jit_solution(7803377094408503304)
XLA Ops:
  7.2 1.1 copy.24
  8.3 1.1 copy.25
  9.4 0.6 fusion.51
  10.0 1.7 %fusion.52 = f32[256,256]{0,1:T(8,128)S(1)} fusion(f32[256,256]{1,0:T(8,128)} %param.19), kind=kOutput, calls=%fused_computation.112 | convolution fusion | flops 201326592 | bytes 524288 | tf_op jit(solution)/shard_map/dot_general | solution.py:40
  11.7 0.7 broadcast_compare_fusion
  12.6 0.6 fusion.28
  13.2 0.6 convolution_add_fusion.5
  13.8 0.6 fusion.38
  14.4 0.6 convolution_add_fusion.4
  15.0 0.6 fusion.34
  15.7 1.3 convolution_add_fusion.3
  17.0 1.4 fusion.49
  18.5 4.9 %collective-permute-start = (bf16[4,32,2,256]{3,2,1,0:T(2,128)(2,1)S(1)}, bf16[4,32,2,256]{3,2,1,0:T(2,128)(2,1)S(1)}, u32[]{:S(2)}, u32[]{:S(2)}) collective-permute-start(bf16[4,32,2,256]{3,2,1,0:T(2,128)(2,1)S(1)} %get-tuple-element.222), channel_id=1, source_target_pairs={{0,2},{1,3},{4,6},{5,7},{8,10},{9,11},{12,14},{13,15},{16,18},{17,... | collective-permute-start | bytes 393224 | tf_op jit(solution)/shard_map/ppermute | solution.py:17
  23.4 1.5 collective-permute-start.1
  24.8 0.6 fusion.32
  25.4 0.6 fusion.40
  26.0 1.3 fusion.36
  27.4 1.3 fusion.54
  28.8 1.4 collective-permute-done.1
  30.2 4.8 %fusion.27 = f32[4,32,36,260]{3,2,1,0:T(8,128)S(1)} fusion(bf16[4,32,2,256]{3,2,1,0:T(2,128)(2,1)S(1)} %collective-permute-done.1, bf16[4,32,32,256]{3,2,1,0:T(8,128)(2,1)} %param.13, bf16[4,32,2,256]{3,2,1,0:T(2,128)(2,1)S(1)} %collective-permute-done), kind=kLoop, calls=%fused_computation.44 | loop fusion | flops 14376960 | bytes 7151616 | tf_op jit(solution)/shard_map/convert_element_type | solution.py:81
  35.1 11.3 %multiply_reduce_fusion = (f32[32]{0:T(128)S(1)}, f32[32]{0:T(128)S(1)}, f32[32]{0:T(128)S(1)}, f32[32]{0:T(128)S(1)}, f32[32]{0:T(128)S(1)}, /*index=5*/f32[32]...) fusion(f32[4,32,36,260]{3,2,1,0:T(8,128)S(1)} %fusion.27, ...), kind=kLoop, calls=%fused_computation.32 | loop fusion | flops 46137056 | bytes 41945360 | tf_op jit(solution)/shard_map/reduce_sum | solution.py:105
  46.4 5.0 %psum.15 = f32[1,32,9]{1,2,0:T(8,128)S(1)} all-reduce(f32[1,32,9]{1,2,0:T(8,128)S(1)} %bitcast.197), channel_id=1, replica_groups=mesh['groups'=2,'tm'=4,'space'=2,'chan'=2] {'space'}, use_global_device_ids=true, to_apply=%region_16.17 | all-reduce | flops 288 | bytes 2304 | tf_op jit(solution)/shard_map/psum | solution.py:110
  51.4 0.6 copy.33
  52.0 12.1 %fusion.23 = f32[1,4,32,1]{2,0,3,1:T(1,128)S(1)} fusion(f32[4,32,32,256]{3,2,1,0:T(8,128)} %get-tuple-element.221, f32[32,256,1,1]{1,0,2,3:T(8,128)S(1)} %bitcast.196), kind=kOutput, calls=%fused_computation.30 | convolution fusion | flops 12582912 | bytes 4227584 | tf_op jit(solution)/shard_map/tchw,hw->tc/dot_general | solution.py:96
  64.2 6.1 %psum.14 = f32[4,256]{1,0:T(4,128)S(1)} all-reduce(f32[4,256]{1,0:T(4,128)S(1)} %convolution_multiply_fusion), channel_id=1, replica_groups=mesh['groups'=2,'tm'=4,'space'=2,'chan'=2] {'space','chan'}, use_global_device_ids=true, to_apply=%region_0.1 | all-reduce | flops 1024 | bytes 8192 | tf_op jit(solution)/shard_map/psum | solution.py:101
  71.1 11.2 %all-gather.3 = f32[4,1,256]{2,1,0:T(1,128)S(1)} all-gather(f32[1,1,256]{2,1,0:T(1,128)S(1)} %bitcast.222), channel_id=3, replica_groups=mesh['groups'=2,'tm'=4,'space'=2,'chan'=2] {'tm'}, dimensions={0}, use_global_device_ids=true | all-gather | bytes 5120 | tf_op jit(solution)/shard_map/all_gather | solution.py:27
  82.3 1.6 %copy.41 = f32[1024,256]{1,0:T(8,128)S(1)} copy(f32[1024,256]{0,1:T(8,128)} %all-gather.9.cloned.1.call-done) | data formatting | bytes 2097152
  83.9 16.7 %while.18 = (s32[]{:T(128)}, f32[256,256]{1,0:T(8,128)S(1)}, f32[256]{0:T(256)S(1)}, f32[256,256]{1,0:T(8,128)S(1)}, s32[]{:T(128)}, /*index=5*/f32[4,256,256]{2...) while((s32[]{:T(128)}, f32[256,256]{1,0:T(8,128)S(1)}, ...), condition=%wide.region_2.3_spmd.clone, body=%wide.region_1.2_spmd.clone.sunk | while | flops 605094912 | bytes 3945090 | solution.py:36
  83.9 1.4 fusion.113
  85.3 1.4 fusion.114
  86.7 1.2 fusion.112
  88.0 1.3 convolution_select_fusion.2
  89.4 1.3 fusion.113
  90.7 1.4 fusion.114
  92.1 1.2 fusion.112
  93.5 1.3 convolution_select_fusion.2
  94.8 1.3 fusion.113
  96.2 1.4 fusion.114
  97.6 1.2 fusion.112
  98.9 1.3 convolution_select_fusion.2
  100.5 1.3 fusion.55
  102.7 1.4 convolution_add_fusion.1
  104.3 11.7 %cholesky.49 = f32[128,128]{1,0:T(8,128)S(1)} custom-call(f32[128,128]{1,0:T(8,128)S(1)} %cholesky.115), custom_call_target="Cholesky" | custom-call | tf_op jit(solution)/shard_map/jit(cholesky)/cholesky | solution.py:139
  116.0 9.8 %custom-call.11 = f32[1,128,128]{1,2,0:T(8,128)S(1)} custom-call(f32[1,128,128]{2,1,0:T(8,128)S(1)} %get-tuple-element.227), custom_call_target="InvertDiagBlocksLowerTriangular" | custom-call | tf_op jit(solution)/shard_map/jit(cholesky)/cholesky | solution.py:139
  126.3 11.7 %cholesky.103 = f32[128,128]{1,0:T(8,128)S(1)} custom-call(f32[128,128]{1,0:T(8,128)S(1)} %convolution_subtract_fusion), custom_call_target="Cholesky" | custom-call | tf_op jit(solution)/shard_map/jit(cholesky)/cholesky | solution.py:139
  138.1 0.6 compare_reduce_fusion
  140.0 0.8 copy.32
  142.2 0.6 pad_maximum_fusion
  (73 shorter events, 4.4 us)
Async XLA Ops:
  7.2 2.3 %copy-start = (f32[256,256]{1,0:T(8,128)S(1)}, f32[256,256]{1,0:T(8,128)}, u32[]{:S(2)}) copy-start(f32[256,256]{1,0:T(8,128)} %param.20) | copy-start | bytes 786436
  7.2 75.1 %all-gather.9.cloned.1.call-start = ((), (), s32[]{:S(2)}) async-start(), calls=%async_computation.1 | async-start | bytes 1310720 | tf_op jit(solution)/shard_map/all_gather | solution.py:27
  13.2 14.2 %copy-start.4 = (f32[32,9]{0,1:T(8,128)S(1)}, f32[32,9]{0,1:T(8,128)}, u32[]{:S(2)}) copy-start(f32[32,9]{0,1:T(8,128)} %param.14) | copy-start | bytes 3460
  13.2 14.2 %copy-start.2 = (f32[256,256]{1,0:T(8,128)S(1)}, f32[256,256]{1,0:T(8,128)}, u32[]{:S(2)}) copy-start(f32[256,256]{1,0:T(8,128)} %param.22) | copy-start | bytes 786436
  13.8 14.9 %copy-start.7 = (s32[4]{0:T(128)S(1)}, s32[4]{0:T(128)}, u32[]{:S(2)}) copy-start(s32[4]{0:T(128)} %param.23) | copy-start | bytes 52
  17.0 66.8 %all-gather.7.cloned.1.call-start = ((), (), s32[]{:S(2)}) async-start(), calls=%async_computation | async-start | bytes 1310720 | tf_op jit(solution)/shard_map/all_gather | solution.py:27
  18.5 10.3 %collective-permute-start = (bf16[4,32,2,256]{3,2,1,0:T(2,128)(2,1)S(1)}, bf16[4,32,2,256]{3,2,1,0:T(2,128)(2,1)S(1)}, u32[]{:S(2)}, u32[]{:S(2)}) collective-permute-start(bf16[4,32,2,256]{3,2,1,0:T(2,128)(2,1)S(1)} %get-tuple-element.222), channel_id=1, source_target_pairs={{0,2},{1,3},{4,6},{5,7},{8,10},{9,11},{12,14},{13,15},{16,18},{17,... | collective-permute-start | bytes 393224 | tf_op jit(solution)/shard_map/ppermute | solution.py:17
  23.4 6.9 %collective-permute-start.1 = (bf16[4,32,2,256]{3,2,1,0:T(2,128)(2,1)S(1)}, bf16[4,32,2,256]{3,2,1,0:T(2,128)(2,1)S(1)}, u32[]{:S(2)}, u32[]{:S(2)}) collective-permute-start(bf16[4,32,2,256]{3,2,1,0:T(2,128)(2,1)S(1)} %get-tuple-element.223), channel_id=1, source_target_pairs={{2,0},{3,1},{6,4},{7,5},{10,8},{11,9},{14,12},{15,13},{18,16},{19,... | collective-permute-start | bytes 393224 | tf_op jit(solution)/shard_map/ppermute | solution.py:20
  35.1 16.9 %copy-start.3 = (f32[32,256]{1,0:T(8,128)S(1)}, f32[32,256]{1,0:T(8,128)}, u32[]{:S(2)}) copy-start(f32[32,256]{1,0:T(8,128)} %param.15) | copy-start | bytes 98308
  46.3 17.8 %copy-start.6 = (f32[256,32]{0,1:T(8,128)S(1)}, f32[256,32]{0,1:T(8,128)}, u32[]{:S(2)}) copy-start(f32[256,32]{0,1:T(8,128)} %param.16) | copy-start | bytes 98308
  83.8 18.4 %copy-start.1 = (f32[256,256]{1,0:T(8,128)S(1)}, f32[256,256]{1,0:T(8,128)}, u32[]{:S(2)}) copy-start(f32[256,256]{1,0:T(8,128)} %fusion.36) | copy-start | bytes 786436
  100.5 40.4 %copy-start.5 = (f32[256]{0:T(256)S(1)}, f32[256]{0:T(256)}, u32[]{:S(2)}) copy-start(f32[256]{0:T(256)} %param.21) | copy-start | bytes 3076
Sparse Core Ops, SparseCore 0:
  17.1 30.6 all-gather.8
  50.0 27.3 all-gather.6
where the time goes:
time: 151 us; the launch traced here: 150 us
  other arithmetic  51.8 us (34%)
  matrix products  44.4 us (29%)
  blocking collectives  22.3 us (15%)
  between operations  15.8 us (10%)
  local copies, waits for them, and re-layouts  7.1 us (5%)
  starting transfers between devices  6.43 us (4%)
    another operation x6, other arithmetic, local(): block_roots = jnp.linalg.cholesky(final_state[2]).T[None]  33.9 us
    dot_general x1, matrix products, local(): tile_sums = jnp.einsum('tchw,hw->tc', response, pooling, precision=precise)  12.1 us
    reduce_sum x1, other arithmetic, local(): jnp.sum(response * window_views[k] * scaling[:, None, None, None], axis=(...  11.3 us
    all_gather x1, blocking collectives, prefix(): pieces = jax.tree.map(lambda part: lax.all_gather(part, axis), value)  11.2 us
    dot_general x8, matrix products, merge_elements(): jnp.dot(carried, second_map.T, precision=precise, preferred_element_type=...  8.5 us
    dot_general x8, matrix products, merge_elements(): jnp.dot(second_map, first_gram, precision=precise, preferred_element_type...  7.54 us
    dot_general x6, matrix products, merge_elements(): jnp.dot(second_map, first_map, precision=precise, preferred_element_type=...  6.5 us
    psum x1, blocking collectives, local(): shifts = lax.psum(gain_part, ('space', 'chan'))  6.1 us
  transfers between devices with their start and end apart: 4, of which 1 were waited for; matrix products, arithmetic and copies ran while one was open for 24% of the time, Pallas kernels for 0%

commit v1 on v0

v1 whole, which is shorter than its diff:
```python
import jax
import jax.numpy as jnp
from jax import lax
from jax.experimental import pallas as pl
from jax.experimental.pallas import tpu as pltpu
from jax.sharding import PartitionSpec as P

DILATION_STEP = 2
PANEL = 32
GROUP = 8
LANES = 128
F32 = jnp.float32
BF16 = jnp.bfloat16

precise = lax.Precision.HIGHEST


def extended(block, axis, dim, width):
    count = lax.axis_size(axis)
    forward = [(i, i + 1) for i in range(count - 1)]
    backward = [(target, source) for source, target in forward]
    low = lax.ppermute(
        lax.slice_in_dim(block, block.shape[dim] - width, None, axis=dim), axis, forward
    )
    high = lax.ppermute(lax.slice_in_dim(block, 0, width, axis=dim), axis, backward)
    return jnp.concatenate([low, block, high], axis=dim)


def history(own, axis):
    count = lax.axis_size(axis)
    held = own
    reach = 1
    while reach < count:
        pairs = [(i, i + reach) for i in range(count - reach)]
        held = jnp.concatenate([held, lax.ppermute(held, axis, pairs)], axis=0)
        reach *= 2
    return held


def split(x):
    high = x.astype(BF16)
    return high, (x - high.astype(F32)).astype(BF16)


def contract(a, b, dims):
    return lax.dot_general(a, b, (dims, ((), ())), preferred_element_type=F32)


def three_pass(a, b, dims):
    return (
        contract(a[0], b[0], dims)
        + contract(a[0], b[1], dims)
        + contract(a[1], b[0], dims)
    )


NN = ((1,), (0,))
NT = ((1,), (1,))
TN = ((0,), (0,))


def prepare_kernel(
    transition, update_map, quiet_root, observed_root, init_root,
    map_high, map_low, grams, first_gram,
):
    for which, ref in ((0, transition), (1, update_map)):
        high, low = split(ref[...])
        map_high[which] = high
        map_low[which] = low
    for which, ref in ((0, quiet_root), (1, observed_root)):
        pair = split(ref[...])
        grams[which] = three_pass(pair, pair, TN)
    pair = split(init_root[...])
    first_gram[...] = three_pass(pair, pair, TN)


def prepare(transition, update_map, quiet_root, observed_root, init_root):
    size = transition.shape[0]
    return pl.pallas_call(
        prepare_kernel,
        out_shape=(
            jax.ShapeDtypeStruct((2, size, size), BF16),
            jax.ShapeDtypeStruct((2, size, size), BF16),
            jax.ShapeDtypeStruct((2, size, size), F32),
            jax.ShapeDtypeStruct((size, size), F32),
        ),
        name="prepare",
    )(transition, update_map, quiet_root, observed_root, init_root)


def upper_factor(gram, out, high, low):
    size = gram.shape[0]
    halves = size // LANES
    tile = (GROUP, LANES)
    zero = jnp.zeros(tile, F32)
    sub = lax.broadcasted_iota(jnp.int32, tile, 0)
    lane = lax.broadcasted_iota(jnp.int32, tile, 1)
    count = PANEL // GROUP
    for top in range(0, size, PANEL):
        first = top // LANES
        start = first * LANES
        panel = gram[top : top + PANEL, start:]
        if top:
            left = (high[:top, top : top + PANEL], low[:top, top : top + PANEL])
            panel = panel - three_pass(left, (high[:top, start:], low[:top, start:]), TN)
        places = range(halves - first)
        part = [
            [
                panel[GROUP * i : GROUP * (i + 1), LANES * h : LANES * (h + 1)]
                for h in places
            ]
            for i in range(count)
        ]
        done = [[zero for _ in places] for _ in range(count)]
        for g in range(count):
            base = top + GROUP * g
            here, at = base // LANES - first, base % LANES
            live = range(here, halves - first)
            column = {
                i: [
                    jnp.broadcast_to(part[i][here][:, at + j : at + j + 1], tile)
                    for j in range(GROUP)
                ]
                for i in range(g, count)
            }
            pivot = {
                (j, m): jnp.broadcast_to(column[g][m][j : j + 1, :], tile)
                for j in range(GROUP)
                for m in range(j, GROUP)
            }
            factor, scale = {}, []
            for j in range(GROUP):
                scale.append(lax.rsqrt(pivot[j, j]))
                for m in range(j + 1, GROUP):
                    factor[j, m] = pivot[j, m] * scale[j]
                for i in range(j + 1, GROUP):
                    for m in range(i, GROUP):
                        pivot[i, m] = pivot[i, m] - factor[j, i] * factor[j, m]
            rows = {}
            for h in live:
                rows[h] = []
                for j in range(GROUP):
                    value = jnp.broadcast_to(part[g][h][j : j + 1, :], tile)
                    for i in range(j):
                        value = value - factor[i, j] * rows[h][i]
                    rows[h].append(value * scale[j])
                value = rows[h][0]
                for j in range(1, GROUP):
                    value = jnp.where(sub == j, rows[h][j], value)
                if h == here:
                    value = jnp.where(lane - at >= sub, value, 0.0)
                done[g][h] = value
            for i in range(g + 1, count):
                left = []
                for j in range(GROUP):
                    value = column[i][j]
                    for m in range(j):
                        value = value - factor[m, j] * left[m]
                    left.append(value * scale[j])
                for h in live:
                    value = part[i][h]
                    for j in range(GROUP):
                        value = value - left[j] * rows[h][j]
                    part[i][h] = value
        for i in range(count):
            low_row = top + GROUP * i
            for h in range(halves):
                value = done[i][h - first] if h >= first else zero
                out[low_row : low_row + GROUP, LANES * h : LANES * (h + 1)] = value
        if top + PANEL < size:
            rows_high, rows_low = split(out[top : top + PANEL, :])
            high[top : top + PANEL, :] = rows_high
            low[top : top + PANEL, :] = rows_low


def covariance_kernel(steps, place, flags, map_high, map_low, grams, first_gram, out, gram, high, low):
    index = place[0]
    gram[...] = first_gram[...]

    def step(t, carry):
        flag = flags[(index - t // steps) * steps + t % steps]
        map_pair = (map_high[flag], map_low[flag])
        carried = three_pass(map_pair, split(gram[...]), NN)
        gram[...] = three_pass(split(carried), map_pair, NT) + grams[flag]
        return carry

    lax.fori_loop(0, (index + 1) * steps, step, 0)
    upper_factor(gram, out, high, low)


def covariance(place, flags, steps, map_high, map_low, grams, first_gram):
    size = first_gram.shape[0]
    vmem = pl.BlockSpec(memory_space=pltpu.VMEM)
    smem = pl.BlockSpec(memory_space=pltpu.SMEM)

    def kernel(*refs):
        covariance_kernel(steps, *refs)

    return pl.pallas_call(
        kernel,
        out_shape=jax.ShapeDtypeStruct((size, size), F32),
        in_specs=[smem, smem, vmem, vmem, vmem, vmem],
        out_specs=vmem,
        scratch_shapes=[
            pltpu.VMEM((size, size), F32),
            pltpu.VMEM((size, size), BF16),
            pltpu.VMEM((size, size), BF16),
        ],
        name="covariance",
    )(place, flags, map_high, map_low, grams, first_gram)


def means_kernel(steps, place, flags, map_high, map_low, shifts, init_mean, out):
    index = place[0]
    size = init_mean.shape[1]

    def step(t, mean):
        at = (index - t // steps) * steps + t % steps
        flag = flags[at]
        mean = three_pass(split(mean), (map_high[flag], map_low[flag]), NT)
        mean = mean + jnp.broadcast_to(shifts[pl.ds(at, 1), :], mean.shape)

        @pl.when(t // steps == index)
        def _():
            out[pl.ds(t % steps, 1), :] = mean[0:1]

        return mean

    lax.fori_loop(
        0, (index + 1) * steps, step, jnp.broadcast_to(init_mean[...], (GROUP, size))
    )


def means(place, flags, steps, map_high, map_low, shifts, init_mean):
    size = init_mean.shape[0]
    vmem = pl.BlockSpec(memory_space=pltpu.VMEM)
    smem = pl.BlockSpec(memory_space=pltpu.SMEM)

    def kernel(*refs):
        means_kernel(steps, *refs)

    return pl.pallas_call(
        kernel,
        out_shape=jax.ShapeDtypeStruct((steps, size), F32),
        in_specs=[smem, smem, vmem, vmem, vmem, vmem],
        out_specs=vmem,
        name="means",
    )(place, flags, map_high, map_low, shifts, init_mean[None])


def local(
    frames,
    conv_taps,
    pooling,
    gain_matrix,
    transition,
    update_map,
    quiet_root,
    observed_root,
    init_mean,
    init_root,
    observed,
):
    step_count, channels, row_tiles, column_list = frames.shape
    place = lax.axis_index("tm").astype(jnp.int32)[None]
    flags = history(observed, "tm")
    extended_frame = extended(frames, "space", 2, DILATION_STEP)
    map_high, map_low, grams, first_gram = prepare(
        transition, update_map, quiet_root, observed_root, init_root
    )
    extended_frame = jnp.pad(
        extended_frame, ((0, 0), (0, 0), (0, 0), (DILATION_STEP, DILATION_STEP))
    ).astype(jnp.float32)
    window_views = [
        extended_frame[
            :,
            :,
            left_element * DILATION_STEP : left_element * DILATION_STEP + row_tiles,
            right_element * DILATION_STEP : right_element * DILATION_STEP + column_list,
        ]
        for left_element in range(3)
        for right_element in range(3)
    ]
    response = jnp.zeros(frames.shape, jnp.float32)
    for k in range(9):
        response = response + conv_taps[:, k][None, :, None, None] * window_views[k]
    weights = observed.astype(jnp.float32)
    tile_sums = jnp.einsum("tchw,hw->tc", response, pooling, precision=precise)
    gain_part = (
        jnp.dot(tile_sums, gain_matrix.T, precision=precise, preferred_element_type=jnp.float32)
        * weights[:, None]
    )
    shifts = lax.psum(gain_part, ("space", "chan"))
    scaling = weights / (row_tiles * lax.axis_size("space") * column_list)
    grad_local = jnp.stack(
        [
            jnp.sum(response * window_views[k] * scaling[:, None, None, None], axis=(0, 2, 3))
            for k in range(9)
        ],
        axis=1,
    )
    tap_gradient = lax.psum(grad_local, "space")[None]
    all_shifts = history(shifts, "tm")
    root = covariance(place, flags, step_count, map_high, map_low, grams, first_gram)
    filtered_means = means(place, flags, step_count, map_high, map_low, all_shifts, init_mean)
    return (filtered_means, root[None], tap_gradient)


def solution(mesh):
    return jax.shard_map(
        local,
        mesh=mesh,
        in_specs=(
            P(("groups", "tm"), "chan", "space", None),
            P("chan", None),
            P("space", None),
            P(None, ("space", "chan")),
            P(),
            P(),
            P(),
            P(),
            P("groups"),
            P("groups", None),
            P(("groups", "tm")),
        ),
        out_specs=(
            P(("groups", "tm"), None),
            P(("groups", "tm"), None, None),
            P(("groups", "tm"), "chan", None),
        ),
        check_vma=False,
    )
```

time: 151 us -> 88.3 us (0.58)
  the two profiles are of different devices: /device:TPU:0 before, /device:TPU:28 now
where the time goes in v1:
time: 88.3 us; the launch traced here: 87.8 us
  Pallas kernels  28.9 us (33%)
  other arithmetic  17.9 us (20%)
  blocking collectives  12.2 us (14%)
  matrix products  10.4 us (12%)
  starting transfers between devices  9.83 us (11%)
  waiting for transfers between devices  4.69 us (5%)
  local copies, waits for them, and re-layouts  3.06 us (3%)
    pallas_call x1, Pallas kernels, covariance(): pl.pallas_call(kernel, out_shape=jax.ShapeDtypeStruct((size, size), F32),...  20.3 us
    reduce_sum x1, other arithmetic, local(): jnp.sum(response * window_views[k] * scaling[:, None, None, None], axis=(...  10.5 us
    dot_general x1, matrix products, local(): tile_sums = jnp.einsum('tchw,hw->tc', response, pooling, precision=precise)  10.3 us
    psum x1, blocking collectives, local(): shifts = lax.psum(gain_part, ('space', 'chan'))  7.21 us
    pallas_call x1, Pallas kernels, means(): pl.pallas_call(kernel, out_shape=jax.ShapeDtypeStruct((steps, size), F32)...  5.7 us
    ppermute x4, starting transfers between devices, history(): held = jnp.concatenate([held, lax.ppermute(held, axis, pairs)], axis=0)  5.13 us
    psum x1, blocking collectives, local(): tap_gradient = lax.psum(grad_local, 'space')[None]  4.99 us
    convert_element_type x1, other arithmetic, local(): extended_frame = jnp.pad(extended_frame, ((0, 0), (0, 0), (0, 0), (DILATI...  4.85 us
  transfers between devices with their start and end apart: 6, of which 2 were waited for; matrix products, arithmetic and copies ran while one was open for 33% of the time, Pallas kernels for 26%

profile of v1, /device:TPU:28, one launch (start us, length us, event | category | flops | bytes accessed | tf_op | source)
XLA Modules:
  0.0 87.8 jit_solution(5420503309712879893)
XLA Ops:
  0.6 0.0 copy-start
  0.6 1.4 %fusion.10 = (bf16[4,32,2,256]{3,2,1,0:T(2,128)(2,1)S(1)}, bf16[4,32,2,256]{3,2,1,0:T(2,128)(2,1)S(1)}) fusion(bf16[4,32,32,256]{3,2,1,0:T(8,128)(2,1)} %param.11), kind=kLoop, calls=%fused_computation.37 | loop fusion | bytes 524288 | tf_op jit(solution)/shard_map/slice | solution.py:23
  2.1 3.4 %collective-permute-start.2 = (bf16[4,32,2,256]{3,2,1,0:T(2,128)(2,1)S(1)}, bf16[4,32,2,256]{3,2,1,0:T(2,128)(2,1)S(1)}, u32[]{:S(2)}, u32[]{:S(2)}) collective-permute-start(bf16[4,32,2,256]{3,2,1,0:T(2,128)(2,1)S(1)} %get-tuple-element.24), channel_id=1, source_target_pairs={{0,2},{1,3},{4,6},{5,7},{8,10},{9,11},{12,14},{13,15},{16,18},{17,... | collective-permute-start | bytes 393224 | tf_op jit(solution)/shard_map/ppermute | solution.py:22
  5.5 1.3 %collective-permute-start.3 = (bf16[4,32,2,256]{3,2,1,0:T(2,128)(2,1)S(1)}, bf16[4,32,2,256]{3,2,1,0:T(2,128)(2,1)S(1)}, u32[]{:S(2)}, u32[]{:S(2)}) collective-permute-start(bf16[4,32,2,256]{3,2,1,0:T(2,128)(2,1)S(1)} %get-tuple-element.25), channel_id=1, source_target_pairs={{2,0},{3,1},{6,4},{7,5},{10,8},{11,9},{14,12},{15,13},{18,16},{19,... | collective-permute-start | bytes 393224 | tf_op jit(solution)/shard_map/ppermute | solution.py:25
  6.8 1.3 %collective-permute-start = (s32[4]{0:T(128)}, s32[4]{0:T(128)S(1)}, u32[]{:S(2)}, u32[]{:S(2)}) collective-permute-start(s32[4]{0:T(128)} %param.21), channel_id=1, source_target_pairs={{0,4},{4,8},{8,12},{1,5},{5,9},{9,13},{2,6},{6,10},{10,14},{3,7},{... | collective-permute-start | bytes 56 | tf_op jit(solution)/shard_map/ppermute | solution.py:35
  8.1 0.7 convert_element_type.9
  8.7 1.0 %slice_bitcast_fusion.8 = (f32[32]{0:T(128)S(1)}, f32[32]{0:T(128)S(1)}, f32[32]{0:T(128)S(1)}, f32[32]{0:T(128)S(1)}, f32[32]{0:T(128)S(1)}, /*index=5*/f32[32]...) fusion(f32[32,9]{0,1:T(8,128)} %param.12), kind=kLoop, calls=%fused_computation.35 | loop fusion | bytes 2304 | tf_op jit(solution)/shard_map/mul | solution.py:286
  9.7 2.9 %prepare.1 = (bf16[2,256,256]{2,1,0:T(8,128)(2,1)}, bf16[2,256,256]{2,1,0:T(8,128)(2,1)}, f32[2,256,256]{2,1,0:T(8,128)}, f32[256,256]{1,0:T(8,128)}) custom-call(f32[256,256]{1,0:T(8,128)} %transition.1, f32[256,256]{1,0:T(8,128)} %update_map.1, f32[256,256]{1,0:T(8,128)} %quiet_root.1, f32[256,256]{1,0:T(8,128)} %observed_root.1, f32[256,256]{1,0:T(8,128)} %init_root.1), custom_call_target="tpu_custom_call" | custom-call | tf_op jit(solution)/shard_map/prepare/pallas_call | solution.py:79
  12.6 0.7 broadcast_multiply_fusion
  13.3 0.0 collective-permute-done.2
  13.3 0.0 collective-permute-done.3
  13.3 4.9 %fusion.8 = f32[4,32,36,260]{3,2,1,0:T(8,128)S(1)} fusion(bf16[4,32,2,256]{3,2,1,0:T(2,128)(2,1)S(1)} %collective-permute-done.3, bf16[4,32,32,256]{3,2,1,0:T(8,128)(2,1)} %param.11, bf16[4,32,2,256]{3,2,1,0:T(2,128)(2,1)S(1)} %collective-permute-done.2), kind=kLoop, calls=%fused_computation.20 | loop fusion | flops 14376960 | bytes 7151616 | tf_op jit(solution)/shard_map/convert_element_type | solution.py:273
  18.1 10.5 %multiply_reduce_fusion = (f32[32]{0:T(128)S(1)}, f32[32]{0:T(128)S(1)}, f32[32]{0:T(128)S(1)}, f32[32]{0:T(128)S(1)}, f32[32]{0:T(128)S(1)}, /*index=5*/f32[32]...) fusion(f32[4,32,36,260]{3,2,1,0:T(8,128)S(1)} %fusion.8, ...), kind=kLoop, calls=%fused_computation.8 | loop fusion | flops 46137056 | bytes 41945360 | tf_op jit(solution)/shard_map/reduce_sum | solution.py:297
  28.6 0.0 copy-start.2
  28.6 0.0 copy-start.1
  28.6 0.0 copy-done
  28.6 10.3 %fusion.4 = f32[1,4,32,1]{2,0,3,1:T(1,128)S(1)} fusion(f32[4,32,32,256]{3,2,1,0:T(8,128)S(1)} %get-tuple-element.23, f32[32,256,1,1]{1,0,2,3:T(8,128)S(1)} %bitcast.37), kind=kOutput, calls=%fused_computation.6 | convolution fusion | flops 12582912 | bytes 4227584 | tf_op jit(solution)/shard_map/tchw,hw->tc/dot_general | solution.py:288
  39.0 0.0 copy-done.2
  39.0 0.1 convolution_multiply_fusion
  39.1 7.2 %psum.14 = f32[4,256]{1,0:T(4,128)S(1)} all-reduce(f32[4,256]{1,0:T(4,128)S(1)} %convolution_multiply_fusion), channel_id=1, replica_groups=mesh['groups'=2,'tm'=4,'space'=2,'chan'=2] {'space','chan'}, use_global_device_ids=true, to_apply=%region_0.1 | all-reduce | flops 1024 | bytes 8192 | tf_op jit(solution)/shard_map/psum | solution.py:293
  46.3 1.3 %collective-permute-start.4 = (f32[4,256]{1,0:T(4,128)S(1)}, f32[4,256]{1,0:T(4,128)S(1)}, u32[]{:S(2)}, u32[]{:S(2)}) collective-permute-start(f32[4,256]{1,0:T(4,128)S(1)} %psum.14), channel_id=1, source_target_pairs={{0,4},{4,8},{8,12},{1,5},{5,9},{9,13},{2,6},{6,10},{10,14},{3,7},{... | collective-permute-start | bytes 12296 | tf_op jit(solution)/shard_map/ppermute | solution.py:35
  47.6 0.0 collective-permute-done
  47.6 0.0 copy-done.1
  47.6 0.1 pad_add_fusion
  47.7 1.3 %collective-permute-start.1 = (s32[8]{0:T(128)S(1)}, s32[8]{0:T(128)S(1)}, u32[]{:S(2)}, u32[]{:S(2)}) collective-permute-start(s32[8]{0:T(128)S(1)} %pad_add_fusion), channel_id=1, source_target_pairs={{0,8},{4,12},{1,9},{5,13},{2,10},{6,14},{3,11},{7,15},{16,24},{20,... | collective-permute-start | bytes 104 | tf_op jit(solution)/shard_map/ppermute | solution.py:35
  49.0 3.2 %collective-permute-done.4 = f32[4,256]{1,0:T(4,128)S(1)} collective-permute-done((f32[4,256]{1,0:T(4,128)S(1)}, f32[4,256]{1,0:T(4,128)S(1)}, u32[]{:S(2)}, u32[]{:S(2)}) %collective-permute-start.4) | collective-permute-done | bytes 4128 | tf_op jit(solution)/shard_map/ppermute | solution.py:35
  52.2 1.3 %collective-permute-start.5 = (f32[8,256]{1,0:T(8,128)S(1)}, f32[8,256]{1,0:T(8,128)S(1)}, u32[]{:S(2)}, u32[]{:S(2)}) collective-permute-start(f32[8,256]{1,0:T(8,128)S(1)} %pad_maximum_fusion.1), channel_id=1, source_target_pairs={{0,8},{4,12},{1,9},{5,13},{2,10},{6,14},{3,11},{7,15},{16,24},{20,... | collective-permute-start | bytes 24584 | tf_op jit(solution)/shard_map/ppermute | solution.py:35
  53.5 1.5 %collective-permute-done.1 = s32[8]{0:T(128)S(1)} collective-permute-done((s32[8]{0:T(128)S(1)}, s32[8]{0:T(128)S(1)}, u32[]{:S(2)}, u32[]{:S(2)}) %collective-permute-start.1) | collective-permute-done | bytes 64 | tf_op jit(solution)/shard_map/ppermute | solution.py:35
  55.0 0.6 pad_add_fusion.1.refs_1_
  55.6 20.3 %covariance.1 = f32[256,256]{1,0:T(8,128)} custom-call(s32[1]{0:T(128)} %bitcast.refs_0_, s32[16]{0:T(128)} %pad_add_fusion.1.refs_1_, bf16[2,256,256]{2,1,0:T(8,128)(2,1)} %get-tuple-element.7.refs_2_, bf16[2,256,256]{2,1,0:T(8,128)(2,1)} %get-tuple-element.8.refs_3_, f32[2,256,256]{2,1,0:T(8,128)} %get-tuple-element.9.refs_4_, ...), custom_call_target="tpu_custom_call" | custom-call | tf_op jit(solution)/shard_map/covariance/pallas_call | solution.py:199
  75.9 5.0 %psum.15 = f32[1,32,9]{1,2,0:T(8,128)S(1)} all-reduce(f32[1,32,9]{1,2,0:T(8,128)S(1)} %bitcast.39), channel_id=1, replica_groups=mesh['groups'=2,'tm'=4,'space'=2,'chan'=2] {'space'}, use_global_device_ids=true, to_apply=%region_10.11 | all-reduce | flops 288 | bytes 2304 | tf_op jit(solution)/shard_map/psum | solution.py:302
  80.9 0.6 copy.14
  81.5 0.0 collective-permute-done.5
  81.5 0.6 pad_maximum_fusion.refs_4_
  82.1 5.7 %means.1 = f32[4,256]{1,0:T(4,128)} custom-call(s32[1]{0:T(128)} %bitcast.refs_0_, s32[16]{0:T(128)} %pad_add_fusion.1.refs_1_, bf16[2,256,256]{2,1,0:T(8,128)(2,1)} %get-tuple-element.7.refs_2_, bf16[2,256,256]{2,1,0:T(8,128)(2,1)} %get-tuple-element.8.refs_3_, f32[16,256]{1,0:T(8,128)} %pad_maximum_fusion.refs_4_, f32[1,256]{1,0:T(1,128)} %bitcast.50), custom_call_target="tpu_custom_call" | custom-call | tf_op jit(solution)/shard_map/means/pallas_call | solution.py:242
  (2 shorter events, 0.0 us)
Async XLA Ops:
  0.6 28.0 %copy-start = (f32[32,256]{1,0:T(8,128)S(1)}, f32[32,256]{1,0:T(8,128)}, u32[]{:S(2)}) copy-start(f32[32,256]{1,0:T(8,128)} %param.13) | copy-start | bytes 98308
  2.1 11.2 %collective-permute-start.2 = (bf16[4,32,2,256]{3,2,1,0:T(2,128)(2,1)S(1)}, bf16[4,32,2,256]{3,2,1,0:T(2,128)(2,1)S(1)}, u32[]{:S(2)}, u32[]{:S(2)}) collective-permute-start(bf16[4,32,2,256]{3,2,1,0:T(2,128)(2,1)S(1)} %get-tuple-element.24), channel_id=1, source_target_pairs={{0,2},{1,3},{4,6},{5,7},{8,10},{9,11},{12,14},{13,15},{16,18},{17,... | collective-permute-start | bytes 393224 | tf_op jit(solution)/shard_map/ppermute | solution.py:22
  5.5 7.8 %collective-permute-start.3 = (bf16[4,32,2,256]{3,2,1,0:T(2,128)(2,1)S(1)}, bf16[4,32,2,256]{3,2,1,0:T(2,128)(2,1)S(1)}, u32[]{:S(2)}, u32[]{:S(2)}) collective-permute-start(bf16[4,32,2,256]{3,2,1,0:T(2,128)(2,1)S(1)} %get-tuple-element.25), channel_id=1, source_target_pairs={{2,0},{3,1},{6,4},{7,5},{10,8},{11,9},{14,12},{15,13},{18,16},{19,... | collective-permute-start | bytes 393224 | tf_op jit(solution)/shard_map/ppermute | solution.py:25
  6.8 40.8 %collective-permute-start = (s32[4]{0:T(128)}, s32[4]{0:T(128)S(1)}, u32[]{:S(2)}, u32[]{:S(2)}) collective-permute-start(s32[4]{0:T(128)} %param.21), channel_id=1, source_target_pairs={{0,4},{4,8},{8,12},{1,5},{5,9},{9,13},{2,6},{6,10},{10,14},{3,7},{... | collective-permute-start | bytes 56 | tf_op jit(solution)/shard_map/ppermute | solution.py:35
  28.6 10.4 %copy-start.2 = (f32[256,32]{0,1:T(8,128)S(1)}, f32[256,32]{0,1:T(8,128)}, u32[]{:S(2)}) copy-start(f32[256,32]{0,1:T(8,128)} %param.14) | copy-start | bytes 98308
  28.6 19.0 %copy-start.1 = (s32[4]{0:T(128)S(1)}, s32[4]{0:T(128)}, u32[]{:S(2)}) copy-start(s32[4]{0:T(128)} %param.21) | copy-start | bytes 52
  46.3 5.8 %collective-permute-start.4 = (f32[4,256]{1,0:T(4,128)S(1)}, f32[4,256]{1,0:T(4,128)S(1)}, u32[]{:S(2)}, u32[]{:S(2)}) collective-permute-start(f32[4,256]{1,0:T(4,128)S(1)} %psum.14), channel_id=1, source_target_pairs={{0,4},{4,8},{8,12},{1,5},{5,9},{9,13},{2,6},{6,10},{10,14},{3,7},{... | collective-permute-start | bytes 12296 | tf_op jit(solution)/shard_map/ppermute | solution.py:35
  47.7 7.3 %collective-permute-start.1 = (s32[8]{0:T(128)S(1)}, s32[8]{0:T(128)S(1)}, u32[]{:S(2)}, u32[]{:S(2)}) collective-permute-start(s32[8]{0:T(128)S(1)} %pad_add_fusion), channel_id=1, source_target_pairs={{0,8},{4,12},{1,9},{5,13},{2,10},{6,14},{3,11},{7,15},{16,24},{20,... | collective-permute-start | bytes 104 | tf_op jit(solution)/shard_map/ppermute | solution.py:35
  52.2 29.3 %collective-permute-start.5 = (f32[8,256]{1,0:T(8,128)S(1)}, f32[8,256]{1,0:T(8,128)S(1)}, u32[]{:S(2)}, u32[]{:S(2)}) collective-permute-start(f32[8,256]{1,0:T(8,128)S(1)} %pad_maximum_fusion.1), channel_id=1, source_target_pairs={{0,8},{4,12},{1,9},{5,13},{2,10},{6,14},{3,11},{7,15},{16,24},{20,... | collective-permute-start | bytes 24584 | tf_op jit(solution)/shard_map/ppermute | solution.py:35

commit v2 on v1

--- a/solution.py
+++ b/solution.py
@@ -1,5 +1,8 @@
+import math
+
 import jax
 import jax.numpy as jnp
+import numpy as np
 from jax import lax
 from jax.experimental import pallas as pl
 from jax.experimental.pallas import tpu as pltpu
@@ -13,17 +16,6 @@
 BF16 = jnp.bfloat16
 
 precise = lax.Precision.HIGHEST
-
-
-def extended(block, axis, dim, width):
-    count = lax.axis_size(axis)
-    forward = [(i, i + 1) for i in range(count - 1)]
-    backward = [(target, source) for source, target in forward]
-    low = lax.ppermute(
-        lax.slice_in_dim(block, block.shape[dim] - width, None, axis=dim), axis, forward
-    )
-    high = lax.ppermute(lax.slice_in_dim(block, 0, width, axis=dim), axis, backward)
-    return jnp.concatenate([low, block, high], axis=dim)
 
 
 def history(own, axis):
@@ -248,6 +240,279 @@
     )(place, flags, map_high, map_low, shifts, init_mean[None])
 
 
+LAGS = (0, DILATION_STEP, 2 * DILATION_STEP, -DILATION_STEP, -2 * DILATION_STEP)
+TAPS = tuple((a, b) for a in (-1, 0, 1) for b in (-1, 0, 1))
+EDGE = 2 * DILATION_STEP
+KINDS = 8
+EDGE_KINDS = 2
+HALO_KINDS = 6
+
+
+def moved(x, by, axis):
+    if by == 0:
+        return x
+    length = x.shape[axis]
+    shape = list(x.shape)
+    shape[axis] = abs(by)
+    zeros = jnp.zeros(shape, x.dtype)
+    if by > 0:
+        return jnp.concatenate(
+            [lax.slice_in_dim(x, by, length, axis=axis), zeros], axis=axis
+        )
+    return jnp.concatenate(
+        [zeros, lax.slice_in_dim(x, 0, length + by, axis=axis)], axis=axis
+    )
+
+
+def folded(x):
+    total = x[:, :LANES]
+    for at in range(LANES, x.shape[1], LANES):
+        total = total + x[:, at : at + LANES]
+    return total
+
+
+def frames_kernel(taps, flags, frames, pooling, part, stats, pooled):
+    steps, block, rows, columns = frames.shape
+    first = pl.program_id(0) * block
+
+    @pl.when(pl.program_id(0) == 0)
+    def _():
+        for k, (a, b) in enumerate(TAPS):
+            pooled[k] = moved(
+                moved(pooling[...], -DILATION_STEP * b, 1), -DILATION_STEP * a, 0
+            )
+
+    lane = lax.broadcasted_iota(jnp.int32, (rows, LANES), 1)
+    row = lax.broadcasted_iota(jnp.int32, (rows, LANES), 0)
+    masks = [lax.rem(lane, rows) - row == lag for lag in LAGS]
+    right_masks = [(lane - row == lag) & (lane < rows) for lag in LAGS[:3]]
+    column = lax.broadcasted_iota(jnp.int32, (rows, columns), 1)
+    left_edge = (column < DILATION_STEP).astype(F32).astype(BF16)
+    right_edge = (column >= columns - DILATION_STEP).astype(F32).astype(BF16)
+    blank = jnp.zeros((rows, 2 * LANES - 5 * rows), F32)
+    for c in range(block):
+        weights = taps[first + c, 0] * pooled[0]
+        for k in range(1, len(TAPS)):
+            weights = weights + taps[first + c, k] * pooled[k]
+        gram = jnp.zeros((rows, 5 * rows), F32)
+        for t in range(steps):
+            frame = frames[t, c]
+            part[t, c : c + 1, :] = jnp.sum(
+                folded(frame.astype(F32) * weights), axis=0, keepdims=True
+            )
+            partners = jnp.concatenate(
+                [
+                    frame,
+                    moved(frame, DILATION_STEP, 1),
+                    moved(frame, 2 * DILATION_STEP, 1),
+                    frame * left_edge,
+                    frame * right_edge,
+                ],
+                axis=0,
+            )
+            gram = gram + contract(frame * flags[t].astype(F32).astype(BF16), partners, NT)
+        near = gram[:, :LANES]
+        far = jnp.concatenate([gram[:, LANES:], blank], axis=1)
+        sums = [jnp.sum(jnp.where(m, near, 0.0), axis=0, keepdims=True) for m in masks]
+        sums += [jnp.sum(jnp.where(m, far, 0.0), axis=0, keepdims=True) for m in right_masks]
+        stats[c : c + 1, :] = jnp.concatenate(sums, axis=1)
+
+
+def frame_sums(taps, flags, frames, pooling):
+    steps, channels, rows, columns = frames.shape
+    block = math.gcd(channels, 16)
+    vmem = pl.BlockSpec(memory_space=pltpu.VMEM)
+    smem = pl.BlockSpec(memory_space=pltpu.SMEM)
+    return pl.pallas_call(
+        frames_kernel,
+        grid=(channels // block,),
+        out_shape=(
+            jax.ShapeDtypeStruct((steps, channels, LANES), F32),
+            jax.ShapeDtypeStruct((channels, KINDS * LANES), F32),
+        ),
+        in_specs=[
+            smem,
+            smem,
+            pl.BlockSpec((steps, block, rows, columns), lambda i: (0, i, 0, 0)),
+            vmem,
+        ],
+        out_specs=(
+            pl.BlockSpec((steps, block, LANES), lambda i: (0, i, 0)),
+            pl.BlockSpec((block, KINDS * LANES), lambda i: (i, 0)),
+        ),
+        scratch_shapes=[pltpu.VMEM((len(TAPS), rows, columns), F32)],
+        name="frame_sums",
+    )(taps, flags, frames, pooling)
+
+
+def selection(rows):
+    near = np.zeros((KINDS, LANES, len(TAPS), len(TAPS)), np.float32)
+    edge = np.zeros((EDGE_KINDS, LANES, len(TAPS), len(TAPS)), np.float32)
+    halo = np.zeros((2, HALO_KINDS, LANES, len(TAPS), len(TAPS)), np.float32)
+    own = np.arange(rows)
+    top, bottom = own[:DILATION_STEP], own[rows - DILATION_STEP :]
+    for i, (a, b) in enumerate(TAPS):
+        for j, (c, d) in enumerate(TAPS):
+            down, across = c - a, d - b
+            if (down, across) < (0, 0):
+                down, across = -down, -across
+            lag = abs(across)
+            kind = down if across >= 0 else down + 2
+            near[kind, lag * rows + own, i, j] += 1
+            if down:
+                if across == 0:
+                    halo[down - 1, :2, :, i, j] += 1
+                else:
+                    halo[down - 1, 1 + lag + (2 if across < 0 else 0), :, i, j] += 1
+            if b == d == 1:
+                near[down, 3 * rows + own, i, j] -= 1
+                if down:
+                    halo[down - 1, 0, :DILATION_STEP, i, j] -= 1
+            if b == d == -1:
+                near[5 + down, own, i, j] -= 1
+                if down:
+                    halo[down - 1, 1, LANES - DILATION_STEP :, i, j] -= 1
+            if a == c != 0:
+                lost = top if a == 1 else bottom
+                edge[0, lag * rows + lost, i, j] -= 1
+                if b == d == 1:
+                    edge[0, 3 * rows + lost, i, j] += 1
+                if b == d == -1:
+                    edge[1, lost, i, j] += 1
+    pairs = len(TAPS) ** 2
+    table = np.concatenate([m.reshape(-1, pairs) for m in (near, edge, halo)], axis=0)
+    return np.pad(table, ((0, 0), (0, LANES - pairs)))
+
+
+def finish_kernel(
+    scale, flags, edges, above, below, part, stats, taps, pooling, gain, table,
+    gain_part, gradient, values,
+):
+    steps, _, channels, columns = edges.shape
+    rows = pooling.shape[0]
+    place, count = lax.axis_index("space"), lax.axis_size("space")
+    has_above = jnp.where(place > 0, 1.0, 0.0).astype(F32)
+    has_below = jnp.where(place < count - 1, 1.0, 0.0).astype(F32)
+    halo_weights = []
+    for side, (a, start, has) in enumerate(
+        ((-1, 0, has_above), (1, rows - DILATION_STEP, has_below))
+    ):
+        for r in range(DILATION_STEP):
+            value = jnp.zeros((channels, columns), F32)
+            for b in (-1, 0, 1):
+                k = TAPS.index((a, b))
+                shifted = moved(pooling[start + r : start + r + 1, :], -DILATION_STEP * b, 1)
+                value = value + taps[:, k : k + 1] * shifted
+            halo_weights.append(value * has)
+    sums = [[None] * 5 for _ in range(2)]
+    ones = jnp.ones((GROUP, LANES), BF16)
+    row_sums = []
+    for t in range(steps):
+        flag = flags[t].astype(F32)
+        upper = [above[t, r].astype(F32) for r in range(DILATION_STEP)]
+        lower = [below[t, r].astype(F32) for r in range(DILATION_STEP)]
+        total = jnp.zeros((channels, columns), F32)
+        for value, weight in zip(upper + lower, halo_weights):
+            total = total + value * weight
+        row_sums.append(part[t] + folded(total))
+        for r in range(DILATION_STEP):
+            near_top = edges[t, DILATION_STEP + r].astype(F32)
+            far_bottom = edges[t, 2 * DILATION_STEP + r].astype(F32)
+            near_bottom = edges[t, 3 * DILATION_STEP + r].astype(F32)
+            high, low = upper[r] * (flag * has_above), lower[r] * (flag * has_below)
+            for n in range(-2, 3):
+                shifted_low = moved(low, DILATION_STEP * n, 1)
+                shifted_high = moved(high, -DILATION_STEP * n, 1)
+                one = near_bottom * shifted_low
+                two = far_bottom * shifted_low + near_top * shifted_high
+                for which, value in ((0, one), (1, two)):
+                    old = sums[which][n]
+                    sums[which][n] = value if old is None else old + value
+    high, low = split(jnp.concatenate(row_sums, axis=0))
+    tile_sums = contract(ones, high, NT) + contract(ones, low, NT)
+    shape = (GROUP, steps * channels)
+    owner = lax.broadcasted_iota(jnp.int32, shape, 1) // channels
+    step = lax.broadcasted_iota(jnp.int32, shape, 0)
+    seen = jnp.zeros(shape, F32)
+    for t in range(steps):
+        seen = jnp.where((owner == t) & (step == t), flags[t].astype(F32), seen)
+    gains = jnp.concatenate([gain[...]] * steps, axis=1)
+    product = three_pass(split(tile_sums * seen), split(gains), NT)
+    gain_part[...] = product[:steps]
+    values[:, : KINDS * LANES] = stats[...]
+    lane = lax.broadcasted_iota(jnp.int32, (channels, LANES), 1) % rows
+    outside = jnp.where(lane < DILATION_STEP, 1.0 - has_above, 0.0)
+    outside = jnp.where(lane >= rows - DILATION_STEP, 1.0 - has_below, outside)
+    at = KINDS * LANES
+    for kind in (0, 5):
+        values[:, at : at + LANES] = stats[:, kind * LANES : (kind + 1) * LANES] * outside
+        at += LANES
+    for which in range(2):
+        centre = sums[which][0]
+        pieces = [centre[:, :LANES], centre[:, columns - LANES :]]
+        for inner in range(LANES, columns - LANES, LANES):
+            pieces[2] = pieces[2] + centre[:, inner : inner + LANES]
+        pieces += [folded(sums[which][n]) for n in (1, 2, -1, -2)]
+        for piece in pieces:
+            values[:, at : at + LANES] = piece
+            at += LANES
+    high, low = split(values[...])
+    pairs = contract(high, table[...], NN) + contract(low, table[...], NN)
+    tap_count = len(TAPS)
+    source = lax.broadcasted_iota(jnp.int32, (tap_count, LANES), 1)
+    spread_row = lax.broadcasted_iota(jnp.int32, (tap_count, LANES), 0)
+    spread = (source // tap_count == spread_row).astype(F32)
+    pair = lax.broadcasted_iota(jnp.int32, (LANES, LANES), 0)
+    target = lax.broadcasted_iota(jnp.int32, (LANES, LANES), 1)
+    gather = (pair % tap_count == target).astype(F32)
+    weights = jnp.dot(taps[...], spread, precision=precise, preferred_element_type=F32)
+    result = jnp.dot(pairs * weights, gather, precision=precise, preferred_element_type=F32)
+    gradient[...] = result * scale
+
+
+def finish(flags, edges, above, below, part, stats, taps, pooling, gain):
+    steps, _, channels, columns = edges.shape
+    rows = pooling.shape[0]
+    scale = 1.0 / (rows * lax.axis_size("space") * columns)
+    table = jnp.asarray(selection(rows), BF16)
+    vmem = pl.BlockSpec(memory_space=pltpu.VMEM)
+    smem = pl.BlockSpec(memory_space=pltpu.SMEM)
+
+    def kernel(*refs):
+        finish_kernel(scale, *refs)
+
+    return pl.pallas_call(
+        kernel,
+        out_shape=(
+            jax.ShapeDtypeStruct((steps, gain.shape[0]), F32),
+            jax.ShapeDtypeStruct((channels, LANES), F32),
+        ),
+        in_specs=[smem] + [vmem] * 9,
+        out_specs=(vmem, vmem),
+        scratch_shapes=[pltpu.VMEM((channels, table.shape[0]), F32)],
+        name="finish",
+    )(flags, edges, above, below, part, stats, taps, pooling, gain, table)
+
+
+def beside(edges, axis):
+    count = lax.axis_size(axis)
+    top = edges[:, :DILATION_STEP]
+    bottom = edges[:, -DILATION_STEP:]
+    if count == 2:
+        sent = jnp.where(lax.axis_index(axis) == 0, bottom, top)
+        got = lax.ppermute(sent, axis, [(0, 1), (1, 0)])
+        return got, got
+    forward = [(i, (i + 1) % count) for i in range(count)]
+    backward = [(target, source) for source, target in forward]
+    return lax.ppermute(bottom, axis, forward), lax.ppermute(top, axis, backward)
+
+
+def total(value, axis):
+    if lax.axis_size(axis) == 2:
+        return value + lax.ppermute(value, axis, [(0, 1), (1, 0)])
+    return lax.psum(value, axis)
+
+
 def local(
     frames,
     conv_taps,
@@ -261,49 +526,25 @@
     init_root,
     observed,
 ):
-    step_count, channels, row_tiles, column_list = frames.shape
+    step_count, channels, rows, columns = frames.shape
     place = lax.axis_index("tm").astype(jnp.int32)[None]
+    edges = jnp.concatenate([frames[:, :, :EDGE], frames[:, :, rows - EDGE :]], axis=2)
+    edges = edges.transpose(0, 2, 1, 3)
+    above, below = beside(edges, "space")
     flags = history(observed, "tm")
-    extended_frame = extended(frames, "space", 2, DILATION_STEP)
+    part, stats = frame_sums(conv_taps, observed, frames, pooling)
     map_high, map_low, grams, first_gram = prepare(
         transition, update_map, quiet_root, observed_root, init_root
     )
-    extended_frame = jnp.pad(
-        extended_frame, ((0, 0), (0, 0), (0, 0), (DILATION_STEP, DILATION_STEP))
-    ).astype(jnp.float32)
-    window_views = [
-        extended_frame[
-            :,
-            :,
-            left_element * DILATION_STEP : left_element * DILATION_STEP + row_tiles,
-            right_element * DILATION_STEP : right_element * DILATION_STEP + column_list,
-        ]
-        for left_element in range(3)
-        for right_element in range(3)
-    ]
-    response = jnp.zeros(frames.shape, jnp.float32)
-    for k in range(9):
-        response = response + conv_taps[:, k][None, :, None, None] * window_views[k]
-    weights = observed.astype(jnp.float32)
-    tile_sums = jnp.einsum("tchw,hw->tc", response, pooling, precision=precise)
-    gain_part = (
-        jnp.dot(tile_sums, gain_matrix.T, precision=precise, preferred_element_type=jnp.float32)
-        * weights[:, None]
+    gain_part, gradient = finish(
+        observed, edges, above, below, part, stats, conv_taps, pooling, gain_matrix
     )
-    shifts = lax.psum(gain_part, ("space", "chan"))
-    scaling = weights / (row_tiles * lax.axis_size("space") * column_list)
-    grad_local = jnp.stack(
-        [
-            jnp.sum(response * window_views[k] * scaling[:, None, None, None], axis=(0, 2, 3))
-            for k in range(9)
-        ],
-        axis=1,
-    )
-    tap_gradient = lax.psum(grad_local, "space")[None]
+    shifts = total(total(gain_part, "chan"), "space")
+    gradient = total(gradient, "space")
     all_shifts = history(shifts, "tm")
     root = covariance(place, flags, step_count, map_high, map_low, grams, first_gram)
     filtered_means = means(place, flags, step_count, map_high, map_low, all_shifts, init_mean)
-    return (filtered_means, root[None], tap_gradient)
+    return (filtered_means, root[None], gradient[None, :, : len(TAPS)])
 
 
 def solution(mesh):

time: 88.3 us -> 62.3 us (0.71)
  other arithmetic: 17.9 us -> 2.01 us
  blocking collectives: 12.2 us -> 0 us
  matrix products: 10.4 us -> 0 us
  Pallas kernels: 28.9 us -> 37.9 us
  waiting for transfers between devices: 4.69 us -> 8.31 us
  local copies, waits for them, and re-layouts: 3.06 us -> 4.25 us
  starting transfers between devices: 9.83 us -> 8.67 us
    psum x2 -> x0, blocking collectives: 12.2 us -> none  [the longest x1 7.21 us: local(): shifts = lax.psum(gain_part, ('space', 'chan'))]
    reduce_sum x1 -> x0, other arithmetic: 10.5 us -> none  [local(): jnp.sum(response * window_views[k] * scaling[:, None, None, None], axis=(...]
    dot_general x2 -> x0, matrix products: 10.4 us -> none  [the longest x1 10.3 us: local(): tile_sums = jnp.einsum('tchw,hw->tc', response, pooling, precision=precise)]
    pallas_call x0 -> x2, Pallas kernels: none -> 9.28 us  [the longest x1 5.84 us: frame_sums(): pl.pallas_call(frames_kernel, grid=(channels // block,), out_shape=(jax.S...]
    convert_element_type x2 -> x0, other arithmetic: 5.51 us -> none  [the longest x1 4.85 us: local(): extended_frame = jnp.pad(extended_frame, ((0, 0), (0, 0), (0, 0), (DILATI...]
    ppermute x2 -> x4, waiting for transfers between devices: 0.01 us -> 2.65 us  [the longest x3 2.64 us: total(): return value + lax.ppermute(value, axis, [(0, 1), (1, 0)])]
    unnamed x7 -> x17, local copies, waits for them, and re-layouts: 0.62 us -> 2.83 us
    ppermute x2 -> x4, starting transfers between devices: 4.69 us -> 3.53 us  [the longest x3 1.97 us: total(): return value + lax.ppermute(value, axis, [(0, 1), (1, 0)])]
  transfers between devices with their start and end apart: 6 -> 8, of which waited for: 2 -> 5; matrix products, arithmetic and copies ran while one was open for 33% -> 6% of each run, Pallas kernels for 26% -> 46%
where the time goes in v2:
time: 62.3 us; the launch traced here: 61.9 us
  Pallas kernels  37.9 us (61%)
  starting transfers between devices  8.67 us (14%)
  waiting for transfers between devices  8.31 us (13%)
  local copies, waits for them, and re-layouts  4.25 us (7%)
  other arithmetic  2.01 us (3%)
  between operations  0.78 us (1%)
    pallas_call x1, Pallas kernels, covariance(): pl.pallas_call(kernel, out_shape=jax.ShapeDtypeStruct((size, size), F32),...  20.1 us
    pallas_call x1, Pallas kernels, frame_sums(): pl.pallas_call(frames_kernel, grid=(channels // block,), out_shape=(jax.S...  5.84 us
    pallas_call x1, Pallas kernels, means(): pl.pallas_call(kernel, out_shape=jax.ShapeDtypeStruct((steps, size), F32)...  5.7 us
    ppermute x4, waiting for transfers between devices, history(): held = jnp.concatenate([held, lax.ppermute(held, axis, pairs)], axis=0)  5.66 us
    ppermute x4, starting transfers between devices, history(): held = jnp.concatenate([held, lax.ppermute(held, axis, pairs)], axis=0)  5.15 us
    pallas_call x1, Pallas kernels, finish(): pl.pallas_call(kernel, out_shape=(jax.ShapeDtypeStruct((steps, gain.shape...  3.44 us
    pallas_call x1, Pallas kernels, prepare(): pl.pallas_call(prepare_kernel, out_shape=(jax.ShapeDtypeStruct((2, size,...  2.87 us
    unnamed x17, local copies, waits for them, and re-layouts  2.83 us
  transfers between devices with their start and end apart: 8, of which 5 were waited for; matrix products, arithmetic and copies ran while one was open for 6% of the time, Pallas kernels for 46%

profile of v2, /device:TPU:28, one launch (start us, length us, event | category | flops | bytes accessed | tf_op | source)
XLA Modules:
  0.0 61.9 jit_solution(9634639745664155611)
XLA Ops:
  0.6 0.0 copy-start.4
  0.6 0.0 copy-start.2
  0.7 1.4 %fusion.1 = (bf16[4,32,4,256]{3,2,1,0:T(4,128)(2,1)S(1)}, bf16[4,32,4,256]{3,2,1,0:T(4,128)(2,1)S(1)}) fusion(bf16[4,32,32,256]{3,2,1,0:T(8,128)(2,1)} %frames.1), kind=kLoop, calls=%fused_computation.8 | loop fusion | bytes 1048576 | tf_op jit(solution)/shard_map/slice | solution.py:531
  2.2 0.0 copy-start
  2.3 1.6 %collective-permute-start.2 = (bf16[4,2,32,256]{3,2,1,0:T(8,128)(2,1)S(1)}, bf16[4,2,32,256]{3,2,1,0:T(8,128)(2,1)S(1)}, u32[]{:S(2)}, u32[]{:S(2)}) collective-permute-start(bf16[4,2,32,256]{3,2,1,0:T(8,128)(2,1)S(1)} %slice_select_fusion), channel_id=1, source_target_pairs={{0,2},{2,0},{1,3},{3,1},{4,6},{6,4},{5,7},{7,5},{8,10},{10,8},{9,1... | collective-permute-start | bytes 393224 | tf_op jit(solution)/shard_map/ppermute | solution.py:503
  3.8 0.0 copy-done.4
  3.8 0.7 %copy.17.taps.refs_6_ = f32[32,9]{1,0:T(8,128)} copy(f32[32,9]{0,1:T(8,128)S(1)} %copy-done.4) | data formatting | bytes 2304 | tf_op args[1]
  4.5 0.0 copy-done.2
  4.5 0.0 copy-start.5
  4.5 0.8 %copy.19.refs_8_ = f32[256,32]{1,0:T(8,128)} copy(f32[256,32]{0,1:T(8,128)S(1)} %copy-done.2) | data formatting | bytes 65536 | tf_op args[3]
  5.3 5.8 %frame_sums.1 = (f32[4,32,128]{2,1,0:T(8,128)}, f32[32,1024]{1,0:T(8,128)}) custom-call(f32[32,9]{1,0:T(8,128)} %copy.17.taps.refs_6_, s32[4]{0:T(128)} %refs_0_.1, bf16[4,32,32,256]{3,2,1,0:T(8,128)(2,1)} %frames.1, f32[32,256]{1,0:T(8,128)} %refs_7_.1), custom_call_target="tpu_custom_call" | custom-call | tf_op jit(solution)/shard_map/frame_sums/pallas_call | solution.py:326
  11.1 0.0 collective-permute-done.2.refs_2_.refs_3_
  11.1 0.0 copy-start.1
  11.1 0.0 copy-done
  11.1 0.6 %copy-done.1 = bf16[4,2,32,256]{3,2,1,0:T(8,128)(2,1)} copy-done((bf16[4,2,32,256]{3,2,1,0:T(8,128)(2,1)}, bf16[4,2,32,256]{3,2,1,0:T(8,128)(2,1)S(1)}, u32[]{:S(2)}) %copy-start.1) | copy-done | bytes 131096
  11.8 3.4 %finish.1 = (f32[4,256]{1,0:T(4,128)}, f32[32,128]{1,0:T(8,128)}) custom-call(s32[4]{0:T(128)} %refs_0_.1, bf16[4,8,32,256]{3,2,1,0:T(8,128)(2,1)} %copy-done, bf16[4,2,32,256]{3,2,1,0:T(8,128)(2,1)} %copy-done.1, bf16[4,2,32,256]{3,2,1,0:T(8,128)(2,1)} %copy-done.1, f32[4,32,128]{2,1,0:T(8,128)} %get-tuple-element.13.refs_4_, ...), custom_call_target="tpu_custom_call" | custom-call | tf_op jit(solution)/shard_map/finish/pallas_call | solution.py:484
  15.2 0.0 copy-start.3
  15.2 0.0 collective-permute-start.3
  15.2 0.0 copy-done.5
  15.2 1.3 %collective-permute-start = (s32[4]{0:T(128)S(1)}, s32[4]{0:T(128)S(1)}, u32[]{:S(2)}, u32[]{:S(2)}) collective-permute-start(s32[4]{0:T(128)S(1)} %copy-done.5), channel_id=1, source_target_pairs={{0,4},{4,8},{8,12},{1,5},{5,9},{9,13},{2,6},{6,10},{10,14},{3,7},{... | collective-permute-start | bytes 56 | tf_op jit(solution)/shard_map/ppermute | solution.py:27
  16.5 2.9 %prepare.1 = (bf16[2,256,256]{2,1,0:T(8,128)(2,1)}, bf16[2,256,256]{2,1,0:T(8,128)(2,1)}, f32[2,256,256]{2,1,0:T(8,128)}, f32[256,256]{1,0:T(8,128)}) custom-call(f32[256,256]{1,0:T(8,128)} %transition.1, f32[256,256]{1,0:T(8,128)} %update_map.1, f32[256,256]{1,0:T(8,128)} %quiet_root.1, f32[256,256]{1,0:T(8,128)} %observed_root.1, f32[256,256]{1,0:T(8,128)} %init_root.1), custom_call_target="tpu_custom_call" | custom-call | tf_op jit(solution)/shard_map/prepare/pallas_call | solution.py:71
  19.4 0.0 collective-permute-done.3
  19.4 0.7 %add.9 = f32[4,256]{1,0:T(4,128)S(1)} add(f32[4,256]{1,0:T(4,128)} %get-tuple-element.15, f32[4,256]{1,0:T(4,128)S(1)} %collective-permute-done.3) | non-fusion elementwise | flops 1024 | bytes 12288 | tf_op jit(solution)/shard_map/add | solution.py:512
  20.1 0.5 collective-permute-start.4
  20.6 0.1 collective-permute-done
  20.7 0.1 pad_add_fusion
  20.8 1.3 %collective-permute-start.1 = (s32[8]{0:T(128)S(1)}, s32[8]{0:T(128)S(1)}, u32[]{:S(2)}, u32[]{:S(2)}) collective-permute-start(s32[8]{0:T(128)S(1)} %pad_add_fusion), channel_id=1, source_target_pairs={{0,8},{4,12},{1,9},{5,13},{2,10},{6,14},{3,11},{7,15},{16,24},{20,... | collective-permute-start | bytes 104 | tf_op jit(solution)/shard_map/ppermute | solution.py:27
  22.0 1.6 %collective-permute-done.4 = f32[4,256]{1,0:T(4,128)S(1)} collective-permute-done((f32[4,256]{1,0:T(4,128)S(1)}, f32[4,256]{1,0:T(4,128)S(1)}, u32[]{:S(2)}, u32[]{:S(2)}) %collective-permute-start.4) | collective-permute-done | bytes 4128 | tf_op jit(solution)/shard_map/ppermute | solution.py:512
  23.7 1.3 %collective-permute-start.5 = (f32[4,256]{1,0:T(4,128)S(1)}, f32[4,256]{1,0:T(4,128)S(1)}, u32[]{:S(2)}, u32[]{:S(2)}) collective-permute-start(f32[4,256]{1,0:T(4,128)S(1)} %add.10), channel_id=1, source_target_pairs={{0,4},{4,8},{8,12},{1,5},{5,9},{9,13},{2,6},{6,10},{10,14},{3,7},{... | collective-permute-start | bytes 12296 | tf_op jit(solution)/shard_map/ppermute | solution.py:27
  25.0 2.1 %collective-permute-done.1 = s32[8]{0:T(128)S(1)} collective-permute-done((s32[8]{0:T(128)S(1)}, s32[8]{0:T(128)S(1)}, u32[]{:S(2)}, u32[]{:S(2)}) %collective-permute-start.1) | collective-permute-done | bytes 64 | tf_op jit(solution)/shard_map/ppermute | solution.py:27
  27.1 0.6 pad_add_fusion.1.refs_1_
  27.7 20.1 %covariance.1 = f32[256,256]{1,0:T(8,128)} custom-call(s32[1]{0:T(128)} %bitcast.refs_0_, s32[16]{0:T(128)} %pad_add_fusion.1.refs_1_, bf16[2,256,256]{2,1,0:T(8,128)(2,1)} %get-tuple-element.11.refs_2_, bf16[2,256,256]{2,1,0:T(8,128)(2,1)} %get-tuple-element.12.refs_3_, f32[2,256,256]{2,1,0:T(8,128)} %get-tuple-element.16.refs_4_, ...), custom_call_target="tpu_custom_call" | custom-call | tf_op jit(solution)/shard_map/covariance/pallas_call | solution.py:191
  47.7 0.0 copy-done.3
  47.7 1.4 %collective-permute-start.7 = (f32[32,128]{1,0:T(8,128)S(1)}, f32[32,128]{1,0:T(8,128)S(1)}, u32[]{:S(2)}, u32[]{:S(2)}) collective-permute-start(f32[32,128]{1,0:T(8,128)S(1)} %copy-done.3), channel_id=1, source_target_pairs={{0,2},{2,0},{1,3},{3,1},{4,6},{6,4},{5,7},{7,5},{8,10},{10,8},{9,1... | collective-permute-start | bytes 49160 | tf_op jit(solution)/shard_map/ppermute | solution.py:512
  49.2 0.0 collective-permute-done.5
  49.2 1.3 %collective-permute-start.6 = (f32[8,256]{1,0:T(8,128)S(1)}, f32[8,256]{1,0:T(8,128)S(1)}, u32[]{:S(2)}, u32[]{:S(2)}) collective-permute-start(f32[8,256]{1,0:T(8,128)S(1)} %pad_maximum_fusion.1), channel_id=1, source_target_pairs={{0,8},{4,12},{1,9},{5,13},{2,10},{6,14},{3,11},{7,15},{16,24},{20,... | collective-permute-start | bytes 24584 | tf_op jit(solution)/shard_map/ppermute | solution.py:27
  50.5 1.0 %collective-permute-done.7 = f32[32,128]{1,0:T(8,128)S(1)} collective-permute-done((f32[32,128]{1,0:T(8,128)S(1)}, f32[32,128]{1,0:T(8,128)S(1)}, u32[]{:S(2)}, u32[]{:S(2)}) %collective-permute-start.7) | collective-permute-done | bytes 16416 | tf_op jit(solution)/shard_map/ppermute | solution.py:512
  51.5 0.7 %copy.20 = f32[1,32,9]{1,0,2:T(1,128)} copy(f32[1,32,9]{2,1,0:T(8,128)S(1)} %fusion) | data formatting | bytes 2304
  52.1 3.5 %collective-permute-done.6 = f32[8,256]{1,0:T(8,128)S(1)} collective-permute-done((f32[8,256]{1,0:T(8,128)S(1)}, f32[8,256]{1,0:T(8,128)S(1)}, u32[]{:S(2)}, u32[]{:S(2)}) %collective-permute-start.6) | collective-permute-done | bytes 8224 | tf_op jit(solution)/shard_map/ppermute | solution.py:27
  55.6 0.6 pad_maximum_fusion.refs_4_
  56.2 5.7 %means.1 = f32[4,256]{1,0:T(4,128)} custom-call(s32[1]{0:T(128)} %bitcast.refs_0_, s32[16]{0:T(128)} %pad_add_fusion.1.refs_1_, bf16[2,256,256]{2,1,0:T(8,128)(2,1)} %get-tuple-element.11.refs_2_, bf16[2,256,256]{2,1,0:T(8,128)(2,1)} %get-tuple-element.12.refs_3_, f32[16,256]{1,0:T(8,128)} %pad_maximum_fusion.refs_4_, f32[1,256]{1,0:T(1,128)} %bitcast.8), custom_call_target="tpu_custom_call" | custom-call | tf_op jit(solution)/shard_map/means/pallas_call | solution.py:234
  (7 shorter events, 0.1 us)
Async XLA Ops:
  0.6 3.2 %copy-start.4 = (f32[32,9]{0,1:T(8,128)S(1)}, f32[32,9]{0,1:T(8,128)}, u32[]{:S(2)}) copy-start(f32[32,9]{0,1:T(8,128)} %param.13) | copy-start | bytes 3460
  0.6 3.9 %copy-start.2 = (f32[256,32]{0,1:T(8,128)S(1)}, f32[256,32]{0,1:T(8,128)}, u32[]{:S(2)}) copy-start(f32[256,32]{0,1:T(8,128)} %param.15) | copy-start | bytes 98308
  2.2 8.9 %copy-start = (bf16[4,8,32,256]{3,2,1,0:T(8,128)(2,1)}, bf16[4,8,32,256]{3,2,1,0:T(8,128)(2,1)S(1)}, u32[]{:S(2)}) copy-start(bf16[4,8,32,256]{3,2,1,0:T(8,128)(2,1)S(1)} %maximum_bitcast_fusion.refs_1_) | copy-start | bytes 1572868
  2.3 8.8 %collective-permute-start.2 = (bf16[4,2,32,256]{3,2,1,0:T(8,128)(2,1)S(1)}, bf16[4,2,32,256]{3,2,1,0:T(8,128)(2,1)S(1)}, u32[]{:S(2)}, u32[]{:S(2)}) collective-permute-start(bf16[4,2,32,256]{3,2,1,0:T(8,128)(2,1)S(1)} %slice_select_fusion), channel_id=1, source_target_pairs={{0,2},{2,0},{1,3},{3,1},{4,6},{6,4},{5,7},{7,5},{8,10},{10,8},{9,1... | collective-permute-start | bytes 393224 | tf_op jit(solution)/shard_map/ppermute | solution.py:503
  4.5 10.7 %copy-start.5 = (s32[4]{0:T(128)S(1)}, s32[4]{0:T(128)}, u32[]{:S(2)}) copy-start(s32[4]{0:T(128)} %refs_0_.1) | copy-start | bytes 52
  11.1 0.7 %copy-start.1 = (bf16[4,2,32,256]{3,2,1,0:T(8,128)(2,1)}, bf16[4,2,32,256]{3,2,1,0:T(8,128)(2,1)S(1)}, u32[]{:S(2)}) copy-start(bf16[4,2,32,256]{3,2,1,0:T(8,128)(2,1)S(1)} %collective-permute-done.2.refs_2_.refs_3_) | copy-start | bytes 393220
  15.2 32.5 %copy-start.3 = (f32[32,128]{1,0:T(8,128)S(1)}, f32[32,128]{1,0:T(8,128)}, u32[]{:S(2)}) copy-start(f32[32,128]{1,0:T(8,128)} %get-tuple-element.18) | copy-start | bytes 49156
  15.2 4.2 %collective-permute-start.3 = (f32[4,256]{1,0:T(4,128)}, f32[4,256]{1,0:T(4,128)S(1)}, u32[]{:S(2)}, u32[]{:S(2)}) collective-permute-start(f32[4,256]{1,0:T(4,128)} %get-tuple-element.15), channel_id=1, source_target_pairs={{0,1},{1,0},{2,3},{3,2},{4,5},{5,4},{6,7},{7,6},{8,9},{9,8},{10,11... | collective-permute-start | bytes 12296 | tf_op jit(solution)/shard_map/ppermute | solution.py:512
  15.2 5.5 %collective-permute-start = (s32[4]{0:T(128)S(1)}, s32[4]{0:T(128)S(1)}, u32[]{:S(2)}, u32[]{:S(2)}) collective-permute-start(s32[4]{0:T(128)S(1)} %copy-done.5), channel_id=1, source_target_pairs={{0,4},{4,8},{8,12},{1,5},{5,9},{9,13},{2,6},{6,10},{10,14},{3,7},{... | collective-permute-start | bytes 56 | tf_op jit(solution)/shard_map/ppermute | solution.py:27
  20.1 3.6 %collective-permute-start.4 = (f32[4,256]{1,0:T(4,128)S(1)}, f32[4,256]{1,0:T(4,128)S(1)}, u32[]{:S(2)}, u32[]{:S(2)}) collective-permute-start(f32[4,256]{1,0:T(4,128)S(1)} %add.9), channel_id=1, source_target_pairs={{0,2},{2,0},{1,3},{3,1},{4,6},{6,4},{5,7},{7,5},{8,10},{10,8},{9,1... | collective-permute-start | bytes 12296 | tf_op jit(solution)/shard_map/ppermute | solution.py:512
  20.8 6.3 %collective-permute-start.1 = (s32[8]{0:T(128)S(1)}, s32[8]{0:T(128)S(1)}, u32[]{:S(2)}, u32[]{:S(2)}) collective-permute-start(s32[8]{0:T(128)S(1)} %pad_add_fusion), channel_id=1, source_target_pairs={{0,8},{4,12},{1,9},{5,13},{2,10},{6,14},{3,11},{7,15},{16,24},{20,... | collective-permute-start | bytes 104 | tf_op jit(solution)/shard_map/ppermute | solution.py:27
  23.7 25.5 %collective-permute-start.5 = (f32[4,256]{1,0:T(4,128)S(1)}, f32[4,256]{1,0:T(4,128)S(1)}, u32[]{:S(2)}, u32[]{:S(2)}) collective-permute-start(f32[4,256]{1,0:T(4,128)S(1)} %add.10), channel_id=1, source_target_pairs={{0,4},{4,8},{8,12},{1,5},{5,9},{9,13},{2,6},{6,10},{10,14},{3,7},{... | collective-permute-start | bytes 12296 | tf_op jit(solution)/shard_map/ppermute | solution.py:27
  47.7 3.7 %collective-permute-start.7 = (f32[32,128]{1,0:T(8,128)S(1)}, f32[32,128]{1,0:T(8,128)S(1)}, u32[]{:S(2)}, u32[]{:S(2)}) collective-permute-start(f32[32,128]{1,0:T(8,128)S(1)} %copy-done.3), channel_id=1, source_target_pairs={{0,2},{2,0},{1,3},{3,1},{4,6},{6,4},{5,7},{7,5},{8,10},{10,8},{9,1... | collective-permute-start | bytes 49160 | tf_op jit(solution)/shard_map/ppermute | solution.py:512
  49.2 6.4 %collective-permute-start.6 = (f32[8,256]{1,0:T(8,128)S(1)}, f32[8,256]{1,0:T(8,128)S(1)}, u32[]{:S(2)}, u32[]{:S(2)}) collective-permute-start(f32[8,256]{1,0:T(8,128)S(1)} %pad_maximum_fusion.1), channel_id=1, source_target_pairs={{0,8},{4,12},{1,9},{5,13},{2,10},{6,14},{3,11},{7,15},{16,24},{20,... | collective-permute-start | bytes 24584 | tf_op jit(solution)/shard_map/ppermute | solution.py:27

commit v3 on v2

--- a/solution.py
+++ b/solution.py
@@ -8,6 +8,7 @@
 from jax.experimental.pallas import tpu as pltpu
 from jax.sharding import PartitionSpec as P
 
+
 DILATION_STEP = 2
 PANEL = 32
 GROUP = 8
@@ -20,6 +21,12 @@
 
 def history(own, axis):
     count = lax.axis_size(axis)
+    if count <= 4:
+        held = [own]
+        for lag in range(1, count):
+            ring = [(i, (i + lag) % count) for i in range(count)]
+            held.append(lax.ppermute(own, axis, ring))
+        return jnp.concatenate(held, axis=0)
     held = own
     reach = 1
     while reach < count:
@@ -46,6 +53,12 @@
     )
 
 
+def exact(a, b, dims):
+    return lax.dot_general(
+        a, b, (dims, ((), ())), precision=precise, preferred_element_type=F32
+    )
+
+
 NN = ((1,), (0,))
 NT = ((1,), (1,))
 TN = ((0,), (0,))
@@ -55,11 +68,9 @@
     transition, update_map, quiet_root, observed_root, init_root,
     map_high, map_low, grams, first_gram,
 ):
-    for which, ref in ((0, transition), (1, update_map)):
-        high, low = split(ref[...])
-        map_high[which] = high
-        map_low[which] = low
-    for which, ref in ((0, quiet_root), (1, observed_root)):
+    for which, ref in enumerate((transition, update_map)):
+        map_high[which], map_low[which] = split(ref[...])
+    for which, ref in enumerate((quiet_root, observed_root)):
         pair = split(ref[...])
         grams[which] = three_pass(pair, pair, TN)
     pair = split(init_root[...])
@@ -80,7 +91,31 @@
     )(transition, update_map, quiet_root, observed_root, init_root)
 
 
-def upper_factor(gram, out, high, low):
+def pairs_kernel(map_high, map_low, grams, pair_high, pair_low, pair_gram):
+    maps = [(map_high[which], map_low[which]) for which in range(2)]
+    for later in range(2):
+        for earlier in range(2):
+            which = 2 * later + earlier
+            joined = three_pass(maps[later], maps[earlier], NN)
+            pair_high[which], pair_low[which] = split(joined)
+            carried = three_pass(maps[later], split(grams[earlier]), NN)
+            pair_gram[which] = three_pass(split(carried), maps[later], NT) + grams[later]
+
+
+def pair_maps(map_high, map_low, grams):
+    size = grams.shape[1]
+    return pl.pallas_call(
+        pairs_kernel,
+        out_shape=(
+            jax.ShapeDtypeStruct((4, size, size), BF16),
+            jax.ShapeDtypeStruct((4, size, size), BF16),
+            jax.ShapeDtypeStruct((4, size, size), F32),
+        ),
+        name="pair_maps",
+    )(map_high, map_low, grams)
+
+
+def upper_factor(gram, out, high, low, beside_work=()):
     size = gram.shape[0]
     halves = size // LANES
     tile = (GROUP, LANES)
@@ -88,6 +123,7 @@
     sub = lax.broadcasted_iota(jnp.int32, tile, 0)
     lane = lax.broadcasted_iota(jnp.int32, tile, 1)
     count = PANEL // GROUP
+    pending = list(beside_work)
     for top in range(0, size, PANEL):
         first = top // LANES
         start = first * LANES
@@ -105,6 +141,8 @@
         ]
         done = [[zero for _ in places] for _ in range(count)]
         for g in range(count):
+            if pending:
+                pending.pop(0)()
             base = top + GROUP * g
             here, at = base // LANES - first, base % LANES
             live = range(here, halves - first)
@@ -163,81 +201,117 @@
             rows_high, rows_low = split(out[top : top + PANEL, :])
             high[top : top + PANEL, :] = rows_high
             low[top : top + PANEL, :] = rows_low
-
-
-def covariance_kernel(steps, place, flags, map_high, map_low, grams, first_gram, out, gram, high, low):
+    for work in pending:
+        work()
+
+
+def recursion_kernel(steps, span, place, flags, span_high, span_low, span_gram, first_gram, gram):
     index = place[0]
+    pieces = steps // span
     gram[...] = first_gram[...]
 
-    def step(t, carry):
-        flag = flags[(index - t // steps) * steps + t % steps]
-        map_pair = (map_high[flag], map_low[flag])
+    def step(n, carry):
+        at = (index - n // pieces) * steps + (n % pieces) * span
+        which = flags[at]
+        for later in range(1, span):
+            which = which + flags[at + later] * 2**later
+        map_pair = (span_high[which], span_low[which])
         carried = three_pass(map_pair, split(gram[...]), NN)
-        gram[...] = three_pass(split(carried), map_pair, NT) + grams[flag]
+        gram[...] = three_pass(split(carried), map_pair, NT) + span_gram[which]
         return carry
 
-    lax.fori_loop(0, (index + 1) * steps, step, 0)
-    upper_factor(gram, out, high, low)
-
-
-def covariance(place, flags, steps, map_high, map_low, grams, first_gram):
-    size = first_gram.shape[0]
+    lax.fori_loop(0, (index + 1) * pieces, step, 0)
+
+
+def recursion(place, flags, steps, span, span_high, span_low, span_gram, first_gram):
     vmem = pl.BlockSpec(memory_space=pltpu.VMEM)
     smem = pl.BlockSpec(memory_space=pltpu.SMEM)
 
     def kernel(*refs):
-        covariance_kernel(steps, *refs)
+        recursion_kernel(steps, span, *refs)
 
     return pl.pallas_call(
         kernel,
-        out_shape=jax.ShapeDtypeStruct((size, size), F32),
+        out_shape=jax.ShapeDtypeStruct(first_gram.shape, F32),
         in_specs=[smem, smem, vmem, vmem, vmem, vmem],
         out_specs=vmem,
+        name="recursion",
+    )(place, flags, span_high, span_low, span_gram, first_gram)
+
+
+def factor_kernel(
+    steps, span, place, flags, gram, map_high, map_low, span_high, span_low, shifts, init_mean,
+    out, mean_out, high, low, carried,
+):
+    index = place[0]
+    size = gram.shape[0]
+    blocks = shifts.shape[0]
+    state = {"mean": jnp.broadcast_to(init_mean[...], (GROUP, size))}
+
+    def first():
+        rows = split(jnp.concatenate([shifts[block] for block in range(blocks)], axis=0))
+        for which in range(2):
+            carried[which] = three_pass(rows, (map_high[which], map_low[which]), NT)
+
+    def one_step(block, t):
+        at = block * steps + t
+        flag = flags[at]
+        mean = three_pass(split(state["mean"]), (map_high[flag], map_low[flag]), NT)
+        return mean + shifts[block, t : t + 1, :]
+
+    def work(block, t):
+        def run():
+            if block == 0:
+                mean = one_step(block, t)
+                mean_out[t : t + 1, :] = mean[0:1]
+                if span == 1:
+                    state["mean"] = mean
+                    return
+            if span == 1:
+                mean = one_step(block, t)
+            else:
+                at = block * steps + t
+                which = flags[at] + 2 * flags[at + 1]
+                mean = three_pass(split(state["mean"]), (span_high[which], span_low[which]), NT)
+                row = block * shifts.shape[1] + t
+                mean = mean + carried[flags[at + 1], row : row + 1, :]
+                mean = mean + shifts[block, t + 1 : t + 2, :]
+                if block == 0:
+                    mean_out[t + 1 : t + 2, :] = mean[0:1]
+            state["mean"] = mean if block == 0 else jnp.where(block <= index, mean, state["mean"])
+
+        return run
+
+    jobs = [first] if span == 2 else []
+    jobs += [work(block, t) for block in reversed(range(blocks)) for t in range(0, steps, span)]
+    upper_factor(gram, out, high, low, jobs)
+
+
+def factor(
+    place, flags, steps, span, gram, map_high, map_low, span_high, span_low, shifts, init_mean
+):
+    size = gram.shape[0]
+    vmem = pl.BlockSpec(memory_space=pltpu.VMEM)
+    smem = pl.BlockSpec(memory_space=pltpu.SMEM)
+
+    def kernel(*refs):
+        factor_kernel(steps, span, *refs)
+
+    return pl.pallas_call(
+        kernel,
+        out_shape=(
+            jax.ShapeDtypeStruct((size, size), F32),
+            jax.ShapeDtypeStruct((steps, size), F32),
+        ),
+        in_specs=[smem, smem] + [vmem] * 7,
+        out_specs=(vmem, vmem),
         scratch_shapes=[
-            pltpu.VMEM((size, size), F32),
             pltpu.VMEM((size, size), BF16),
             pltpu.VMEM((size, size), BF16),
+            pltpu.VMEM((2, shifts.shape[0] * shifts.shape[1], size), F32),
         ],
-        name="covariance",
-    )(place, flags, map_high, map_low, grams, first_gram)
-
-
-def means_kernel(steps, place, flags, map_high, map_low, shifts, init_mean, out):
-    index = place[0]
-    size = init_mean.shape[1]
-
-    def step(t, mean):
-        at = (index - t // steps) * steps + t % steps
-        flag = flags[at]
-        mean = three_pass(split(mean), (map_high[flag], map_low[flag]), NT)
-        mean = mean + jnp.broadcast_to(shifts[pl.ds(at, 1), :], mean.shape)
-
-        @pl.when(t // steps == index)
-        def _():
-            out[pl.ds(t % steps, 1), :] = mean[0:1]
-
-        return mean
-
-    lax.fori_loop(
-        0, (index + 1) * steps, step, jnp.broadcast_to(init_mean[...], (GROUP, size))
-    )
-
-
-def means(place, flags, steps, map_high, map_low, shifts, init_mean):
-    size = init_mean.shape[0]
-    vmem = pl.BlockSpec(memory_space=pltpu.VMEM)
-    smem = pl.BlockSpec(memory_space=pltpu.SMEM)
-
-    def kernel(*refs):
-        means_kernel(steps, *refs)
-
-    return pl.pallas_call(
-        kernel,
-        out_shape=jax.ShapeDtypeStruct((steps, size), F32),
-        in_specs=[smem, smem, vmem, vmem, vmem, vmem],
-        out_specs=vmem,
-        name="means",
-    )(place, flags, map_high, map_low, shifts, init_mean[None])
+        name="factor",
+    )(place, flags, gram, map_high, map_low, span_high, span_low, shifts, init_mean[None])
 
 
 LAGS = (0, DILATION_STEP, 2 * DILATION_STEP, -DILATION_STEP, -2 * DILATION_STEP)
@@ -291,9 +365,9 @@
     right_edge = (column >= columns - DILATION_STEP).astype(F32).astype(BF16)
     blank = jnp.zeros((rows, 2 * LANES - 5 * rows), F32)
     for c in range(block):
-        weights = taps[first + c, 0] * pooled[0]
+        weights = taps[0, first + c] * pooled[0]
         for k in range(1, len(TAPS)):
-            weights = weights + taps[first + c, k] * pooled[k]
+            weights = weights + taps[k, first + c] * pooled[k]
         gram = jnp.zeros((rows, 5 * rows), F32)
         for t in range(steps):
             frame = frames[t, c]
@@ -384,42 +458,81 @@
     return np.pad(table, ((0, 0), (0, LANES - pairs)))
 
 
-def finish_kernel(
-    scale, flags, edges, above, below, part, stats, taps, pooling, gain, table,
-    gain_part, gradient, values,
-):
-    steps, _, channels, columns = edges.shape
-    rows = pooling.shape[0]
+def beside_tile():
     place, count = lax.axis_index("space"), lax.axis_size("space")
     has_above = jnp.where(place > 0, 1.0, 0.0).astype(F32)
     has_below = jnp.where(place < count - 1, 1.0, 0.0).astype(F32)
+    return has_above, has_below
+
+
+def spread():
+    shape = (len(TAPS), LANES)
+    source = lax.broadcasted_iota(jnp.int32, shape, 1)
+    return source, lax.broadcasted_iota(jnp.int32, shape, 0)
+
+
+def gain_kernel(flags, above, below, part, taps, pooling, gain, gain_part):
+    steps, _, channels, columns = above.shape
+    rows = pooling.shape[0]
+    has_above, has_below = beside_tile()
+    source, tap = spread()
+    tap_columns = exact(taps[...], (source == tap).astype(F32), TN)
     halo_weights = []
-    for side, (a, start, has) in enumerate(
-        ((-1, 0, has_above), (1, rows - DILATION_STEP, has_below))
-    ):
+    for a, start, has in ((-1, 0, has_above), (1, rows - DILATION_STEP, has_below)):
         for r in range(DILATION_STEP):
             value = jnp.zeros((channels, columns), F32)
             for b in (-1, 0, 1):
                 k = TAPS.index((a, b))
                 shifted = moved(pooling[start + r : start + r + 1, :], -DILATION_STEP * b, 1)
-                value = value + taps[:, k : k + 1] * shifted
+                value = value + tap_columns[:, k : k + 1] * shifted
             halo_weights.append(value * has)
-    sums = [[None] * 5 for _ in range(2)]
-    ones = jnp.ones((GROUP, LANES), BF16)
     row_sums = []
     for t in range(steps):
+        total = jnp.zeros((channels, columns), F32)
+        for r in range(DILATION_STEP):
+            total = total + above[t, r].astype(F32) * halo_weights[r]
+            total = total + below[t, r].astype(F32) * halo_weights[DILATION_STEP + r]
+        row_sums.append(part[t] + folded(total))
+    ones = jnp.ones((GROUP, LANES), BF16)
+    high, low = split(jnp.concatenate(row_sums, axis=0))
+    tile_sums = contract(ones, high, NT) + contract(ones, low, NT)
+    shape = (GROUP, steps * channels)
+    owner = lax.broadcasted_iota(jnp.int32, shape, 1) // channels
+    step = lax.broadcasted_iota(jnp.int32, shape, 0)
+    seen = jnp.zeros(shape, F32)
+    for t in range(steps):
+        seen = jnp.where((owner == t) & (step == t), flags[t].astype(F32), seen)
+    gains = jnp.concatenate([gain[...]] * steps, axis=0)
+    product = three_pass(split(tile_sums * seen), split(gains), NN)
+    gain_part[...] = product[:steps]
+
+
+def gain_sums(flags, above, below, part, taps, pooling, gain):
+    vmem = pl.BlockSpec(memory_space=pltpu.VMEM)
+    smem = pl.BlockSpec(memory_space=pltpu.SMEM)
+    return pl.pallas_call(
+        gain_kernel,
+        out_shape=jax.ShapeDtypeStruct((above.shape[0], gain.shape[1]), F32),
+        in_specs=[smem] + [vmem] * 6,
+        out_specs=vmem,
+        name="gain_sums",
+    )(flags, above, below, part, taps, pooling, gain)
+
+
+def gradient_kernel(
+    scale, rows, flags, edges, above, below, stats, taps, table, gradient, values
+):
+    steps, _, channels, columns = edges.shape
+    has_above, has_below = beside_tile()
+    sums = [[None] * 5 for _ in range(2)]
+    for t in range(steps):
         flag = flags[t].astype(F32)
-        upper = [above[t, r].astype(F32) for r in range(DILATION_STEP)]
-        lower = [below[t, r].astype(F32) for r in range(DILATION_STEP)]
-        total = jnp.zeros((channels, columns), F32)
-        for value, weight in zip(upper + lower, halo_weights):
-            total = total + value * weight
-        row_sums.append(part[t] + folded(total))
         for r in range(DILATION_STEP):
             near_top = edges[t, DILATION_STEP + r].astype(F32)
             far_bottom = edges[t, 2 * DILATION_STEP + r].astype(F32)
             near_bottom = edges[t, 3 * DILATION_STEP + r].astype(F32)
-            high, low = upper[r] * (flag * has_above), lower[r] * (flag * has_below)
+            high = above[t, r].astype(F32) * (flag * has_above)
+            low = below[t, r].astype(F32) * (flag * has_below)
             for n in range(-2, 3):
                 shifted_low = moved(low, DILATION_STEP * n, 1)
                 shifted_high = moved(high, -DILATION_STEP * n, 1)
@@ -428,19 +541,8 @@
                 for which, value in ((0, one), (1, two)):
                     old = sums[which][n]
                     sums[which][n] = value if old is None else old + value
-    high, low = split(jnp.concatenate(row_sums, axis=0))
-    tile_sums = contract(ones, high, NT) + contract(ones, low, NT)
-    shape = (GROUP, steps * channels)
-    owner = lax.broadcasted_iota(jnp.int32, shape, 1) // channels
-    step = lax.broadcasted_iota(jnp.int32, shape, 0)
-    seen = jnp.zeros(shape, F32)
-    for t in range(steps):
-        seen = jnp.where((owner == t) & (step == t), flags[t].astype(F32), seen)
-    gains = jnp.concatenate([gain[...]] * steps, axis=1)
-    product = three_pass(split(tile_sums * seen), split(gains), NT)
-    gain_part[...] = product[:steps]
     values[:, : KINDS * LANES] = stats[...]
-    lane = lax.broadcasted_iota(jnp.int32, (channels, LANES), 1) % rows
+    lane = lax.rem(lax.broadcasted_iota(jnp.int32, (channels, LANES), 1), rows)
     outside = jnp.where(lane < DILATION_STEP, 1.0 - has_above, 0.0)
     outside = jnp.where(lane >= rows - DILATION_STEP, 1.0 - has_below, outside)
     at = KINDS * LANES
@@ -450,48 +552,43 @@
     for which in range(2):
         centre = sums[which][0]
         pieces = [centre[:, :LANES], centre[:, columns - LANES :]]
+        pieces += [folded(sums[which][n]) for n in (1, 2, -1, -2)]
         for inner in range(LANES, columns - LANES, LANES):
-            pieces[2] = pieces[2] + centre[:, inner : inner + LANES]
-        pieces += [folded(sums[which][n]) for n in (1, 2, -1, -2)]
+            middle = jnp.sum(centre[:, inner : inner + LANES], axis=1, keepdims=True)
+            pieces[0] = pieces[0] + jnp.where(lane_of(channels) == LANES // 2, middle, 0.0)
         for piece in pieces:
             values[:, at : at + LANES] = piece
             at += LANES
     high, low = split(values[...])
     pairs = contract(high, table[...], NN) + contract(low, table[...], NN)
-    tap_count = len(TAPS)
-    source = lax.broadcasted_iota(jnp.int32, (tap_count, LANES), 1)
-    spread_row = lax.broadcasted_iota(jnp.int32, (tap_count, LANES), 0)
-    spread = (source // tap_count == spread_row).astype(F32)
-    pair = lax.broadcasted_iota(jnp.int32, (LANES, LANES), 0)
-    target = lax.broadcasted_iota(jnp.int32, (LANES, LANES), 1)
-    gather = (pair % tap_count == target).astype(F32)
-    weights = jnp.dot(taps[...], spread, precision=precise, preferred_element_type=F32)
-    result = jnp.dot(pairs * weights, gather, precision=precise, preferred_element_type=F32)
-    gradient[...] = result * scale
-
-
-def finish(flags, edges, above, below, part, stats, taps, pooling, gain):
-    steps, _, channels, columns = edges.shape
-    rows = pooling.shape[0]
+    source, tap = spread()
+    weights = exact(taps[...], (source // len(TAPS) == tap).astype(F32), TN)
+    gathered = (source % len(TAPS) == tap).astype(F32)
+    gradient[...] = exact(gathered, pairs * weights, NT) * scale
+
+
+def lane_of(channels):
+    return lax.broadcasted_iota(jnp.int32, (channels, LANES), 1)
+
+
+def tap_sums(flags, edges, above, below, stats, taps, rows):
+    _, _, channels, columns = edges.shape
     scale = 1.0 / (rows * lax.axis_size("space") * columns)
     table = jnp.asarray(selection(rows), BF16)
     vmem = pl.BlockSpec(memory_space=pltpu.VMEM)
     smem = pl.BlockSpec(memory_space=pltpu.SMEM)
 
     def kernel(*refs):
-        finish_kernel(scale, *refs)
+        gradient_kernel(scale, rows, *refs)
 
     return pl.pallas_call(
         kernel,
-        out_shape=(
-            jax.ShapeDtypeStruct((steps, gain.shape[0]), F32),
-            jax.ShapeDtypeStruct((channels, LANES), F32),
-        ),
-        in_specs=[smem] + [vmem] * 9,
-        out_specs=(vmem, vmem),
+        out_shape=jax.ShapeDtypeStruct((len(TAPS), channels), F32),
+        in_specs=[smem] + [vmem] * 6,
+        out_specs=vmem,
         scratch_shapes=[pltpu.VMEM((channels, table.shape[0]), F32)],
-        name="finish",
-    )(flags, edges, above, below, part, stats, taps, pooling, gain, table)
+        name="tap_sums",
+    )(flags, edges, above, below, stats, taps, table)
 
 
 def beside(edges, axis):
@@ -526,25 +623,35 @@
     init_root,
     observed,
 ):
-    step_count, channels, rows, columns = frames.shape
+    step_count, _, rows, _ = frames.shape
     place = lax.axis_index("tm").astype(jnp.int32)[None]
     edges = jnp.concatenate([frames[:, :, :EDGE], frames[:, :, rows - EDGE :]], axis=2)
     edges = edges.transpose(0, 2, 1, 3)
     above, below = beside(edges, "space")
-    flags = history(observed, "tm")
-    part, stats = frame_sums(conv_taps, observed, frames, pooling)
+    taps, gain = conv_taps.T, gain_matrix.T
+    span = 2 if step_count % 2 == 0 else 1
+    part, stats = frame_sums(taps, observed, frames, pooling)
+    gain_part = gain_sums(observed, above, below, part, taps, pooling, gain)
     map_high, map_low, grams, first_gram = prepare(
         transition, update_map, quiet_root, observed_root, init_root
     )
-    gain_part, gradient = finish(
-        observed, edges, above, below, part, stats, conv_taps, pooling, gain_matrix
+    shifts = total(gain_part, "chan")
+    gradient = tap_sums(observed, edges, above, below, stats, taps, rows)
+    shifts = total(shifts, "space")
+    flag_row = jnp.pad(observed.astype(F32)[None], ((0, 0), (0, shifts.shape[1] - step_count)))
+    held = history(jnp.concatenate([shifts, flag_row], axis=0)[None], "tm")
+    flags = held[:, step_count, :step_count].astype(jnp.int32).reshape(-1)
+    if span == 2:
+        span_high, span_low, span_gram = pair_maps(map_high, map_low, grams)
+    else:
+        span_high, span_low, span_gram = map_high, map_low, grams
+    gradient = total(gradient, "space")
+    gram = recursion(place, flags, step_count, span, span_high, span_low, span_gram, first_gram)
+    root, filtered_means = factor(
+        place, flags, step_count, span, gram,
+        map_high, map_low, span_high, span_low, held, init_mean,
     )
-    shifts = total(total(gain_part, "chan"), "space")
-    gradient = total(gradient, "space")
-    all_shifts = history(shifts, "tm")
-    root = covariance(place, flags, step_count, map_high, map_low, grams, first_gram)
-    filtered_means = means(place, flags, step_count, map_high, map_low, all_shifts, init_mean)
-    return (filtered_means, root[None], gradient[None, :, : len(TAPS)])
+    return (filtered_means, root[None], gradient.T[None])
 
 
 def solution(mesh):

time: 62.3 us -> 52.5 us (0.84)
  the two profiles are of different devices: /device:TPU:28 before, /device:TPU:0 now
where the time goes in v3:
time: 52.5 us; the launch traced here: 52.1 us
  Pallas kernels  32.2 us (61%)
  starting transfers between devices  9.73 us (19%)
  waiting for transfers between devices  4.52 us (9%)
  local copies, waits for them, and re-layouts  3.39 us (6%)
  other arithmetic  1.5 us (3%)
  between operations  0.72 us (1%)
    pallas_call x1, Pallas kernels, factor(): pl.pallas_call(kernel, out_shape=(jax.ShapeDtypeStruct((size, size), F32)...  10.6 us
    pallas_call x1, Pallas kernels, frame_sums(): pl.pallas_call(frames_kernel, grid=(channels // block,), out_shape=(jax.S...  5.68 us
    ppermute x3, starting transfers between devices, history(): held.append(lax.ppermute(own, axis, ring))  4.67 us
    pallas_call x1, Pallas kernels, pair_maps(): pl.pallas_call(pairs_kernel, out_shape=(jax.ShapeDtypeStruct((4, size, si...  4.19 us
    pallas_call x1, Pallas kernels, recursion(): pl.pallas_call(kernel, out_shape=jax.ShapeDtypeStruct(first_gram.shape, F...  3.51 us
    ppermute x3, waiting for transfers between devices, history(): held.append(lax.ppermute(own, axis, ring))  3.13 us
    pallas_call x1, Pallas kernels, tap_sums(): pl.pallas_call(kernel, out_shape=jax.ShapeDtypeStruct((len(TAPS), channel...  3.1 us
    ppermute x1, starting transfers between devices, beside(): got = lax.ppermute(sent, axis, [(0, 1), (1, 0)])  3.03 us
  transfers between devices with their start and end apart: 7, of which 3 were waited for; matrix products, arithmetic and copies ran while one was open for 3% of the time, Pallas kernels for 30%

profile of v3, /device:TPU:0, one launch (start us, length us, event | category | flops | bytes accessed | tf_op | source)
XLA Modules:
  0.0 52.1 jit_solution(15160103926996221363)
XLA Ops:
  0.6 1.4 %fusion.2 = (bf16[4,32,4,256]{3,2,1,0:T(4,128)(2,1)S(1)}, bf16[4,32,4,256]{3,2,1,0:T(4,128)(2,1)S(1)}) fusion(bf16[4,32,32,256]{3,2,1,0:T(8,128)(2,1)} %frames.1), kind=kLoop, calls=%fused_computation.10 | loop fusion | bytes 1048576 | tf_op jit(solution)/shard_map/slice | solution.py:628
  2.1 0.0 copy-start.3
  2.2 0.0 copy-start
  2.2 3.0 %collective-permute-start = (bf16[4,2,32,256]{3,2,1,0:T(8,128)(2,1)S(1)}, bf16[4,2,32,256]{3,2,1,0:T(8,128)(2,1)S(1)}, u32[]{:S(2)}, u32[]{:S(2)}) collective-permute-start(bf16[4,2,32,256]{3,2,1,0:T(8,128)(2,1)S(1)} %slice_select_fusion), channel_id=1, source_target_pairs={{0,2},{2,0},{1,3},{3,1},{4,6},{6,4},{5,7},{7,5},{8,10},{10,8},{9,1... | collective-permute-start | bytes 393224 | tf_op jit(solution)/shard_map/ppermute | solution.py:600
  5.3 5.7 %frame_sums.1 = (f32[4,32,128]{2,1,0:T(8,128)}, f32[32,1024]{1,0:T(8,128)}) custom-call(f32[9,32]{1,0:T(8,128)} %bitcast.15, s32[4]{0:T(128)} %refs_0_.1, bf16[4,32,32,256]{3,2,1,0:T(8,128)(2,1)} %frames.1, f32[32,256]{1,0:T(8,128)} %pooling.3), custom_call_target="tpu_custom_call" | custom-call | tf_op jit(solution)/shard_map/frame_sums/pallas_call | solution.py:400
  11.0 0.0 collective-permute-done.above.below.refs_2_.refs_3_
  11.0 0.0 copy-start.1
  11.0 0.6 %copy-done.1 = bf16[4,2,32,256]{3,2,1,0:T(8,128)(2,1)} copy-done((bf16[4,2,32,256]{3,2,1,0:T(8,128)(2,1)}, bf16[4,2,32,256]{3,2,1,0:T(8,128)(2,1)S(1)}, u32[]{:S(2)}) %copy-start.1) | copy-done | bytes 131096
  11.6 2.3 %gain_sums.1 = f32[4,256]{1,0:T(4,128)} custom-call(s32[4]{0:T(128)} %refs_0_.1, bf16[4,2,32,256]{3,2,1,0:T(8,128)(2,1)} %copy-done.1, bf16[4,2,32,256]{3,2,1,0:T(8,128)(2,1)} %copy-done.1, f32[4,32,128]{2,1,0:T(8,128)} %get-tuple-element.14.part, f32[9,32]{1,0:T(8,128)} %bitcast.16, f32[32,256]{1,0:T(8,128)} %pooling.3, f32[32,256]{1,0:T(8,128)} %bitcast.18), custom_call_target="tpu_custom_call" | custom-call | tf_op jit(solution)/shard_map/gain_sums/pallas_call | solution.py:513
  13.9 0.0 collective-permute-start.1
  13.9 1.4 %collective-permute-done.1 = f32[4,256]{1,0:T(4,128)S(1)} collective-permute-done((f32[4,256]{1,0:T(4,128)}, f32[4,256]{1,0:T(4,128)S(1)}, u32[]{:S(2)}, u32[]{:S(2)}) %collective-permute-start.1) | collective-permute-done | bytes 4128 | tf_op jit(solution)/shard_map/ppermute | solution.py:609
  15.3 0.7 %add.11 = f32[4,256]{1,0:T(4,128)S(1)} add(f32[4,256]{1,0:T(4,128)} %gain_sums.1, f32[4,256]{1,0:T(4,128)S(1)} %collective-permute-done.1) | non-fusion elementwise | flops 1024 | bytes 12288 | tf_op jit(solution)/shard_map/add | solution.py:609
  15.9 0.1 collective-permute-start.2
  16.0 0.0 copy-done.3
  16.1 2.8 %prepare.1 = (bf16[2,256,256]{2,1,0:T(8,128)(2,1)}, bf16[2,256,256]{2,1,0:T(8,128)(2,1)}, f32[2,256,256]{2,1,0:T(8,128)}, f32[256,256]{1,0:T(8,128)}) custom-call(f32[256,256]{1,0:T(8,128)} %transition.1, f32[256,256]{1,0:T(8,128)} %update_map.1, f32[256,256]{1,0:T(8,128)} %quiet_root.1, f32[256,256]{1,0:T(8,128)} %observed_root.1, f32[256,256]{1,0:T(8,128)} %init_root.1), custom_call_target="tpu_custom_call" | custom-call | tf_op jit(solution)/shard_map/prepare/pallas_call | solution.py:82
  18.9 0.0 copy-done
  18.9 4.2 %pair_maps.1 = (bf16[4,256,256]{2,1,0:T(8,128)(2,1)}, bf16[4,256,256]{2,1,0:T(8,128)(2,1)}, f32[4,256,256]{2,1,0:T(8,128)}) custom-call(bf16[2,256,256]{2,1,0:T(8,128)(2,1)} %get-tuple-element.15.map_high.refs_3_, bf16[2,256,256]{2,1,0:T(8,128)(2,1)} %get-tuple-element.16.map_low.refs_4_, f32[2,256,256]{2,1,0:T(8,128)} %get-tuple-element.17.grams), custom_call_target="tpu_custom_call" | custom-call | tf_op jit(solution)/shard_map/pair_maps/pallas_call | solution.py:107
  23.1 3.1 %tap_sums.1 = f32[9,32]{1,0:T(8,128)} custom-call(s32[4]{0:T(128)} %refs_0_.1, bf16[4,8,32,256]{3,2,1,0:T(8,128)(2,1)} %copy-done, bf16[4,2,32,256]{3,2,1,0:T(8,128)(2,1)} %copy-done.1, bf16[4,2,32,256]{3,2,1,0:T(8,128)(2,1)} %copy-done.1, f32[32,1024]{1,0:T(8,128)} %get-tuple-element.24.refs_4_, f32[9,32]{1,0:T(8,128)} %bitcast.17, ...), custom_call_target="tpu_custom_call" | custom-call | tf_op jit(solution)/shard_map/tap_sums/pallas_call | solution.py:584
  26.2 1.9 %collective-permute-start.6 = (f32[9,32]{1,0:T(8,128)}, f32[9,32]{1,0:T(8,128)S(1)}, u32[]{:S(2)}, u32[]{:S(2)}) collective-permute-start(f32[9,32]{1,0:T(8,128)} %tap_sums.1), channel_id=1, source_target_pairs={{0,2},{2,0},{1,3},{3,1},{4,6},{6,4},{5,7},{7,5},{8,10},{10,8},{9,1... | collective-permute-start | bytes 3464 | tf_op jit(solution)/shard_map/ppermute | solution.py:609
  28.1 0.0 collective-permute-done.2
  28.1 3.7 %collective-permute-start.5 = (f32[1,5,256]{2,1,0:T(8,128)S(1)}, f32[1,5,256]{2,1,0:T(8,128)S(1)}, u32[]{:S(2)}, u32[]{:S(2)}) collective-permute-start(f32[1,5,256]{2,1,0:T(8,128)S(1)} %fusion), channel_id=1, source_target_pairs={{0,12},{4,0},{8,4},{12,8},{1,13},{5,1},{9,5},{13,9},{2,14},{6,2},{... | collective-permute-start | bytes 15368 | tf_op jit(solution)/shard_map/ppermute | solution.py:28
  31.8 0.0 collective-permute-start.4
  31.8 1.0 %collective-permute-start.3 = (f32[1,5,256]{2,1,0:T(8,128)S(1)}, f32[1,5,256]{2,1,0:T(8,128)S(1)}, u32[]{:S(2)}, u32[]{:S(2)}) collective-permute-start(f32[1,5,256]{2,1,0:T(8,128)S(1)} %fusion), channel_id=1, source_target_pairs={{0,4},{4,8},{8,12},{12,0},{1,5},{5,9},{9,13},{13,1},{2,6},{6,10},{... | collective-permute-start | bytes 15368 | tf_op jit(solution)/shard_map/ppermute | solution.py:28
  32.8 0.0 collective-permute-done.6
  32.8 0.7 %add_bitcast_fusion = f32[1,32,9]{1,2,0:T(8,128)S(1)} fusion(f32[9,32]{1,0:T(8,128)} %tap_sums.1, f32[9,32]{1,0:T(8,128)S(1)} %collective-permute-done.6), kind=kLoop, calls=%fused_computation.6 | loop fusion | flops 288 | bytes 3456 | tf_op jit(solution)/shard_map/broadcast_in_dim | solution.py:654
  33.5 0.6 %copy.17 = f32[1,32,9]{1,0,2:T(1,128)} copy(f32[1,32,9]{1,2,0:T(8,128)S(1)} %add_bitcast_fusion) | data formatting | bytes 2304
  34.1 0.0 collective-permute-done.5
  34.1 2.2 %collective-permute-done.4 = f32[1,5,256]{2,1,0:T(8,128)S(1)} collective-permute-done((f32[1,5,256]{2,1,0:T(8,128)S(1)}, f32[1,5,256]{2,1,0:T(8,128)S(1)}, u32[]{:S(2)}, u32[]{:S(2)}) %collective-permute-start.4) | collective-permute-done | bytes 5152 | tf_op jit(solution)/shard_map/ppermute | solution.py:28
  36.3 0.9 %collective-permute-done.3 = f32[1,5,256]{2,1,0:T(8,128)S(1)} collective-permute-done((f32[1,5,256]{2,1,0:T(8,128)S(1)}, f32[1,5,256]{2,1,0:T(8,128)S(1)}, u32[]{:S(2)}, u32[]{:S(2)}) %collective-permute-start.3) | collective-permute-done | bytes 5152 | tf_op jit(solution)/shard_map/ppermute | solution.py:28
  37.3 0.0 copy-start.2
  37.3 0.7 %convert_element_type.14.refs_1_ = s32[16]{0:T(128)} reshape(s32[4,4]{1,0:T(4,128)S(1)} %fusion.1) | data formatting | bytes 128 | tf_op jit(solution)/shard_map/convert_element_type | solution.py:643
  37.9 3.5 %recursion.1.refs_2_ = f32[256,256]{1,0:T(8,128)} custom-call(s32[1]{0:T(128)} %bitcast.refs_0_, s32[16]{0:T(128)} %convert_element_type.14.refs_1_, bf16[4,256,256]{2,1,0:T(8,128)(2,1)} %get-tuple-element.18.refs_2_.refs_5_, bf16[4,256,256]{2,1,0:T(8,128)(2,1)} %get-tuple-element.19.refs_3_.refs_6_, f32[4,256,256]{2,1,0:T(8,128)} %get-tuple-element.20.refs_4_, ...), custom_call_target="tpu_custom_call" | custom-call | tf_op jit(solution)/shard_map/recursion/pallas_call | solution.py:233
  41.5 0.0 copy-done.2
  41.5 10.6 %factor.1 = (f32[256,256]{1,0:T(8,128)}, f32[4,256]{1,0:T(4,128)}) custom-call(s32[1]{0:T(128)} %bitcast.refs_0_, s32[16]{0:T(128)} %convert_element_type.14.refs_1_, f32[256,256]{1,0:T(8,128)} %recursion.1.refs_2_, bf16[2,256,256]{2,1,0:T(8,128)(2,1)} %get-tuple-element.15.map_high.refs_3_, bf16[2,256,256]{2,1,0:T(8,128)(2,1)} %get-tuple-element.16.map_low.refs_4_, ...), custom_call_target="tpu_custom_call" | custom-call | tf_op jit(solution)/shard_map/factor/pallas_call | solution.py:300
  (9 shorter events, 0.2 us)
Async XLA Ops:
  2.1 13.9 %copy-start.3 = (s32[4]{0:T(128)S(1)}, s32[4]{0:T(128)}, u32[]{:S(2)}) copy-start(s32[4]{0:T(128)} %refs_0_.1) | copy-start | bytes 52
  2.2 16.7 %copy-start = (bf16[4,8,32,256]{3,2,1,0:T(8,128)(2,1)}, bf16[4,8,32,256]{3,2,1,0:T(8,128)(2,1)S(1)}, u32[]{:S(2)}) copy-start(bf16[4,8,32,256]{3,2,1,0:T(8,128)(2,1)S(1)} %maximum_bitcast_fusion.refs_1_) | copy-start | bytes 1572868
  2.2 8.7 %collective-permute-start = (bf16[4,2,32,256]{3,2,1,0:T(8,128)(2,1)S(1)}, bf16[4,2,32,256]{3,2,1,0:T(8,128)(2,1)S(1)}, u32[]{:S(2)}, u32[]{:S(2)}) collective-permute-start(bf16[4,2,32,256]{3,2,1,0:T(8,128)(2,1)S(1)} %slice_select_fusion), channel_id=1, source_target_pairs={{0,2},{2,0},{1,3},{3,1},{4,6},{6,4},{5,7},{7,5},{8,10},{10,8},{9,1... | collective-permute-start | bytes 393224 | tf_op jit(solution)/shard_map/ppermute | solution.py:600
  11.0 0.6 %copy-start.1 = (bf16[4,2,32,256]{3,2,1,0:T(8,128)(2,1)}, bf16[4,2,32,256]{3,2,1,0:T(8,128)(2,1)S(1)}, u32[]{:S(2)}) copy-start(bf16[4,2,32,256]{3,2,1,0:T(8,128)(2,1)S(1)} %collective-permute-done.above.below.refs_2_.refs_3_) | copy-start | bytes 393220
  13.9 1.4 %collective-permute-start.1 = (f32[4,256]{1,0:T(4,128)}, f32[4,256]{1,0:T(4,128)S(1)}, u32[]{:S(2)}, u32[]{:S(2)}) collective-permute-start(f32[4,256]{1,0:T(4,128)} %gain_sums.1), channel_id=1, source_target_pairs={{0,1},{1,0},{2,3},{3,2},{4,5},{5,4},{6,7},{7,6},{8,9},{9,8},{10,11... | collective-permute-start | bytes 12296 | tf_op jit(solution)/shard_map/ppermute | solution.py:609
  15.9 12.2 %collective-permute-start.2 = (f32[4,256]{1,0:T(4,128)S(1)}, f32[4,256]{1,0:T(4,128)S(1)}, u32[]{:S(2)}, u32[]{:S(2)}) collective-permute-start(f32[4,256]{1,0:T(4,128)S(1)} %add.11), channel_id=1, source_target_pairs={{0,2},{2,0},{1,3},{3,1},{4,6},{6,4},{5,7},{7,5},{8,10},{10,8},{9,1... | collective-permute-start | bytes 12296 | tf_op jit(solution)/shard_map/ppermute | solution.py:609
  26.2 6.6 %collective-permute-start.6 = (f32[9,32]{1,0:T(8,128)}, f32[9,32]{1,0:T(8,128)S(1)}, u32[]{:S(2)}, u32[]{:S(2)}) collective-permute-start(f32[9,32]{1,0:T(8,128)} %tap_sums.1), channel_id=1, source_target_pairs={{0,2},{2,0},{1,3},{3,1},{4,6},{6,4},{5,7},{7,5},{8,10},{10,8},{9,1... | collective-permute-start | bytes 3464 | tf_op jit(solution)/shard_map/ppermute | solution.py:609
  28.1 6.0 %collective-permute-start.5 = (f32[1,5,256]{2,1,0:T(8,128)S(1)}, f32[1,5,256]{2,1,0:T(8,128)S(1)}, u32[]{:S(2)}, u32[]{:S(2)}) collective-permute-start(f32[1,5,256]{2,1,0:T(8,128)S(1)} %fusion), channel_id=1, source_target_pairs={{0,12},{4,0},{8,4},{12,8},{1,13},{5,1},{9,5},{13,9},{2,14},{6,2},{... | collective-permute-start | bytes 15368 | tf_op jit(solution)/shard_map/ppermute | solution.py:28
  31.8 4.5 %collective-permute-start.4 = (f32[1,5,256]{2,1,0:T(8,128)S(1)}, f32[1,5,256]{2,1,0:T(8,128)S(1)}, u32[]{:S(2)}, u32[]{:S(2)}) collective-permute-start(f32[1,5,256]{2,1,0:T(8,128)S(1)} %fusion), channel_id=1, source_target_pairs={{0,8},{4,12},{8,0},{12,4},{1,9},{5,13},{9,1},{13,5},{2,10},{6,14},... | collective-permute-start | bytes 15368 | tf_op jit(solution)/shard_map/ppermute | solution.py:28
  31.8 5.4 %collective-permute-start.3 = (f32[1,5,256]{2,1,0:T(8,128)S(1)}, f32[1,5,256]{2,1,0:T(8,128)S(1)}, u32[]{:S(2)}, u32[]{:S(2)}) collective-permute-start(f32[1,5,256]{2,1,0:T(8,128)S(1)} %fusion), channel_id=1, source_target_pairs={{0,4},{4,8},{8,12},{12,0},{1,5},{5,9},{9,13},{13,1},{2,6},{6,10},{... | collective-permute-start | bytes 15368 | tf_op jit(solution)/shard_map/ppermute | solution.py:28
  37.3 4.2 %copy-start.2 = (f32[4,5,256]{2,1,0:T(8,128)}, f32[4,5,256]{2,1,0:T(8,128)S(1)}, u32[]{:S(2)}) copy-start(f32[4,5,256]{2,1,0:T(8,128)S(1)} %pad_maximum_fusion.refs_7_) | copy-start | bytes 61444

commit v4 on v3

--- a/solution.py
+++ b/solution.py
@@ -17,6 +17,7 @@
 BF16 = jnp.bfloat16
 
 precise = lax.Precision.HIGHEST
+SMALL = pltpu.CompilerParams(vmem_limit_bytes=16 * 2**20)
 
 
 def history(own, axis):
@@ -36,6 +37,10 @@
     return held
 
 
+def on_chip(*arrays):
+    return [pltpu.with_memory_space_constraint(array, pltpu.VMEM) for array in arrays]
+
+
 def split(x):
     high = x.astype(BF16)
     return high, (x - high.astype(F32)).astype(BF16)
@@ -82,13 +87,14 @@
     return pl.pallas_call(
         prepare_kernel,
         out_shape=(
-            jax.ShapeDtypeStruct((2, size, size), BF16),
-            jax.ShapeDtypeStruct((2, size, size), BF16),
-            jax.ShapeDtypeStruct((2, size, size), F32),
-            jax.ShapeDtypeStruct((size, size), F32),
+            pltpu.VMEM((2, size, size), BF16),
+            pltpu.VMEM((2, size, size), BF16),
+            pltpu.VMEM((2, size, size), F32),
+            pltpu.VMEM((size, size), F32),
         ),
+        compiler_params=SMALL,
         name="prepare",
-    )(transition, update_map, quiet_root, observed_root, init_root)
+    )(*on_chip(transition, update_map, quiet_root, observed_root, init_root))
 
 
 def pairs_kernel(map_high, map_low, grams, pair_high, pair_low, pair_gram):
@@ -107,12 +113,13 @@
     return pl.pallas_call(
         pairs_kernel,
         out_shape=(
-            jax.ShapeDtypeStruct((4, size, size), BF16),
-            jax.ShapeDtypeStruct((4, size, size), BF16),
-            jax.ShapeDtypeStruct((4, size, size), F32),
+            pltpu.VMEM((4, size, size), BF16),
+            pltpu.VMEM((4, size, size), BF16),
+            pltpu.VMEM((4, size, size), F32),
         ),
+        compiler_params=SMALL,
         name="pair_maps",
-    )(map_high, map_low, grams)
+    )(*on_chip(map_high, map_low, grams))
 
 
 def upper_factor(gram, out, high, low, beside_work=()):
@@ -216,8 +223,17 @@
         for later in range(1, span):
             which = which + flags[at + later] * 2**later
         map_pair = (span_high[which], span_low[which])
-        carried = three_pass(map_pair, split(gram[...]), NN)
-        gram[...] = three_pass(split(carried), map_pair, NT) + span_gram[which]
+        old = split(gram[...])
+        half = gram.shape[0] // 2
+        new = []
+        for at in (0, half):
+            left = (map_pair[0][at : at + half], map_pair[1][at : at + half])
+            carried = three_pass(left, old, NN)
+            new.append(
+                three_pass(split(carried), map_pair, NT) + span_gram[which, at : at + half]
+            )
+        for n_half, at in enumerate((0, half)):
+            gram[at : at + half] = new[n_half]
         return carry
 
     lax.fori_loop(0, (index + 1) * pieces, step, 0)
@@ -232,11 +248,12 @@
 
     return pl.pallas_call(
         kernel,
-        out_shape=jax.ShapeDtypeStruct(first_gram.shape, F32),
+        out_shape=pltpu.VMEM(first_gram.shape, F32),
         in_specs=[smem, smem, vmem, vmem, vmem, vmem],
         out_specs=vmem,
+        compiler_params=SMALL,
         name="recursion",
-    )(place, flags, span_high, span_low, span_gram, first_gram)
+    )(place, flags, *on_chip(span_high, span_low, span_gram, first_gram))
 
 
 def factor_kernel(
@@ -310,8 +327,13 @@
             pltpu.VMEM((size, size), BF16),
             pltpu.VMEM((2, shifts.shape[0] * shifts.shape[1], size), F32),
         ],
+        compiler_params=SMALL,
         name="factor",
-    )(place, flags, gram, map_high, map_low, span_high, span_low, shifts, init_mean[None])
+    )(
+        place,
+        flags,
+        *on_chip(gram, map_high, map_low, span_high, span_low, shifts, init_mean[None]),
+    )
 
 
 LAGS = (0, DILATION_STEP, 2 * DILATION_STEP, -DILATION_STEP, -2 * DILATION_STEP)
@@ -345,17 +367,12 @@
     return total
 
 
-def frames_kernel(taps, flags, frames, pooling, part, stats, pooled):
-    steps, block, rows, columns = frames.shape
-    first = pl.program_id(0) * block
-
-    @pl.when(pl.program_id(0) == 0)
-    def _():
-        for k, (a, b) in enumerate(TAPS):
-            pooled[k] = moved(
-                moved(pooling[...], -DILATION_STEP * b, 1), -DILATION_STEP * a, 0
-            )
-
+def frames_kernel(unroll, taps, flags, frames, pooling, part, stats, pooled):
+    steps, channels, rows, columns = frames.shape
+    for k, (a, b) in enumerate(TAPS):
+        pooled[k] = moved(
+            moved(pooling[...], -DILATION_STEP * b, 1), -DILATION_STEP * a, 0
+        )
     lane = lax.broadcasted_iota(jnp.int32, (rows, LANES), 1)
     row = lax.broadcasted_iota(jnp.int32, (rows, LANES), 0)
     masks = [lax.rem(lane, rows) - row == lag for lag in LAGS]
@@ -364,14 +381,15 @@
     left_edge = (column < DILATION_STEP).astype(F32).astype(BF16)
     right_edge = (column >= columns - DILATION_STEP).astype(F32).astype(BF16)
     blank = jnp.zeros((rows, 2 * LANES - 5 * rows), F32)
-    for c in range(block):
-        weights = taps[0, first + c] * pooled[0]
+
+    def channel(c):
+        weights = taps[0, c] * pooled[0]
         for k in range(1, len(TAPS)):
-            weights = weights + taps[k, first + c] * pooled[k]
+            weights = weights + taps[k, c] * pooled[k]
         gram = jnp.zeros((rows, 5 * rows), F32)
         for t in range(steps):
             frame = frames[t, c]
-            part[t, c : c + 1, :] = jnp.sum(
+            part[t, pl.ds(c, 1), :] = jnp.sum(
                 folded(frame.astype(F32) * weights), axis=0, keepdims=True
             )
             partners = jnp.concatenate(
@@ -389,34 +407,36 @@
         far = jnp.concatenate([gram[:, LANES:], blank], axis=1)
         sums = [jnp.sum(jnp.where(m, near, 0.0), axis=0, keepdims=True) for m in masks]
         sums += [jnp.sum(jnp.where(m, far, 0.0), axis=0, keepdims=True) for m in right_masks]
-        stats[c : c + 1, :] = jnp.concatenate(sums, axis=1)
+        stats[pl.ds(c, 1), :] = jnp.concatenate(sums, axis=1)
+
+    def several(n, carry):
+        for u in range(unroll):
+            channel(n * unroll + u)
+        return carry
+
+    lax.fori_loop(0, channels // unroll, several, 0)
 
 
 def frame_sums(taps, flags, frames, pooling):
     steps, channels, rows, columns = frames.shape
-    block = math.gcd(channels, 16)
     vmem = pl.BlockSpec(memory_space=pltpu.VMEM)
     smem = pl.BlockSpec(memory_space=pltpu.SMEM)
+
+    def kernel(*refs):
+        frames_kernel(math.gcd(channels, 8), *refs)
+
     return pl.pallas_call(
-        frames_kernel,
-        grid=(channels // block,),
+        kernel,
         out_shape=(
-            jax.ShapeDtypeStruct((steps, channels, LANES), F32),
-            jax.ShapeDtypeStruct((channels, KINDS * LANES), F32),
+            pltpu.VMEM((steps, channels, LANES), F32),
+            pltpu.VMEM((channels, KINDS * LANES), F32),
         ),
-        in_specs=[
-            smem,
-            smem,
-            pl.BlockSpec((steps, block, rows, columns), lambda i: (0, i, 0, 0)),
-            vmem,
-        ],
-        out_specs=(
-            pl.BlockSpec((steps, block, LANES), lambda i: (0, i, 0)),
-            pl.BlockSpec((block, KINDS * LANES), lambda i: (i, 0)),
-        ),
+        in_specs=[smem, smem, vmem, vmem],
+        out_specs=(vmem, vmem),
         scratch_shapes=[pltpu.VMEM((len(TAPS), rows, columns), F32)],
+        compiler_params=SMALL,
         name="frame_sums",
-    )(taps, flags, frames, pooling)
+    )(taps, flags, *on_chip(frames, pooling))
 
 
 def selection(rows):
@@ -515,8 +535,9 @@
         out_shape=jax.ShapeDtypeStruct((above.shape[0], gain.shape[1]), F32),
         in_specs=[smem] + [vmem] * 6,
         out_specs=vmem,
+        compiler_params=SMALL,
         name="gain_sums",
-    )(flags, above, below, part, taps, pooling, gain)
+    )(flags, *on_chip(above, below, part, taps, pooling, gain))
 
 
 def gradient_kernel(
@@ -587,8 +608,9 @@
         in_specs=[smem] + [vmem] * 6,
         out_specs=vmem,
         scratch_shapes=[pltpu.VMEM((channels, table.shape[0]), F32)],
+        compiler_params=SMALL,
         name="tap_sums",
-    )(flags, edges, above, below, stats, taps, table)
+    )(flags, *on_chip(edges, above, below, stats, taps, table))
 
 
 def beside(edges, axis):

time: 52.5 us -> 47.8 us (0.910)
  Pallas kernels: 32.2 us -> 21.8 us
  local copies, waits for them, and re-layouts: 3.39 us -> 8.91 us
    pallas_call x4, Pallas kernels: 16.2 us -> 9.36 us  [the longest x1 5.04 us: frame_sums(): pl.pallas_call(kernel, out_shape=(pltpu.VMEM((steps, channels, LANES), F3...]
    unnamed x11 -> x35, local copies, waits for them, and re-layouts: 1.32 us -> 7.27 us
    pallas_call x1, Pallas kernels: 3.1 us -> 1.54 us  [tap_sums(): pl.pallas_call(kernel, out_shape=jax.ShapeDtypeStruct((len(TAPS), channel...]
    pallas_call x1, Pallas kernels: 2.28 us -> 1.22 us  [gain_sums(): pl.pallas_call(gain_kernel, out_shape=jax.ShapeDtypeStruct((above.shape[0...]
    transpose x1, other arithmetic: 0.05 us -> 1.04 us  [local(): edges = edges.transpose(0, 2, 1, 3)]
    pallas_call x1, Pallas kernels: 10.6 us -> 9.71 us  [factor(): pl.pallas_call(kernel, out_shape=(jax.ShapeDtypeStruct((size, size), F32)...]
    broadcast_in_dim x1, other arithmetic: 0.7 us -> 0.01 us  [local(): return (filtered_means, root[None], gradient.T[None])]
    ppermute x3, waiting for transfers between devices: 3.13 us -> 3.83 us  [history(): held.append(lax.ppermute(own, axis, ring))]
  transfers between devices with their start and end apart: 7 -> 7, of which waited for: 3 -> 3; matrix products, arithmetic and copies ran while one was open for 3% -> 1% of each run, Pallas kernels for 30% -> 19%
where the time goes in v4:
time: 47.8 us; the launch traced here: 47.5 us
  Pallas kernels  21.8 us (46%)
  starting transfers between devices  9.79 us (20%)
  local copies, waits for them, and re-layouts  8.91 us (19%)
  waiting for transfers between devices  5.02 us (11%)
  other arithmetic  1.11 us (2%)
  between operations  0.82 us (2%)
    pallas_call x1, Pallas kernels, factor(): pl.pallas_call(kernel, out_shape=(jax.ShapeDtypeStruct((size, size), F32)...  9.71 us
    unnamed x35, local copies, waits for them, and re-layouts  7.27 us
    pallas_call x1, Pallas kernels, frame_sums(): pl.pallas_call(kernel, out_shape=(pltpu.VMEM((steps, channels, LANES), F3...  5.04 us
    ppermute x3, starting transfers between devices, history(): held.append(lax.ppermute(own, axis, ring))  4.67 us
    ppermute x3, waiting for transfers between devices, history(): held.append(lax.ppermute(own, axis, ring))  3.83 us
    ppermute x1, starting transfers between devices, beside(): got = lax.ppermute(sent, axis, [(0, 1), (1, 0)])  3.03 us
    ppermute x3, starting transfers between devices, total(): return value + lax.ppermute(value, axis, [(0, 1), (1, 0)])  2.09 us
    pallas_call x1, Pallas kernels, pair_maps(): pl.pallas_call(pairs_kernel, out_shape=(pltpu.VMEM((4, size, size), BF16)...  2.04 us
  transfers between devices with their start and end apart: 7, of which 3 were waited for; matrix products, arithmetic and copies ran while one was open for 1% of the time, Pallas kernels for 19%

profile of v4, /device:TPU:0, one launch (start us, length us, event | category | flops | bytes accessed | tf_op | source)
XLA Modules:
  0.0 47.5 jit_solution(5683137256259865182)
XLA Ops:
  0.6 0.0 copy-start
  0.6 0.0 copy-start.14
  0.7 0.0 copy-start.9
  0.7 0.0 copy-start.12
  0.7 1.6 %fusion.2 = (bf16[4,32,4,256]{3,2,1,0:T(4,128)(2,1)S(1)}, bf16[4,32,4,256]{3,2,1,0:T(4,128)(2,1)S(1)}) fusion(bf16[4,32,32,256]{3,2,1,0:T(8,128)(2,1)} %refs_2_.1), kind=kLoop, calls=%fused_computation.10 | loop fusion | bytes 1048576 | tf_op jit(solution)/shard_map/slice | solution.py:650
  2.3 0.0 copy-start.13
  2.3 0.7 %copy.19 = bf16[4,32,4,256]{3,1,2,0:T(8,128)(2,1)} copy(bf16[4,32,4,256]{3,2,1,0:T(4,128)(2,1)S(1)} %get-tuple-element.29) | data formatting | bytes 524288
  3.0 1.0 %maximum_bitcast_fusion.refs_1_ = bf16[4,8,32,256]{3,2,1,0:T(8,128)(2,1)S(1)} fusion(bf16[4,32,4,256]{3,1,2,0:T(8,128)(2,1)} %copy.19, bf16[4,32,4,256]{3,1,2,0:T(8,128)(2,1)S(1)} %copy.18), kind=kLoop, calls=%fused_computation | loop fusion | flops 262144 | bytes 1048576 | tf_op jit(solution)/shard_map/transpose | solution.py:651
  4.1 3.0 %collective-permute-start = (bf16[4,2,32,256]{3,2,1,0:T(8,128)(2,1)S(1)}, bf16[4,2,32,256]{3,2,1,0:T(8,128)(2,1)S(1)}, u32[]{:S(2)}, u32[]{:S(2)}) collective-permute-start(bf16[4,2,32,256]{3,2,1,0:T(8,128)(2,1)S(1)} %slice_select_fusion), channel_id=1, source_target_pairs={{0,2},{2,0},{1,3},{3,1},{4,6},{6,4},{5,7},{7,5},{8,10},{10,8},{9,1... | collective-permute-start | bytes 393224 | tf_op jit(solution)/shard_map/ppermute | solution.py:622
  7.1 0.0 copy-done
  7.1 0.0 copy-done.14
  7.1 0.0 copy-done.9
  7.1 0.0 copy-done.12
  7.1 5.0 %frame_sums.1 = (f32[4,32,128]{2,1,0:T(8,128)S(1)}, f32[32,1024]{1,0:T(8,128)S(1)}) custom-call(f32[9,32]{1,0:T(8,128)S(1)} %bitcast.15, s32[4]{0:T(128)S(1)} %copy-done.14, bf16[4,32,32,256]{3,2,1,0:T(8,128)(2,1)S(1)} %copy-done, f32[32,256]{1,0:T(8,128)S(1)} %copy-done.9), custom_call_target="tpu_custom_call" | custom-call | tf_op jit(solution)/shard_map/frame_sums/pallas_call | solution.py:428
  12.2 0.0 copy-start.10
  12.2 0.0 collective-permute-done.above.below.refs_2_.refs_3_
  12.2 0.0 copy-done.13
  12.2 1.2 %gain_sums.1 = f32[4,256]{1,0:T(4,128)S(1)} custom-call(s32[4]{0:T(128)S(1)} %copy-done.14, bf16[4,2,32,256]{3,2,1,0:T(8,128)(2,1)S(1)} %collective-permute-done.above.below.refs_2_.refs_3_, bf16[4,2,32,256]{3,2,1,0:T(8,128)(2,1)S(1)} %collective-permute-done.above.below.refs_2_.refs_3_, f32[4,32,128]{2,1,0:T(8,128)S(1)} %get-tuple-element.14.part, ...), custom_call_target="tpu_custom_call" | custom-call | tf_op jit(solution)/shard_map/gain_sums/pallas_call | solution.py:533
  13.4 0.0 collective-permute-start.1
  13.4 1.2 %collective-permute-done.1 = f32[4,256]{1,0:T(4,128)S(1)} collective-permute-done((f32[4,256]{1,0:T(4,128)S(1)}, f32[4,256]{1,0:T(4,128)S(1)}, u32[]{:S(2)}, u32[]{:S(2)}) %collective-permute-start.1) | collective-permute-done | bytes 4128 | tf_op jit(solution)/shard_map/ppermute | solution.py:631
  14.6 0.1 collective-permute-start.2
  14.8 0.0 copy-done.10
  14.8 0.0 copy-done.2
  14.8 0.9 %copy-done.3 = f32[256,256]{1,0:T(8,128)S(1)} copy-done((f32[256,256]{1,0:T(8,128)S(1)}, f32[256,256]{1,0:T(8,128)}, u32[]{:S(2)}) %copy-start.3) | copy-done | bytes 262168
  15.7 0.9 %copy-done.4 = f32[256,256]{1,0:T(8,128)S(1)} copy-done((f32[256,256]{1,0:T(8,128)S(1)}, f32[256,256]{1,0:T(8,128)}, u32[]{:S(2)}) %copy-start.4) | copy-done | bytes 262168
  16.7 0.9 %copy-done.5 = f32[256,256]{1,0:T(8,128)S(1)} copy-done((f32[256,256]{1,0:T(8,128)S(1)}, f32[256,256]{1,0:T(8,128)}, u32[]{:S(2)}) %copy-start.5) | copy-done | bytes 262168
  17.6 0.9 %copy-done.6 = f32[256,256]{1,0:T(8,128)S(1)} copy-done((f32[256,256]{1,0:T(8,128)S(1)}, f32[256,256]{1,0:T(8,128)}, u32[]{:S(2)}) %copy-start.6) | copy-done | bytes 262168
  18.6 0.6 %prepare.1 = (bf16[2,256,256]{2,1,0:T(8,128)(2,1)S(1)}, bf16[2,256,256]{2,1,0:T(8,128)(2,1)S(1)}, f32[2,256,256]{2,1,0:T(8,128)S(1)}, f32[256,256]{1,0:T(8,128)S(1)}) custom-call(f32[256,256]{1,0:T(8,128)S(1)} %copy-done.2, f32[256,256]{1,0:T(8,128)S(1)} %copy-done.3, f32[256,256]{1,0:T(8,128)S(1)} %copy-done.4, f32[256,256]{1,0:T(8,128)S(1)} %copy-done.5, ...), custom_call_target="tpu_custom_call" | custom-call | tf_op jit(solution)/shard_map/prepare/pallas_call | solution.py:87
  19.2 0.0 copy-start.7
  19.2 2.0 %pair_maps.1 = (bf16[4,256,256]{2,1,0:T(8,128)(2,1)S(1)}, bf16[4,256,256]{2,1,0:T(8,128)(2,1)S(1)}, f32[4,256,256]{2,1,0:T(8,128)S(1)}) custom-call(bf16[2,256,256]{2,1,0:T(8,128)(2,1)S(1)} %get-tuple-element.15.map_high.refs_3_, bf16[2,256,256]{2,1,0:T(8,128)(2,1)S(1)} %get-tuple-element.16.map_low.refs_4_, f32[2,256,256]{2,1,0:T(8,128)S(1)} %get-tuple-element.17.grams), custom_call_target="tpu_custom_call" | custom-call | tf_op jit(solution)/shard_map/pair_maps/pallas_call | solution.py:113
  21.3 0.0 copy-done.11
  21.3 0.0 copy-start.1
  21.3 1.1 %copy-done.1 = bf16[2816,128]{1,0:T(8,128)(2,1)S(1)} copy-done((bf16[2816,128]{1,0:T(8,128)(2,1)S(1)}, bf16[2816,128]{1,0:T(8,128)(2,1)}, u32[]{:S(2)}) %copy-start.1) | copy-done | bytes 720920
  22.4 1.5 %tap_sums.1 = f32[9,32]{1,0:T(8,128)S(1)} custom-call(s32[4]{0:T(128)S(1)} %copy-done.14, bf16[4,8,32,256]{3,2,1,0:T(8,128)(2,1)S(1)} %maximum_bitcast_fusion.refs_1_, bf16[4,2,32,256]{3,2,1,0:T(8,128)(2,1)S(1)} %collective-permute-done.above.below.refs_2_.refs_3_, bf16[4,2,32,256]{3,2,1,0:T(8,128)(2,1)S(1)} %collective-permute-done.above.below.refs_2_.refs_3_, ...), custom_call_target="tpu_custom_call" | custom-call | tf_op jit(solution)/shard_map/tap_sums/pallas_call | solution.py:605
  23.9 1.9 %collective-permute-start.6 = (f32[9,32]{1,0:T(8,128)S(1)}, f32[9,32]{1,0:T(8,128)S(1)}, u32[]{:S(2)}, u32[]{:S(2)}) collective-permute-start(f32[9,32]{1,0:T(8,128)S(1)} %tap_sums.1), channel_id=1, source_target_pairs={{0,2},{2,0},{1,3},{3,1},{4,6},{6,4},{5,7},{7,5},{8,10},{10,8},{9,1... | collective-permute-start | bytes 3464 | tf_op jit(solution)/shard_map/ppermute | solution.py:631
  25.9 0.0 collective-permute-done.2
  25.9 3.7 %collective-permute-start.5 = (f32[1,5,256]{2,1,0:T(8,128)S(1)}, f32[1,5,256]{2,1,0:T(8,128)S(1)}, u32[]{:S(2)}, u32[]{:S(2)}) collective-permute-start(f32[1,5,256]{2,1,0:T(8,128)S(1)} %fusion), channel_id=1, source_target_pairs={{0,12},{4,0},{8,4},{12,8},{1,13},{5,1},{9,5},{13,9},{2,14},{6,2},{... | collective-permute-start | bytes 15368 | tf_op jit(solution)/shard_map/ppermute | solution.py:29
  29.5 0.0 collective-permute-start.4
  29.5 1.0 %collective-permute-start.3 = (f32[1,5,256]{2,1,0:T(8,128)S(1)}, f32[1,5,256]{2,1,0:T(8,128)S(1)}, u32[]{:S(2)}, u32[]{:S(2)}) collective-permute-start(f32[1,5,256]{2,1,0:T(8,128)S(1)} %fusion), channel_id=1, source_target_pairs={{0,4},{4,8},{8,12},{12,0},{1,5},{5,9},{9,13},{13,1},{2,6},{6,10},{... | collective-permute-start | bytes 15368 | tf_op jit(solution)/shard_map/ppermute | solution.py:29
  30.6 0.0 collective-permute-done.6
  30.6 0.6 %copy.17 = f32[1,32,9]{1,0,2:T(1,128)} copy(f32[1,32,9]{1,2,0:T(8,128)S(1)} %add_bitcast_fusion) | data formatting | bytes 2304
  31.2 0.0 collective-permute-done.5
  31.2 2.9 %collective-permute-done.4 = f32[1,5,256]{2,1,0:T(8,128)S(1)} collective-permute-done((f32[1,5,256]{2,1,0:T(8,128)S(1)}, f32[1,5,256]{2,1,0:T(8,128)S(1)}, u32[]{:S(2)}, u32[]{:S(2)}) %collective-permute-start.4) | collective-permute-done | bytes 5152 | tf_op jit(solution)/shard_map/ppermute | solution.py:29
  34.1 0.9 %collective-permute-done.3 = f32[1,5,256]{2,1,0:T(8,128)S(1)} collective-permute-done((f32[1,5,256]{2,1,0:T(8,128)S(1)}, f32[1,5,256]{2,1,0:T(8,128)S(1)}, u32[]{:S(2)}, u32[]{:S(2)}) %collective-permute-start.3) | collective-permute-done | bytes 5152 | tf_op jit(solution)/shard_map/ppermute | solution.py:29
  35.0 0.1 convert_element_type.14.refs_1_
  35.1 0.9 %copy-done.8 = f32[256,256]{1,0:T(8,128)S(1)} copy-done((f32[256,256]{1,0:T(8,128)S(1)}, f32[256,256]{1,0:T(8,128)}, u32[]{:S(2)}) %copy-start.8) | copy-done | bytes 262168
  36.1 1.7 %recursion.1.refs_2_ = f32[256,256]{1,0:T(8,128)S(1)} custom-call(s32[1]{0:T(128)} %bitcast.refs_0_, s32[16]{0:T(128)S(1)} %convert_element_type.14.refs_1_, bf16[4,256,256]{2,1,0:T(8,128)(2,1)S(1)} %get-tuple-element.18.refs_2_.refs_5_, bf16[4,256,256]{2,1,0:T(8,128)(2,1)S(1)} %get-tuple-element.19.refs_3_.refs_6_, ...), custom_call_target="tpu_custom_call" | custom-call | tf_op jit(solution)/shard_map/recursion/pallas_call | solution.py:249
  37.8 9.7 %factor.1 = (f32[256,256]{1,0:T(8,128)}, f32[4,256]{1,0:T(4,128)}) custom-call(s32[1]{0:T(128)} %bitcast.refs_0_, s32[16]{0:T(128)S(1)} %convert_element_type.14.refs_1_, f32[256,256]{1,0:T(8,128)S(1)} %recursion.1.refs_2_, bf16[2,256,256]{2,1,0:T(8,128)(2,1)S(1)} %get-tuple-element.15.map_high.refs_3_, ...), custom_call_target="tpu_custom_call" | custom-call | tf_op jit(solution)/shard_map/factor/pallas_call | solution.py:317
  (19 shorter events, 0.1 us)
Async XLA Ops:
  0.6 6.5 %copy-start = (bf16[4,32,32,256]{3,2,1,0:T(8,128)(2,1)S(1)}, bf16[4,32,32,256]{3,2,1,0:T(8,128)(2,1)}, u32[]{:S(2)}) copy-start(bf16[4,32,32,256]{3,2,1,0:T(8,128)(2,1)} %refs_2_.1) | copy-start | bytes 6291460
  0.6 6.5 %copy-start.14 = (s32[4]{0:T(128)S(1)}, s32[4]{0:T(128)}, u32[]{:S(2)}) copy-start(s32[4]{0:T(128)} %refs_0_.1) | copy-start | bytes 52
  0.7 6.5 %copy-start.9 = (f32[32,256]{1,0:T(8,128)S(1)}, f32[32,256]{1,0:T(8,128)}, u32[]{:S(2)}) copy-start(f32[32,256]{1,0:T(8,128)} %pooling.1) | copy-start | bytes 98308
  0.7 6.5 %copy-start.12 = (f32[32,9]{0,1:T(8,128)S(1)}, f32[32,9]{0,1:T(8,128)}, u32[]{:S(2)}) copy-start(f32[32,9]{0,1:T(8,128)} %param.13) | copy-start | bytes 3460
  2.3 9.9 %copy-start.13 = (f32[256,32]{0,1:T(8,128)S(1)}, f32[256,32]{0,1:T(8,128)}, u32[]{:S(2)}) copy-start(f32[256,32]{0,1:T(8,128)} %param.15) | copy-start | bytes 98308
  3.0 11.8 %copy-start.2 = (f32[256,256]{1,0:T(8,128)S(1)}, f32[256,256]{1,0:T(8,128)}, u32[]{:S(2)}) copy-start(f32[256,256]{1,0:T(8,128)} %transition.1) | copy-start | bytes 786436
  4.1 8.1 %collective-permute-start = (bf16[4,2,32,256]{3,2,1,0:T(8,128)(2,1)S(1)}, bf16[4,2,32,256]{3,2,1,0:T(8,128)(2,1)S(1)}, u32[]{:S(2)}, u32[]{:S(2)}) collective-permute-start(bf16[4,2,32,256]{3,2,1,0:T(8,128)(2,1)S(1)} %slice_select_fusion), channel_id=1, source_target_pairs={{0,2},{2,0},{1,3},{3,1},{4,6},{6,4},{5,7},{7,5},{8,10},{10,8},{9,1... | collective-permute-start | bytes 393224 | tf_op jit(solution)/shard_map/ppermute | solution.py:622
  12.2 2.6 %copy-start.10 = (f32[32,1024]{1,0:T(8,128)}, f32[32,1024]{1,0:T(8,128)S(1)}, u32[]{:S(2)}) copy-start(f32[32,1024]{1,0:T(8,128)S(1)} %get-tuple-element.24.refs_4_) | copy-start | bytes 393220
  13.4 1.2 %collective-permute-start.1 = (f32[4,256]{1,0:T(4,128)S(1)}, f32[4,256]{1,0:T(4,128)S(1)}, u32[]{:S(2)}, u32[]{:S(2)}) collective-permute-start(f32[4,256]{1,0:T(4,128)S(1)} %gain_sums.1), channel_id=1, source_target_pairs={{0,1},{1,0},{2,3},{3,2},{4,5},{5,4},{6,7},{7,6},{8,9},{9,8},{10,11... | collective-permute-start | bytes 12296 | tf_op jit(solution)/shard_map/ppermute | solution.py:631
  14.6 11.2 %collective-permute-start.2 = (f32[4,256]{1,0:T(4,128)S(1)}, f32[4,256]{1,0:T(4,128)S(1)}, u32[]{:S(2)}, u32[]{:S(2)}) collective-permute-start(f32[4,256]{1,0:T(4,128)S(1)} %add.11), channel_id=1, source_target_pairs={{0,2},{2,0},{1,3},{3,1},{4,6},{6,4},{5,7},{7,5},{8,10},{10,8},{9,1... | collective-permute-start | bytes 12296 | tf_op jit(solution)/shard_map/ppermute | solution.py:631
  14.8 1.0 %copy-start.3 = (f32[256,256]{1,0:T(8,128)S(1)}, f32[256,256]{1,0:T(8,128)}, u32[]{:S(2)}) copy-start(f32[256,256]{1,0:T(8,128)} %update_map.1) | copy-start | bytes 786436
  15.7 0.9 %copy-start.4 = (f32[256,256]{1,0:T(8,128)S(1)}, f32[256,256]{1,0:T(8,128)}, u32[]{:S(2)}) copy-start(f32[256,256]{1,0:T(8,128)} %quiet_root.1) | copy-start | bytes 786436
  16.7 0.9 %copy-start.5 = (f32[256,256]{1,0:T(8,128)S(1)}, f32[256,256]{1,0:T(8,128)}, u32[]{:S(2)}) copy-start(f32[256,256]{1,0:T(8,128)} %observed_root.1) | copy-start | bytes 786436
  17.6 0.9 %copy-start.6 = (f32[256,256]{1,0:T(8,128)S(1)}, f32[256,256]{1,0:T(8,128)}, u32[]{:S(2)}) copy-start(f32[256,256]{1,0:T(8,128)} %init_root.1) | copy-start | bytes 786436
  18.6 2.7 %copy-start.11 = (f32[32,1024]{1,0:T(8,128)S(1)}, f32[32,1024]{1,0:T(8,128)}, u32[]{:S(2)}) copy-start(f32[32,1024]{1,0:T(8,128)} %copy-done.10) | copy-start | bytes 393220
  19.2 4.7 %copy-start.7 = (f32[256,256]{1,0:T(8,128)}, f32[256,256]{1,0:T(8,128)S(1)}, u32[]{:S(2)}) copy-start(f32[256,256]{1,0:T(8,128)S(1)} %get-tuple-element.21.refs_5_) | copy-start | bytes 786436
  21.3 1.1 %copy-start.1 = (bf16[2816,128]{1,0:T(8,128)(2,1)S(1)}, bf16[2816,128]{1,0:T(8,128)(2,1)}, u32[]{:S(2)}) copy-start(bf16[2816,128]{1,0:T(8,128)(2,1)} %constant.15.clone.refs_6_) | copy-start | bytes 2162692
  22.4 15.4 %copy-start.15 = (f32[256]{0:T(256)S(1)}, f32[256]{0:T(256)}, u32[]{:S(2)}) copy-start(f32[256]{0:T(256)} %param.20) | copy-start | bytes 3076
  23.9 6.6 %collective-permute-start.6 = (f32[9,32]{1,0:T(8,128)S(1)}, f32[9,32]{1,0:T(8,128)S(1)}, u32[]{:S(2)}, u32[]{:S(2)}) collective-permute-start(f32[9,32]{1,0:T(8,128)S(1)} %tap_sums.1), channel_id=1, source_target_pairs={{0,2},{2,0},{1,3},{3,1},{4,6},{6,4},{5,7},{7,5},{8,10},{10,8},{9,1... | collective-permute-start | bytes 3464 | tf_op jit(solution)/shard_map/ppermute | solution.py:631
  25.9 5.3 %collective-permute-start.5 = (f32[1,5,256]{2,1,0:T(8,128)S(1)}, f32[1,5,256]{2,1,0:T(8,128)S(1)}, u32[]{:S(2)}, u32[]{:S(2)}) collective-permute-start(f32[1,5,256]{2,1,0:T(8,128)S(1)} %fusion), channel_id=1, source_target_pairs={{0,12},{4,0},{8,4},{12,8},{1,13},{5,1},{9,5},{13,9},{2,14},{6,2},{... | collective-permute-start | bytes 15368 | tf_op jit(solution)/shard_map/ppermute | solution.py:29
  29.5 4.5 %collective-permute-start.4 = (f32[1,5,256]{2,1,0:T(8,128)S(1)}, f32[1,5,256]{2,1,0:T(8,128)S(1)}, u32[]{:S(2)}, u32[]{:S(2)}) collective-permute-start(f32[1,5,256]{2,1,0:T(8,128)S(1)} %fusion), channel_id=1, source_target_pairs={{0,8},{4,12},{8,0},{12,4},{1,9},{5,13},{9,1},{13,5},{2,10},{6,14},... | collective-permute-start | bytes 15368 | tf_op jit(solution)/shard_map/ppermute | solution.py:29
  29.5 5.4 %collective-permute-start.3 = (f32[1,5,256]{2,1,0:T(8,128)S(1)}, f32[1,5,256]{2,1,0:T(8,128)S(1)}, u32[]{:S(2)}, u32[]{:S(2)}) collective-permute-start(f32[1,5,256]{2,1,0:T(8,128)S(1)} %fusion), channel_id=1, source_target_pairs={{0,4},{4,8},{8,12},{12,0},{1,5},{5,9},{9,13},{13,1},{2,6},{6,10},{... | collective-permute-start | bytes 15368 | tf_op jit(solution)/shard_map/ppermute | solution.py:29
  35.1 1.0 %copy-start.8 = (f32[256,256]{1,0:T(8,128)S(1)}, f32[256,256]{1,0:T(8,128)}, u32[]{:S(2)}) copy-start(f32[256,256]{1,0:T(8,128)} %copy-done.7) | copy-start | bytes 786436

commit v5 on v4

--- a/solution.py
+++ b/solution.py
@@ -20,21 +20,55 @@
 SMALL = pltpu.CompilerParams(vmem_limit_bytes=16 * 2**20)
 
 
+def paired(count):
+    return count & (count - 1) == 0
+
+
+def slot_of(block, place, count):
+    return block ^ place if paired(count) else block
+
+
+def join_kernel(a, b, out):
+    length = a.shape[0]
+    out[:length] = a[...]
+    out[length:] = b[...]
+
+
+def joined(a, b):
+    return pl.pallas_call(
+        join_kernel,
+        out_shape=jax.ShapeDtypeStruct((2 * a.shape[0],) + a.shape[1:], a.dtype),
+        compiler_params=SMALL,
+        name="joined",
+    )(*on_chip(a, b))
+
+
+def add_kernel(a, b, out):
+    out[...] = a[...] + b[...]
+
+
+def added(a, b):
+    return pl.pallas_call(
+        add_kernel,
+        out_shape=jax.ShapeDtypeStruct(a.shape, a.dtype),
+        compiler_params=SMALL,
+        name="added",
+    )(*on_chip(a, b))
+
+
 def history(own, axis):
     count = lax.axis_size(axis)
-    if count <= 4:
-        held = [own]
-        for lag in range(1, count):
-            ring = [(i, (i + lag) % count) for i in range(count)]
-            held.append(lax.ppermute(own, axis, ring))
-        return jnp.concatenate(held, axis=0)
-    held = own
+    if not paired(count):
+        return [lax.all_gather(own[0], axis)]
+    pieces = [own]
     reach = 1
     while reach < count:
-        pairs = [(i, i + reach) for i in range(count - reach)]
-        held = jnp.concatenate([held, lax.ppermute(held, axis, pairs)], axis=0)
+        sent = pieces[0]
+        for piece in pieces[1:]:
+            sent = joined(sent, piece)
+        pieces.append(lax.ppermute(sent, axis, [(i, i ^ reach) for i in range(count)]))
         reach *= 2
-    return held
+    return pieces
 
 
 def on_chip(*arrays):
@@ -70,26 +104,50 @@
 
 
 def prepare_kernel(
-    transition, update_map, quiet_root, observed_root, init_root,
-    map_high, map_low, grams, first_gram,
+    span, transition, update_map, quiet_root, observed_root, init_root,
+    map_high, map_low, span_high, span_low, span_gram, first_gram,
 ):
-    for which, ref in enumerate((transition, update_map)):
-        map_high[which], map_low[which] = split(ref[...])
-    for which, ref in enumerate((quiet_root, observed_root)):
+    maps = [split(transition[...]), split(update_map[...])]
+    for which, (high, low) in enumerate(maps):
+        map_high[which] = high
+        map_low[which] = low
+    grams = []
+    for ref in (quiet_root, observed_root):
         pair = split(ref[...])
-        grams[which] = three_pass(pair, pair, TN)
+        grams.append(three_pass(pair, pair, TN))
     pair = split(init_root[...])
     first_gram[...] = three_pass(pair, pair, TN)
-
-
-def prepare(transition, update_map, quiet_root, observed_root, init_root):
+    if span == 1:
+        for which, (high, low) in enumerate(maps):
+            span_high[which] = high
+            span_low[which] = low
+            span_gram[which] = grams[which]
+        return
+    for later in range(2):
+        for earlier in range(2):
+            which = 2 * later + earlier
+            span_high[which], span_low[which] = split(
+                three_pass(maps[later], maps[earlier], NN)
+            )
+            carried = three_pass(maps[later], split(grams[earlier]), NN)
+            span_gram[which] = three_pass(split(carried), maps[later], NT) + grams[later]
+
+
+def prepare(span, transition, update_map, quiet_root, observed_root, init_root):
     size = transition.shape[0]
+    many = 2**span
+
+    def kernel(*refs):
+        prepare_kernel(span, *refs)
+
     return pl.pallas_call(
-        prepare_kernel,
+        kernel,
         out_shape=(
             pltpu.VMEM((2, size, size), BF16),
             pltpu.VMEM((2, size, size), BF16),
-            pltpu.VMEM((2, size, size), F32),
+            pltpu.VMEM((many, size, size), BF16),
+            pltpu.VMEM((many, size, size), BF16),
+            pltpu.VMEM((many, size, size), F32),
             pltpu.VMEM((size, size), F32),
         ),
         compiler_params=SMALL,
@@ -97,32 +155,7 @@
     )(*on_chip(transition, update_map, quiet_root, observed_root, init_root))
 
 
-def pairs_kernel(map_high, map_low, grams, pair_high, pair_low, pair_gram):
-    maps = [(map_high[which], map_low[which]) for which in range(2)]
-    for later in range(2):
-        for earlier in range(2):
-            which = 2 * later + earlier
-            joined = three_pass(maps[later], maps[earlier], NN)
-            pair_high[which], pair_low[which] = split(joined)
-            carried = three_pass(maps[later], split(grams[earlier]), NN)
-            pair_gram[which] = three_pass(split(carried), maps[later], NT) + grams[later]
-
-
-def pair_maps(map_high, map_low, grams):
-    size = grams.shape[1]
-    return pl.pallas_call(
-        pairs_kernel,
-        out_shape=(
-            pltpu.VMEM((4, size, size), BF16),
-            pltpu.VMEM((4, size, size), BF16),
-            pltpu.VMEM((4, size, size), F32),
-        ),
-        compiler_params=SMALL,
-        name="pair_maps",
-    )(*on_chip(map_high, map_low, grams))
-
-
-def upper_factor(gram, out, high, low, beside_work=()):
+def upper_factor(gram, out, high, low, begin, end, beside_work=()):
     size = gram.shape[0]
     halves = size // LANES
     tile = (GROUP, LANES)
@@ -131,7 +164,7 @@
     lane = lax.broadcasted_iota(jnp.int32, tile, 1)
     count = PANEL // GROUP
     pending = list(beside_work)
-    for top in range(0, size, PANEL):
+    for top in range(begin, end, PANEL):
         first = top // LANES
         start = first * LANES
         panel = gram[top : top + PANEL, start:]
@@ -212,16 +245,32 @@
         work()
 
 
-def recursion_kernel(steps, span, place, flags, span_high, span_low, span_gram, first_gram, gram):
+def flag_reader(pieces, table):
+    slot = 0
+    for piece in pieces:
+        for row in range(piece.shape[0]):
+            for t in range(piece.shape[1]):
+                table[slot + row, t] = piece[row, t]
+        slot += piece.shape[0]
+    return lambda slot, t: table[slot, t]
+
+
+def recursion_kernel(
+    steps, span, pieces, place, *refs
+):
+    flag_at = flag_reader(refs[:pieces], refs[-1])
+    span_high, span_low, span_gram, first_gram, gram, _ = refs[pieces:]
+    count = refs[-1].shape[0]
     index = place[0]
-    pieces = steps // span
+    parts = steps // span
     gram[...] = first_gram[...]
 
     def step(n, carry):
-        at = (index - n // pieces) * steps + (n % pieces) * span
-        which = flags[at]
+        slot = slot_of(n // parts, index, count)
+        t = (n % parts) * span
+        which = flag_at(slot, t)
         for later in range(1, span):
-            which = which + flags[at + later] * 2**later
+            which = which + flag_at(slot, t + later) * 2**later
         map_pair = (span_high[which], span_low[which])
         old = split(gram[...])
         half = gram.shape[0] // 2
@@ -236,7 +285,7 @@
             gram[at : at + half] = new[n_half]
         return carry
 
-    lax.fori_loop(0, (index + 1) * pieces, step, 0)
+    lax.fori_loop(0, (index + 1) * parts, step, 0)
 
 
 def recursion(place, flags, steps, span, span_high, span_low, span_gram, first_gram):
@@ -244,95 +293,144 @@
     smem = pl.BlockSpec(memory_space=pltpu.SMEM)
 
     def kernel(*refs):
-        recursion_kernel(steps, span, *refs)
-
+        recursion_kernel(steps, span, len(flags), *refs)
+
+    count = sum(piece.shape[0] for piece in flags)
     return pl.pallas_call(
         kernel,
         out_shape=pltpu.VMEM(first_gram.shape, F32),
-        in_specs=[smem, smem, vmem, vmem, vmem, vmem],
+        in_specs=[smem] * (1 + len(flags)) + [vmem] * 4,
         out_specs=vmem,
+        scratch_shapes=[pltpu.SMEM((count, steps), jnp.int32)],
         compiler_params=SMALL,
         name="recursion",
-    )(place, flags, *on_chip(span_high, span_low, span_gram, first_gram))
+    )(place, *flags, *on_chip(span_high, span_low, span_gram, first_gram))
+
+
+def factor_top_kernel(gram, out, high, low):
+    upper_factor(gram, out, high, low, 0, out.shape[0])
+
+
+def factor_top(gram):
+    size = gram.shape[0]
+    rows = size // (2 * PANEL) * PANEL
+    return pl.pallas_call(
+        factor_top_kernel,
+        out_shape=(
+            pltpu.VMEM((rows, size), F32),
+            pltpu.VMEM((rows, size), BF16),
+            pltpu.VMEM((rows, size), BF16),
+        ),
+        compiler_params=SMALL,
+        name="factor_top",
+    )(*on_chip(gram))
 
 
 def factor_kernel(
-    steps, span, place, flags, gram, map_high, map_low, span_high, span_low, shifts, init_mean,
-    out, mean_out, high, low, carried,
+    steps, span, flag_pieces, shift_pieces, place, *refs
 ):
+    flag_at = flag_reader(refs[:flag_pieces], refs[-1])
+    gram, top, top_high, top_low, map_high, map_low = refs[flag_pieces : flag_pieces + 6]
+    span_high, span_low, init_mean, gradient, gradient_beside = refs[
+        flag_pieces + 6 : flag_pieces + 11
+    ]
+    received = refs[flag_pieces + 11 : flag_pieces + 11 + shift_pieces]
+    out, mean_out, gradient_out, high, low, carried, shifts, _ = refs[
+        flag_pieces + 11 + shift_pieces :
+    ]
     index = place[0]
     size = gram.shape[0]
-    blocks = shifts.shape[0]
+    count = shifts.shape[0]
+    slot = 0
+    for piece in received:
+        shifts[slot : slot + piece.shape[0]] = piece[...]
+        slot += piece.shape[0]
+    begin = top.shape[0]
+    gradient_out[:, 0, :] = gradient[...] + gradient_beside[...]
+    out[:begin] = top[...]
+    high[:begin] = top_high[...]
+    low[:begin] = top_low[...]
     state = {"mean": jnp.broadcast_to(init_mean[...], (GROUP, size))}
 
     def first():
-        rows = split(jnp.concatenate([shifts[block] for block in range(blocks)], axis=0))
+        rows = split(jnp.concatenate([shifts[slot] for slot in range(count)], axis=0))
         for which in range(2):
-            carried[which] = three_pass(rows, (map_high[which], map_low[which]), NT)
-
-    def one_step(block, t):
-        at = block * steps + t
-        flag = flags[at]
-        mean = three_pass(split(state["mean"]), (map_high[flag], map_low[flag]), NT)
-        return mean + shifts[block, t : t + 1, :]
+            values = three_pass(rows, (map_high[which], map_low[which]), NT)
+            for slot in range(count):
+                carried[which, slot] = values[slot * steps : (slot + 1) * steps]
 
     def work(block, t):
+        own = block == count
+        slot = slot_of(index, index, count) if own else slot_of(block, index, count)
+
+        def one_step():
+            flag = flag_at(slot, t)
+            mean = three_pass(split(state["mean"]), (map_high[flag], map_low[flag]), NT)
+            return mean + shifts[slot, t : t + 1, :]
+
         def run():
-            if block == 0:
-                mean = one_step(block, t)
-                mean_out[t : t + 1, :] = mean[0:1]
-                if span == 1:
-                    state["mean"] = mean
-                    return
             if span == 1:
-                mean = one_step(block, t)
+                mean = one_step()
             else:
-                at = block * steps + t
-                which = flags[at] + 2 * flags[at + 1]
+                if own:
+                    mean_out[t : t + 1, :] = one_step()[0:1]
+                first_flag, last_flag = flag_at(slot, t), flag_at(slot, t + 1)
+                which = first_flag + 2 * last_flag
                 mean = three_pass(split(state["mean"]), (span_high[which], span_low[which]), NT)
-                row = block * shifts.shape[1] + t
-                mean = mean + carried[flags[at + 1], row : row + 1, :]
-                mean = mean + shifts[block, t + 1 : t + 2, :]
-                if block == 0:
-                    mean_out[t + 1 : t + 2, :] = mean[0:1]
-            state["mean"] = mean if block == 0 else jnp.where(block <= index, mean, state["mean"])
+                mean = mean + carried[last_flag, slot, t : t + 1, :]
+                mean = mean + shifts[slot, t + 1 : t + 2, :]
+            if own:
+                mean_out[t + span - 1 : t + span, :] = mean[0:1]
+            else:
+                mean = jnp.where(block < index, mean, state["mean"])
+            state["mean"] = mean
 
         return run
 
     jobs = [first] if span == 2 else []
-    jobs += [work(block, t) for block in reversed(range(blocks)) for t in range(0, steps, span)]
-    upper_factor(gram, out, high, low, jobs)
+    blocks = list(range(count - 1)) + [count]
+    jobs += [work(block, t) for block in blocks for t in range(0, steps, span)]
+    upper_factor(gram, out, high, low, begin, size, jobs)
 
 
 def factor(
-    place, flags, steps, span, gram, map_high, map_low, span_high, span_low, shifts, init_mean
+    place, flags, steps, span, gram, tops, map_high, map_low, span_high, span_low, shifts,
+    init_mean, gradient, gradient_beside,
 ):
     size = gram.shape[0]
+    taps, channels = gradient.shape
+    count = sum(piece.shape[0] for piece in flags)
     vmem = pl.BlockSpec(memory_space=pltpu.VMEM)
     smem = pl.BlockSpec(memory_space=pltpu.SMEM)
 
     def kernel(*refs):
-        factor_kernel(steps, span, *refs)
+        factor_kernel(steps, span, len(flags), len(shifts), *refs)
 
     return pl.pallas_call(
         kernel,
         out_shape=(
             jax.ShapeDtypeStruct((size, size), F32),
             jax.ShapeDtypeStruct((steps, size), F32),
+            jax.ShapeDtypeStruct((taps, 1, channels), F32),
         ),
-        in_specs=[smem, smem] + [vmem] * 7,
-        out_specs=(vmem, vmem),
+        in_specs=[smem] * (1 + len(flags)) + [vmem] * (11 + len(shifts)),
+        out_specs=(vmem, vmem, vmem),
         scratch_shapes=[
             pltpu.VMEM((size, size), BF16),
             pltpu.VMEM((size, size), BF16),
-            pltpu.VMEM((2, shifts.shape[0] * shifts.shape[1], size), F32),
+            pltpu.VMEM((2, count, steps, size), F32),
+            pltpu.VMEM((count, steps, size), F32),
+            pltpu.SMEM((count, steps), jnp.int32),
         ],
         compiler_params=SMALL,
         name="factor",
     )(
         place,
-        flags,
-        *on_chip(gram, map_high, map_low, span_high, span_low, shifts, init_mean[None]),
+        *flags,
+        *on_chip(
+            gram, *tops, map_high, map_low, span_high, span_low, init_mean[None],
+            gradient, gradient_beside, *shifts,
+        ),
     )
 
 
@@ -341,7 +439,7 @@
 EDGE = 2 * DILATION_STEP
 KINDS = 8
 EDGE_KINDS = 2
-HALO_KINDS = 6
+HALO_KINDS = 7
 
 
 def moved(x, by, axis):
@@ -367,8 +465,17 @@
     return total
 
 
-def frames_kernel(unroll, taps, flags, frames, pooling, part, stats, pooled):
+def frames_kernel(
+    unroll, taps, flags, source, pooling, part, stats, pooled, frames, arrived
+):
     steps, channels, rows, columns = frames.shape
+    copies = []
+    for n in range(channels // unroll):
+        piece = (slice(None), pl.ds(n * unroll, unroll))
+        copies.append(
+            pltpu.make_async_copy(source.at[piece], frames.at[piece], arrived.at[n])
+        )
+        copies[-1].start()
     for k, (a, b) in enumerate(TAPS):
         pooled[k] = moved(
             moved(pooling[...], -DILATION_STEP * b, 1), -DILATION_STEP * a, 0
@@ -376,17 +483,20 @@
     lane = lax.broadcasted_iota(jnp.int32, (rows, LANES), 1)
     row = lax.broadcasted_iota(jnp.int32, (rows, LANES), 0)
     masks = [lax.rem(lane, rows) - row == lag for lag in LAGS]
-    right_masks = [(lane - row == lag) & (lane < rows) for lag in LAGS[:3]]
-    column = lax.broadcasted_iota(jnp.int32, (rows, columns), 1)
-    left_edge = (column < DILATION_STEP).astype(F32).astype(BF16)
-    right_edge = (column >= columns - DILATION_STEP).astype(F32).astype(BF16)
-    blank = jnp.zeros((rows, 2 * LANES - 5 * rows), F32)
+    left_edge = (lane < DILATION_STEP).astype(F32).astype(BF16)
+    right_edge = (lane >= LANES - DILATION_STEP).astype(F32).astype(BF16)
+    left_half = (lane < LANES // 2).astype(F32).astype(BF16)
+    right_half = (lane >= LANES // 2).astype(F32).astype(BF16)
+    middle = LANES // 2 - DILATION_STEP
+    blank = jnp.zeros((LANES - 3 * rows, columns), BF16)
+    edge_blank = jnp.zeros((LANES - 2 * rows, LANES), BF16)
 
     def channel(c):
         weights = taps[0, c] * pooled[0]
         for k in range(1, len(TAPS)):
             weights = weights + taps[k, c] * pooled[k]
-        gram = jnp.zeros((rows, 5 * rows), F32)
+        gram = jnp.zeros((rows, LANES), F32)
+        borders = jnp.zeros((rows, LANES), BF16)
         for t in range(steps):
             frame = frames[t, c]
             part[t, pl.ds(c, 1), :] = jnp.sum(
@@ -397,19 +507,27 @@
                     frame,
                     moved(frame, DILATION_STEP, 1),
                     moved(frame, 2 * DILATION_STEP, 1),
-                    frame * left_edge,
-                    frame * right_edge,
+                    blank,
                 ],
                 axis=0,
             )
-            gram = gram + contract(frame * flags[t].astype(F32).astype(BF16), partners, NT)
-        near = gram[:, :LANES]
-        far = jnp.concatenate([gram[:, LANES:], blank], axis=1)
-        sums = [jnp.sum(jnp.where(m, near, 0.0), axis=0, keepdims=True) for m in masks]
-        sums += [jnp.sum(jnp.where(m, far, 0.0), axis=0, keepdims=True) for m in right_masks]
+            seen = frame * flags[t].astype(F32).astype(BF16)
+            gram = gram + contract(seen, partners, NT)
+            at = DILATION_STEP * t
+            borders = borders + moved(seen[:, :LANES] * left_edge, -at, 1)
+            borders = borders + moved(seen[:, columns - LANES :] * right_edge, middle - at, 1)
+        edge = contract(
+            borders,
+            jnp.concatenate([borders * left_half, borders * right_half, edge_blank], axis=0),
+            NT,
+        )
+        sums = [jnp.sum(jnp.where(m, gram, 0.0), axis=0, keepdims=True) for m in masks]
+        sums += [jnp.sum(jnp.where(m, edge, 0.0), axis=0, keepdims=True) for m in masks[:3]]
         stats[pl.ds(c, 1), :] = jnp.concatenate(sums, axis=1)
 
     def several(n, carry):
+        piece = (slice(None), pl.ds(n * unroll, unroll))
+        pltpu.make_async_copy(source.at[piece], frames.at[piece], arrived.at[n]).wait()
         for u in range(unroll):
             channel(n * unroll + u)
         return carry
@@ -422,8 +540,10 @@
     vmem = pl.BlockSpec(memory_space=pltpu.VMEM)
     smem = pl.BlockSpec(memory_space=pltpu.SMEM)
 
+    unroll = math.gcd(channels, 8)
+
     def kernel(*refs):
-        frames_kernel(math.gcd(channels, 8), *refs)
+        frames_kernel(unroll, *refs)
 
     return pl.pallas_call(
         kernel,
@@ -431,18 +551,24 @@
             pltpu.VMEM((steps, channels, LANES), F32),
             pltpu.VMEM((channels, KINDS * LANES), F32),
         ),
-        in_specs=[smem, smem, vmem, vmem],
+        in_specs=[smem, smem, pl.BlockSpec(memory_space=pltpu.HBM), vmem],
         out_specs=(vmem, vmem),
-        scratch_shapes=[pltpu.VMEM((len(TAPS), rows, columns), F32)],
+        scratch_shapes=[
+            pltpu.VMEM((len(TAPS), rows, columns), F32),
+            pltpu.VMEM(frames.shape, frames.dtype),
+            pltpu.SemaphoreType.DMA((channels // unroll,)),
+        ],
         compiler_params=SMALL,
         name="frame_sums",
-    )(taps, flags, *on_chip(frames, pooling))
+    )(
+        taps, flags, pltpu.with_memory_space_constraint(frames, pltpu.HBM), *on_chip(pooling)
+    )
 
 
 def selection(rows):
     near = np.zeros((KINDS, LANES, len(TAPS), len(TAPS)), np.float32)
     edge = np.zeros((EDGE_KINDS, LANES, len(TAPS), len(TAPS)), np.float32)
-    halo = np.zeros((2, HALO_KINDS, LANES, len(TAPS), len(TAPS)), np.float32)
+    halo = np.zeros((2, HALO_KINDS, len(TAPS), len(TAPS)), np.float32)
     own = np.arange(rows)
     top, bottom = own[:DILATION_STEP], own[rows - DILATION_STEP :]
     for i, (a, b) in enumerate(TAPS):
@@ -454,28 +580,22 @@
             kind = down if across >= 0 else down + 2
             near[kind, lag * rows + own, i, j] += 1
             if down:
-                if across == 0:
-                    halo[down - 1, :2, :, i, j] += 1
-                else:
-                    halo[down - 1, 1 + lag + (2 if across < 0 else 0), :, i, j] += 1
-            if b == d == 1:
-                near[down, 3 * rows + own, i, j] -= 1
-                if down:
-                    halo[down - 1, 0, :DILATION_STEP, i, j] -= 1
-            if b == d == -1:
-                near[5 + down, own, i, j] -= 1
-                if down:
-                    halo[down - 1, 1, LANES - DILATION_STEP :, i, j] -= 1
+                halo[down - 1, across + 2, i, j] += 1
+            for side, group in ((1, 0), (-1, 1)):
+                if b == d == side:
+                    near[5 + down, group * rows + own, i, j] -= 1
+                    if down:
+                        halo[down - 1, 5 + group, i, j] -= 1
             if a == c != 0:
                 lost = top if a == 1 else bottom
                 edge[0, lag * rows + lost, i, j] -= 1
-                if b == d == 1:
-                    edge[0, 3 * rows + lost, i, j] += 1
-                if b == d == -1:
-                    edge[1, lost, i, j] += 1
+                for side, group in ((1, 0), (-1, 1)):
+                    if b == d == side:
+                        edge[1, group * rows + lost, i, j] += 1
     pairs = len(TAPS) ** 2
-    table = np.concatenate([m.reshape(-1, pairs) for m in (near, edge, halo)], axis=0)
-    return np.pad(table, ((0, 0), (0, LANES - pairs)))
+    table = np.concatenate([m.reshape(-1, pairs) for m in (near, edge)], axis=0)
+    halo = np.pad(halo.reshape(-1, pairs), ((0, -2 * HALO_KINDS % GROUP), (0, 0)))
+    return [np.pad(m, ((0, 0), (0, LANES - pairs))) for m in (table, halo)]
 
 
 def beside_tile():
@@ -541,17 +661,18 @@
 
 
 def gradient_kernel(
-    scale, rows, flags, edges, above, below, stats, taps, table, gradient, values
+    scale, rows, flags, tops, bottoms, above, below, stats, taps, table, halo_table,
+    gradient, values,
 ):
-    steps, _, channels, columns = edges.shape
+    steps, _, channels, columns = tops.shape
     has_above, has_below = beside_tile()
     sums = [[None] * 5 for _ in range(2)]
     for t in range(steps):
         flag = flags[t].astype(F32)
         for r in range(DILATION_STEP):
-            near_top = edges[t, DILATION_STEP + r].astype(F32)
-            far_bottom = edges[t, 2 * DILATION_STEP + r].astype(F32)
-            near_bottom = edges[t, 3 * DILATION_STEP + r].astype(F32)
+            near_top = tops[t, DILATION_STEP + r].astype(F32)
+            far_bottom = bottoms[t, r].astype(F32)
+            near_bottom = bottoms[t, DILATION_STEP + r].astype(F32)
             high = above[t, r].astype(F32) * (flag * has_above)
             low = below[t, r].astype(F32) * (flag * has_below)
             for n in range(-2, 3):
@@ -570,32 +691,30 @@
     for kind in (0, 5):
         values[:, at : at + LANES] = stats[:, kind * LANES : (kind + 1) * LANES] * outside
         at += LANES
-    for which in range(2):
-        centre = sums[which][0]
-        pieces = [centre[:, :LANES], centre[:, columns - LANES :]]
-        pieces += [folded(sums[which][n]) for n in (1, 2, -1, -2)]
-        for inner in range(LANES, columns - LANES, LANES):
-            middle = jnp.sum(centre[:, inner : inner + LANES], axis=1, keepdims=True)
-            pieces[0] = pieces[0] + jnp.where(lane_of(channels) == LANES // 2, middle, 0.0)
-        for piece in pieces:
-            values[:, at : at + LANES] = piece
-            at += LANES
     high, low = split(values[...])
     pairs = contract(high, table[...], NN) + contract(low, table[...], NN)
+    lane = lax.broadcasted_iota(jnp.int32, (channels, LANES), 1)
+    for which in range(2):
+        pieces = [folded(sums[which][n]) for n in range(-2, 3)]
+        centre = sums[which][0]
+        pieces.append(jnp.where(lane < DILATION_STEP, centre[:, :LANES], 0.0))
+        pieces.append(
+            jnp.where(lane >= LANES - DILATION_STEP, centre[:, columns - LANES :], 0.0)
+        )
+        for n, piece in enumerate(pieces):
+            at = which * HALO_KINDS + n
+            pairs = pairs + jnp.sum(piece, axis=1, keepdims=True) * halo_table[at : at + 1, :]
     source, tap = spread()
     weights = exact(taps[...], (source // len(TAPS) == tap).astype(F32), TN)
     gathered = (source % len(TAPS) == tap).astype(F32)
     gradient[...] = exact(gathered, pairs * weights, NT) * scale
 
 
-def lane_of(channels):
-    return lax.broadcasted_iota(jnp.int32, (channels, LANES), 1)
-
-
-def tap_sums(flags, edges, above, below, stats, taps, rows):
-    _, _, channels, columns = edges.shape
+def tap_sums(flags, tops, bottoms, above, below, stats, taps, rows):
+    _, _, channels, columns = tops.shape
     scale = 1.0 / (rows * lax.axis_size("space") * columns)
-    table = jnp.asarray(selection(rows), BF16)
+    table, halo_table = selection(rows)
+    table = jnp.asarray(table, BF16)
     vmem = pl.BlockSpec(memory_space=pltpu.VMEM)
     smem = pl.BlockSpec(memory_space=pltpu.SMEM)
 
@@ -605,18 +724,16 @@
     return pl.pallas_call(
         kernel,
         out_shape=jax.ShapeDtypeStruct((len(TAPS), channels), F32),
-        in_specs=[smem] + [vmem] * 6,
+        in_specs=[smem] + [vmem] * 8,
         out_specs=vmem,
         scratch_shapes=[pltpu.VMEM((channels, table.shape[0]), F32)],
         compiler_params=SMALL,
         name="tap_sums",
-    )(flags, *on_chip(edges, above, below, stats, taps, table))
-
-
-def beside(edges, axis):
+    )(flags, *on_chip(tops, bottoms, above, below, stats, taps, table, jnp.asarray(halo_table)))
+
+
+def beside(top, bottom, axis):
     count = lax.axis_size(axis)
-    top = edges[:, :DILATION_STEP]
-    bottom = edges[:, -DILATION_STEP:]
     if count == 2:
         sent = jnp.where(lax.axis_index(axis) == 0, bottom, top)
         got = lax.ppermute(sent, axis, [(0, 1), (1, 0)])
@@ -626,9 +743,15 @@
     return lax.ppermute(bottom, axis, forward), lax.ppermute(top, axis, backward)
 
 
+def partner(value, axis):
+    if lax.axis_size(axis) == 2:
+        return lax.ppermute(value, axis, [(0, 1), (1, 0)])
+    return lax.psum(value, axis) - value
+
+
 def total(value, axis):
     if lax.axis_size(axis) == 2:
-        return value + lax.ppermute(value, axis, [(0, 1), (1, 0)])
+        return added(value, partner(value, axis))
     return lax.psum(value, axis)
 
 
@@ -647,33 +770,29 @@
 ):
     step_count, _, rows, _ = frames.shape
     place = lax.axis_index("tm").astype(jnp.int32)[None]
-    edges = jnp.concatenate([frames[:, :, :EDGE], frames[:, :, rows - EDGE :]], axis=2)
-    edges = edges.transpose(0, 2, 1, 3)
-    above, below = beside(edges, "space")
+    flags = history(observed[None], "tm")
+    tops = frames[:, :, :EDGE].transpose(0, 2, 1, 3)
+    bottoms = frames[:, :, rows - EDGE :].transpose(0, 2, 1, 3)
+    above, below = beside(tops[:, :DILATION_STEP], bottoms[:, DILATION_STEP:], "space")
     taps, gain = conv_taps.T, gain_matrix.T
     span = 2 if step_count % 2 == 0 else 1
     part, stats = frame_sums(taps, observed, frames, pooling)
     gain_part = gain_sums(observed, above, below, part, taps, pooling, gain)
-    map_high, map_low, grams, first_gram = prepare(
-        transition, update_map, quiet_root, observed_root, init_root
+    shifts = total(gain_part, "chan")
+    gradient = tap_sums(observed, tops, bottoms, above, below, stats, taps, rows)
+    shifts = total(shifts, "space")
+    map_high, map_low, span_high, span_low, span_gram, first_gram = prepare(
+        span, transition, update_map, quiet_root, observed_root, init_root
     )
-    shifts = total(gain_part, "chan")
-    gradient = tap_sums(observed, edges, above, below, stats, taps, rows)
-    shifts = total(shifts, "space")
-    flag_row = jnp.pad(observed.astype(F32)[None], ((0, 0), (0, shifts.shape[1] - step_count)))
-    held = history(jnp.concatenate([shifts, flag_row], axis=0)[None], "tm")
-    flags = held[:, step_count, :step_count].astype(jnp.int32).reshape(-1)
-    if span == 2:
-        span_high, span_low, span_gram = pair_maps(map_high, map_low, grams)
-    else:
-        span_high, span_low, span_gram = map_high, map_low, grams
-    gradient = total(gradient, "space")
+    held = history(shifts[None], "tm")
+    gradient_beside = partner(gradient, "space")
     gram = recursion(place, flags, step_count, span, span_high, span_low, span_gram, first_gram)
-    root, filtered_means = factor(
-        place, flags, step_count, span, gram,
-        map_high, map_low, span_high, span_low, held, init_mean,
+    tops = factor_top(gram)
+    root, filtered_means, gradient = factor(
+        place, flags, step_count, span, gram, tops,
+        map_high, map_low, span_high, span_low, held, init_mean, gradient, gradient_beside,
     )
-    return (filtered_means, root[None], gradient.T[None])
+    return (filtered_means, root[None], gradient.transpose(1, 2, 0))
 
 
 def solution(mesh):

time: 47.8 us -> 45 us (0.941)
  local copies, waits for them, and re-layouts: 8.91 us -> 1.6 us
  waiting for transfers between devices: 5.02 us -> 10.9 us
  other arithmetic: 1.11 us -> 0.02 us
    unnamed x35 -> x24, local copies, waits for them, and re-layouts: 7.27 us -> 0.07 us
    ppermute x6 -> x7, waiting for transfers between devices: 5.01 us -> 10.9 us  [the longest x4 6.17 us: history(): lax.ppermute(sent, axis, [(i, i ^ reach) for i in range(count)])]
    pallas_call x1, Pallas kernels: 9.71 us -> 5.68 us  [factor(): pl.pallas_call(kernel, out_shape=(jax.ShapeDtypeStruct((size, size), F32)...]
    pallas_call x2 -> x6, Pallas kernels: 2.64 us -> 6.41 us  [the longest x1 4.03 us: factor_top(): pl.pallas_call(factor_top_kernel, out_shape=(pltpu.VMEM((rows, size), F32...]
    transpose x1 -> x0, other arithmetic: 1.04 us -> none  [local(): edges = edges.transpose(0, 2, 1, 3)]
    ppermute x6 -> x7, starting transfers between devices: 6.76 us -> 6.81 us  [the longest x4 6.14 us: history(): lax.ppermute(sent, axis, [(i, i ^ reach) for i in range(count)])]
  transfers between devices with their start and end apart: 7 -> 8, of which waited for: 3 -> 4; matrix products, arithmetic and copies ran while one was open for 1% -> 0% of each run, Pallas kernels for 19% -> 33%
where the time goes in v5:
time: 45 us; the launch traced here: 44.8 us
  Pallas kernels  21.6 us (48%)
  waiting for transfers between devices  10.9 us (24%)
  starting transfers between devices  9.84 us (22%)
  local copies, waits for them, and re-layouts  1.6 us (4%)
  between operations  0.87 us (2%)
    ppermute x4, waiting for transfers between devices, history(): lax.ppermute(sent, axis, [(i, i ^ reach) for i in range(count)])  6.17 us
    ppermute x4, starting transfers between devices, history(): lax.ppermute(sent, axis, [(i, i ^ reach) for i in range(count)])  6.14 us
    pallas_call x1, Pallas kernels, factor(): pl.pallas_call(kernel, out_shape=(jax.ShapeDtypeStruct((size, size), F32)...  5.68 us
    pallas_call x1, Pallas kernels, frame_sums(): pl.pallas_call(kernel, out_shape=(pltpu.VMEM((steps, channels, LANES), F3...  5.13 us
    ppermute x3, waiting for transfers between devices, partner(): return lax.ppermute(value, axis, [(0, 1), (1, 0)])  4.72 us
    pallas_call x1, Pallas kernels, factor_top(): pl.pallas_call(factor_top_kernel, out_shape=(pltpu.VMEM((rows, size), F32...  4.03 us
    ppermute x1, starting transfers between devices, beside(): got = lax.ppermute(sent, axis, [(0, 1), (1, 0)])  3.03 us
    pallas_call x1, Pallas kernels, prepare(): pl.pallas_call(kernel, out_shape=(pltpu.VMEM((2, size, size), BF16), pltp...  2.37 us
  transfers between devices with their start and end apart: 8, of which 4 were waited for; matrix products, arithmetic and copies ran while one was open for 0% of the time, Pallas kernels for 33%

profile of v5, /device:TPU:0, one launch (start us, length us, event | category | flops | bytes accessed | tf_op | source)
XLA Modules:
  0.0 44.8 jit_solution(9532903389614685220)
XLA Ops:
  0.6 0.0 copy-start.9
  0.6 0.0 copy-start.7
  0.7 0.0 copy-start.6
  0.7 0.0 copy-start.8
  0.7 1.4 %fusion = (bf16[4,32,4,256]{3,2,1,0:T(4,128)(2,1)S(1)}, bf16[4,32,4,256]{3,2,1,0:T(4,128)(2,1)S(1)}) fusion(bf16[4,32,32,256]{3,2,1,0:T(8,128)(2,1)} %refs_2_.3), kind=kLoop, calls=%fused_computation.3 | loop fusion | bytes 1048576 | tf_op jit(solution)/shard_map/slice | solution.py:775
  2.1 0.0 copy-start
  2.1 0.0 copy-start.10
  2.1 0.1 copy_bitcast_fusion
  2.2 0.0 copy-start.1
  2.3 0.0 copy-start.2
  2.3 0.0 copy-start.3
  2.3 0.0 copy-start.4
  2.3 0.0 copy-start.5
  2.3 3.0 %collective-permute-start.2 = (bf16[4,2,32,256]{3,2,1,0:T(8,128)(2,1)S(1)}, bf16[4,2,32,256]{3,2,1,0:T(8,128)(2,1)S(1)}, u32[]{:S(2)}, u32[]{:S(2)}) collective-permute-start(bf16[4,2,32,256]{3,2,1,0:T(8,128)(2,1)S(1)} %slice_select_fusion), channel_id=1, source_target_pairs={{0,2},{2,0},{1,3},{3,1},{4,6},{6,4},{5,7},{7,5},{8,10},{10,8},{9,1... | collective-permute-start | bytes 393224 | tf_op jit(solution)/shard_map/ppermute | solution.py:739
  5.4 0.0 copy-done.9
  5.4 0.0 copy-done.7
  5.4 0.0 copy-done.6
  5.4 5.1 %frame_sums.1 = (f32[4,32,128]{2,1,0:T(8,128)S(1)}, f32[32,1024]{1,0:T(8,128)S(1)}) custom-call(f32[9,32]{1,0:T(8,128)S(1)} %bitcast.12, s32[4]{0:T(128)S(1)} %copy-done.9, bf16[4,32,32,256]{3,2,1,0:T(8,128)(2,1)} %refs_2_.3, f32[32,256]{1,0:T(8,128)S(1)} %copy-done.6), custom_call_target="tpu_custom_call" | custom-call | tf_op jit(solution)/shard_map/frame_sums/pallas_call | solution.py:548
  10.5 0.0 collective-permute-done.2.refs_3_.refs_4_.above.below
  10.5 0.0 copy-done.8
  10.5 1.2 %gain_sums.1.a = f32[4,256]{1,0:T(4,128)S(1)} custom-call(s32[4]{0:T(128)S(1)} %copy-done.9, bf16[4,2,32,256]{3,2,1,0:T(8,128)(2,1)S(1)} %collective-permute-done.2.refs_3_.refs_4_.above.below, bf16[4,2,32,256]{3,2,1,0:T(8,128)(2,1)S(1)} %collective-permute-done.2.refs_3_.refs_4_.above.below, f32[4,32,128]{2,1,0:T(8,128)S(1)} %get-tuple-element.27.part, ...), custom_call_target="tpu_custom_call" | custom-call | tf_op jit(solution)/shard_map/gain_sums/pallas_call | solution.py:653
  11.8 0.0 collective-permute-start.4
  11.8 1.2 %collective-permute-done.4.b = f32[4,256]{1,0:T(4,128)S(1)} collective-permute-done((f32[4,256]{1,0:T(4,128)S(1)}, f32[4,256]{1,0:T(4,128)S(1)}, u32[]{:S(2)}, u32[]{:S(2)}) %collective-permute-start.4) | collective-permute-done | bytes 4128 | tf_op jit(solution)/shard_map/ppermute | solution.py:748
  12.9 0.1 collective-permute-start.5
  13.0 3.5 %collective-permute-done.5.b = f32[4,256]{1,0:T(4,128)S(1)} collective-permute-done((f32[4,256]{1,0:T(4,128)S(1)}, f32[4,256]{1,0:T(4,128)S(1)}, u32[]{:S(2)}, u32[]{:S(2)}) %collective-permute-start.5) | collective-permute-done | bytes 4128 | tf_op jit(solution)/shard_map/ppermute | solution.py:748
  16.6 1.6 %collective-permute-start.6 = (f32[1,4,256]{2,1,0:T(4,128)S(1)}, f32[1,4,256]{2,1,0:T(4,128)S(1)}, u32[]{:S(2)}, u32[]{:S(2)}) collective-permute-start(f32[1,4,256]{2,1,0:T(4,128)S(1)} %bitcast.15), channel_id=1, source_target_pairs={{0,4},{4,0},{8,12},{12,8},{1,5},{5,1},{9,13},{13,9},{2,6},{6,2},{1... | collective-permute-start | bytes 12296 | tf_op jit(solution)/shard_map/ppermute | solution.py:69
  18.1 2.0 %collective-permute-done.6.b.refs_16_ = f32[1,4,256]{2,1,0:T(4,128)S(1)} collective-permute-done((f32[1,4,256]{2,1,0:T(4,128)S(1)}, f32[1,4,256]{2,1,0:T(4,128)S(1)}, u32[]{:S(2)}, u32[]{:S(2)}) %collective-permute-start.6) | collective-permute-done | bytes 4128 | tf_op jit(solution)/shard_map/ppermute | solution.py:69
  20.2 2.6 %collective-permute-start.7 = (f32[2,4,256]{2,1,0:T(4,128)S(1)}, f32[2,4,256]{2,1,0:T(4,128)S(1)}, u32[]{:S(2)}, u32[]{:S(2)}) collective-permute-start(f32[2,4,256]{2,1,0:T(4,128)S(1)} %joined.3), channel_id=1, source_target_pairs={{0,8},{4,12},{8,0},{12,4},{1,9},{5,13},{9,1},{13,5},{2,10},{6,14},... | collective-permute-start | bytes 24584 | tf_op jit(solution)/shard_map/ppermute | solution.py:69
  22.8 0.0 copy-done
  22.8 0.0 copy-done.10
  22.8 1.5 %tap_sums.1.refs_13_ = f32[9,32]{1,0:T(8,128)S(1)} custom-call(s32[4]{0:T(128)S(1)} %copy-done.9, bf16[4,4,32,256]{3,2,1,0:T(8,128)(2,1)S(1)} %get-tuple-element.34.refs_1_, bf16[4,4,32,256]{3,2,1,0:T(8,128)(2,1)S(1)} %get-tuple-element.33.refs_2_, bf16[4,2,32,256]{3,2,1,0:T(8,128)(2,1)S(1)} %collective-permute-done.2.refs_3_.refs_4_.above.below, ...), custom_call_target="tpu_custom_call" | custom-call | tf_op jit(solution)/shard_map/tap_sums/pallas_call | solution.py:724
  24.2 0.6 %collective-permute-start.3 = (f32[9,32]{1,0:T(8,128)S(1)}, f32[9,32]{1,0:T(8,128)S(1)}, u32[]{:S(2)}, u32[]{:S(2)}) collective-permute-start(f32[9,32]{1,0:T(8,128)S(1)} %tap_sums.1.refs_13_), channel_id=1, source_target_pairs={{0,2},{2,0},{1,3},{3,1},{4,6},{6,4},{5,7},{7,5},{8,10},{10,8},{9,1... | collective-permute-start | bytes 3464 | tf_op jit(solution)/shard_map/ppermute | solution.py:748
  24.8 1.6 %collective-permute-start = (s32[1,4]{1,0:T(1,128)S(1)}, s32[1,4]{1,0:T(1,128)S(1)}, u32[]{:S(2)}, u32[]{:S(2)}) collective-permute-start(s32[1,4]{1,0:T(1,128)S(1)} %bitcast.19), channel_id=1, source_target_pairs={{0,4},{4,0},{8,12},{12,8},{1,5},{5,1},{9,13},{13,9},{2,6},{6,2},{1... | collective-permute-start | bytes 56 | tf_op jit(solution)/shard_map/ppermute | solution.py:69
  26.4 0.0 copy-done.1
  26.4 0.0 copy-done.2
  26.4 0.0 copy-done.3
  26.4 0.0 copy-done.4
  26.4 0.0 copy-done.5
  26.4 0.0 copy-start.11
  26.4 2.4 %prepare.1 = (bf16[2,256,256]{2,1,0:T(8,128)(2,1)S(1)}, bf16[2,256,256]{2,1,0:T(8,128)(2,1)S(1)}, bf16[4,256,256]{2,1,0:T(8,128)(2,1)S(1)}, bf16[4,256,256]{2,1,...) custom-call(f32[256,256]{1,0:T(8,128)S(1)} %copy-done.1, f32[256,256]{1,0:T(8,128)S(1)} %copy-done.2, ...), custom_call_target="tpu_custom_call" | custom-call | tf_op jit(solution)/shard_map/prepare/pallas_call | solution.py:143
  28.8 0.0 collective-permute-done.b.refs_2_
  28.8 0.4 collective-permute-start.1
  29.2 4.1 %collective-permute-done.1.refs_3_ = s32[2,4]{1,0:T(2,128)S(1)} collective-permute-done((s32[2,4]{1,0:T(2,128)S(1)}, s32[2,4]{1,0:T(2,128)S(1)}, u32[]{:S(2)}, u32[]{:S(2)}) %collective-permute-start.1) | collective-permute-done | bytes 64 | tf_op jit(solution)/shard_map/ppermute | solution.py:69
  33.4 1.7 %recursion.1.gram.refs_4_ = f32[256,256]{1,0:T(8,128)S(1)} custom-call(s32[1]{0:T(128)} %bitcast.refs_0_, s32[1,4]{1,0:T(1,128)S(1)} %bitcast.21, s32[1,4]{1,0:T(1,128)S(1)} %collective-permute-done.b.refs_2_, s32[2,4]{1,0:T(2,128)S(1)} %collective-permute-done.1.refs_3_, bf16[4,256,256]{2,1,0:T(8,128)(2,1)S(1)} %get-tuple-element.17.refs_4_.refs_10_, ...), custom_call_target="tpu_custom_call" | custom-call | tf_op jit(solution)/shard_map/recursion/pallas_call | solution.py:299
  35.1 4.0 %factor_top.1 = (f32[128,256]{1,0:T(8,128)S(1)}, bf16[128,256]{1,0:T(8,128)(2,1)S(1)}, bf16[128,256]{1,0:T(8,128)(2,1)S(1)}) custom-call(f32[256,256]{1,0:T(8,128)S(1)} %recursion.1.gram.refs_4_), custom_call_target="tpu_custom_call" | custom-call | tf_op jit(solution)/shard_map/factor_top/pallas_call | solution.py:317
  39.1 0.0 collective-permute-done.3.refs_14_
  39.1 0.0 collective-permute-done.7.refs_17_
  39.1 5.7 %factor.1 = (f32[256,256]{1,0:T(8,128)}, f32[4,256]{1,0:T(4,128)}, f32[9,1,32]{2,1,0:T(1,128)}) custom-call(s32[1]{0:T(128)} %bitcast.refs_0_, s32[1,4]{1,0:T(1,128)S(1)} %bitcast.22, s32[1,4]{1,0:T(1,128)S(1)} %collective-permute-done.b.refs_2_, s32[2,4]{1,0:T(2,128)S(1)} %collective-permute-done.1.refs_3_, f32[256,256]{1,0:T(8,128)S(1)} %recursion.1.gram.refs_4_, ...), custom_call_target="tpu_custom_call" | custom-call | tf_op jit(solution)/shard_map/factor/pallas_call | solution.py:409
  (6 shorter events, 0.0 us)
Async XLA Ops:
  0.6 4.7 %copy-start.9 = (s32[4]{0:T(128)S(1)}, s32[4]{0:T(128)}, u32[]{:S(2)}) copy-start(s32[4]{0:T(128)} %flags.1) | copy-start | bytes 52
  0.6 4.7 %copy-start.7 = (f32[32,9]{0,1:T(8,128)S(1)}, f32[32,9]{0,1:T(8,128)}, u32[]{:S(2)}) copy-start(f32[32,9]{0,1:T(8,128)} %param.14) | copy-start | bytes 3460
  0.7 4.7 %copy-start.6 = (f32[32,256]{1,0:T(8,128)S(1)}, f32[32,256]{1,0:T(8,128)}, u32[]{:S(2)}) copy-start(f32[32,256]{1,0:T(8,128)} %pooling.1) | copy-start | bytes 98308
  0.7 9.9 %copy-start.8 = (f32[256,32]{0,1:T(8,128)S(1)}, f32[256,32]{0,1:T(8,128)}, u32[]{:S(2)}) copy-start(f32[256,32]{0,1:T(8,128)} %param.16) | copy-start | bytes 98308
  2.1 20.6 %copy-start = (bf16[1280,128]{1,0:T(8,128)(2,1)S(1)}, bf16[1280,128]{1,0:T(8,128)(2,1)}, u32[]{:S(2)}) copy-start(bf16[1280,128]{1,0:T(8,128)(2,1)} %constant.15.clone.refs_7_) | copy-start | bytes 983044
  2.1 20.6 %copy-start.10 = (f32[16,128]{1,0:T(8,128)S(1)}, f32[16,128]{1,0:T(8,128)}, u32[]{:S(2)}) copy-start(f32[16,128]{1,0:T(8,128)} %constant.16.clone.refs_8_) | copy-start | bytes 24580
  2.2 24.2 %copy-start.1 = (f32[256,256]{1,0:T(8,128)S(1)}, f32[256,256]{1,0:T(8,128)}, u32[]{:S(2)}) copy-start(f32[256,256]{1,0:T(8,128)} %refs_0_.2) | copy-start | bytes 786436
  2.3 24.1 %copy-start.2 = (f32[256,256]{1,0:T(8,128)S(1)}, f32[256,256]{1,0:T(8,128)}, u32[]{:S(2)}) copy-start(f32[256,256]{1,0:T(8,128)} %refs_1_.2) | copy-start | bytes 786436
  2.3 24.1 %copy-start.3 = (f32[256,256]{1,0:T(8,128)S(1)}, f32[256,256]{1,0:T(8,128)}, u32[]{:S(2)}) copy-start(f32[256,256]{1,0:T(8,128)} %refs_2_.2) | copy-start | bytes 786436
  2.3 24.1 %copy-start.4 = (f32[256,256]{1,0:T(8,128)S(1)}, f32[256,256]{1,0:T(8,128)}, u32[]{:S(2)}) copy-start(f32[256,256]{1,0:T(8,128)} %refs_3_.2) | copy-start | bytes 786436
  2.3 24.1 %copy-start.5 = (f32[256,256]{1,0:T(8,128)S(1)}, f32[256,256]{1,0:T(8,128)}, u32[]{:S(2)}) copy-start(f32[256,256]{1,0:T(8,128)} %refs_4_.1) | copy-start | bytes 786436
  2.3 8.2 %collective-permute-start.2 = (bf16[4,2,32,256]{3,2,1,0:T(8,128)(2,1)S(1)}, bf16[4,2,32,256]{3,2,1,0:T(8,128)(2,1)S(1)}, u32[]{:S(2)}, u32[]{:S(2)}) collective-permute-start(bf16[4,2,32,256]{3,2,1,0:T(8,128)(2,1)S(1)} %slice_select_fusion), channel_id=1, source_target_pairs={{0,2},{2,0},{1,3},{3,1},{4,6},{6,4},{5,7},{7,5},{8,10},{10,8},{9,1... | collective-permute-start | bytes 393224 | tf_op jit(solution)/shard_map/ppermute | solution.py:739
  11.8 1.2 %collective-permute-start.4 = (f32[4,256]{1,0:T(4,128)S(1)}, f32[4,256]{1,0:T(4,128)S(1)}, u32[]{:S(2)}, u32[]{:S(2)}) collective-permute-start(f32[4,256]{1,0:T(4,128)S(1)} %gain_sums.1.a), channel_id=1, source_target_pairs={{0,1},{1,0},{2,3},{3,2},{4,5},{5,4},{6,7},{7,6},{8,9},{9,8},{10,11... | collective-permute-start | bytes 12296 | tf_op jit(solution)/shard_map/ppermute | solution.py:748
  12.9 3.6 %collective-permute-start.5 = (f32[4,256]{1,0:T(4,128)S(1)}, f32[4,256]{1,0:T(4,128)S(1)}, u32[]{:S(2)}, u32[]{:S(2)}) collective-permute-start(f32[4,256]{1,0:T(4,128)S(1)} %added.2.a), channel_id=1, source_target_pairs={{0,2},{2,0},{1,3},{3,1},{4,6},{6,4},{5,7},{7,5},{8,10},{10,8},{9,1... | collective-permute-start | bytes 12296 | tf_op jit(solution)/shard_map/ppermute | solution.py:748
  16.6 3.6 %collective-permute-start.6 = (f32[1,4,256]{2,1,0:T(4,128)S(1)}, f32[1,4,256]{2,1,0:T(4,128)S(1)}, u32[]{:S(2)}, u32[]{:S(2)}) collective-permute-start(f32[1,4,256]{2,1,0:T(4,128)S(1)} %bitcast.15), channel_id=1, source_target_pairs={{0,4},{4,0},{8,12},{12,8},{1,5},{5,1},{9,13},{13,9},{2,6},{6,2},{1... | collective-permute-start | bytes 12296 | tf_op jit(solution)/shard_map/ppermute | solution.py:69
  20.2 19.0 %collective-permute-start.7 = (f32[2,4,256]{2,1,0:T(4,128)S(1)}, f32[2,4,256]{2,1,0:T(4,128)S(1)}, u32[]{:S(2)}, u32[]{:S(2)}) collective-permute-start(f32[2,4,256]{2,1,0:T(4,128)S(1)} %joined.3), channel_id=1, source_target_pairs={{0,8},{4,12},{8,0},{12,4},{1,9},{5,13},{9,1},{13,5},{2,10},{6,14},... | collective-permute-start | bytes 24584 | tf_op jit(solution)/shard_map/ppermute | solution.py:69
  24.2 14.9 %collective-permute-start.3 = (f32[9,32]{1,0:T(8,128)S(1)}, f32[9,32]{1,0:T(8,128)S(1)}, u32[]{:S(2)}, u32[]{:S(2)}) collective-permute-start(f32[9,32]{1,0:T(8,128)S(1)} %tap_sums.1.refs_13_), channel_id=1, source_target_pairs={{0,2},{2,0},{1,3},{3,1},{4,6},{6,4},{5,7},{7,5},{8,10},{10,8},{9,1... | collective-permute-start | bytes 3464 | tf_op jit(solution)/shard_map/ppermute | solution.py:748
  24.8 4.0 %collective-permute-start = (s32[1,4]{1,0:T(1,128)S(1)}, s32[1,4]{1,0:T(1,128)S(1)}, u32[]{:S(2)}, u32[]{:S(2)}) collective-permute-start(s32[1,4]{1,0:T(1,128)S(1)} %bitcast.19), channel_id=1, source_target_pairs={{0,4},{4,0},{8,12},{12,8},{1,5},{5,1},{9,13},{13,9},{2,6},{6,2},{1... | collective-permute-start | bytes 56 | tf_op jit(solution)/shard_map/ppermute | solution.py:69
  26.4 12.7 %copy-start.11 = (f32[256]{0:T(256)S(1)}, f32[256]{0:T(256)}, u32[]{:S(2)}) copy-start(f32[256]{0:T(256)} %param.21) | copy-start | bytes 3076
  28.8 4.5 %collective-permute-start.1 = (s32[2,4]{1,0:T(2,128)S(1)}, s32[2,4]{1,0:T(2,128)S(1)}, u32[]{:S(2)}, u32[]{:S(2)}) collective-permute-start(s32[2,4]{1,0:T(2,128)S(1)} %joined.2), channel_id=1, source_target_pairs={{0,8},{4,12},{8,0},{12,4},{1,9},{5,13},{9,1},{13,5},{2,10},{6,14},... | collective-permute-start | bytes 104 | tf_op jit(solution)/shard_map/ppermute | solution.py:69

commit v6 on v5

--- a/solution.py
+++ b/solution.py
@@ -54,6 +54,38 @@
         compiler_params=SMALL,
         name="added",
     )(*on_chip(a, b))
+
+
+def packed_kernel(mine, got, gradient, out):
+    steps = mine.shape[0]
+    taps, channels = gradient.shape
+    out[...] = jnp.zeros(out.shape, F32)
+    out[:steps] = mine[...] + got[...]
+    out[TAP_ROW : TAP_ROW + taps, :channels] = gradient[...]
+
+
+def packed(mine, got, gradient):
+    rows = TAP_ROW + -(-gradient.shape[0] // GROUP) * GROUP
+    return pl.pallas_call(
+        packed_kernel,
+        out_shape=jax.ShapeDtypeStruct((rows, mine.shape[1]), F32),
+        compiler_params=SMALL,
+        name="packed",
+    )(*on_chip(mine, got, gradient))
+
+
+def first_sum_kernel(mine, got, out):
+    steps = out.shape[1]
+    out[0] = mine[:steps] + got[:steps]
+
+
+def first_sum(mine, got, steps):
+    return pl.pallas_call(
+        first_sum_kernel,
+        out_shape=jax.ShapeDtypeStruct((1, steps, mine.shape[1]), F32),
+        compiler_params=SMALL,
+        name="first_sum",
+    )(*on_chip(mine, got))
 
 
 def history(own, axis):
@@ -346,7 +378,8 @@
         shifts[slot : slot + piece.shape[0]] = piece[...]
         slot += piece.shape[0]
     begin = top.shape[0]
-    gradient_out[:, 0, :] = gradient[...] + gradient_beside[...]
+    area = (pl.ds(TAP_ROW, gradient_out.shape[0]), pl.ds(0, gradient_out.shape[2]))
+    gradient_out[:, 0, :] = gradient[area] + gradient_beside[area]
     out[:begin] = top[...]
     high[:begin] = top_high[...]
     low[:begin] = top_low[...]
@@ -395,10 +428,10 @@
 
 def factor(
     place, flags, steps, span, gram, tops, map_high, map_low, span_high, span_low, shifts,
-    init_mean, gradient, gradient_beside,
+    init_mean, gradient, gradient_beside, channels,
 ):
     size = gram.shape[0]
-    taps, channels = gradient.shape
+    taps = len(TAPS)
     count = sum(piece.shape[0] for piece in flags)
     vmem = pl.BlockSpec(memory_space=pltpu.VMEM)
     smem = pl.BlockSpec(memory_space=pltpu.SMEM)
@@ -438,6 +471,7 @@
 TAPS = tuple((a, b) for a in (-1, 0, 1) for b in (-1, 0, 1))
 EDGE = 2 * DILATION_STEP
 KINDS = 8
+TAP_ROW = 8
 EDGE_KINDS = 2
 HALO_KINDS = 7
 
@@ -540,7 +574,7 @@
     vmem = pl.BlockSpec(memory_space=pltpu.VMEM)
     smem = pl.BlockSpec(memory_space=pltpu.SMEM)
 
-    unroll = math.gcd(channels, 8)
+    unroll = math.gcd(channels, 16)
 
     def kernel(*refs):
         frames_kernel(unroll, *refs)
@@ -768,7 +802,7 @@
     init_root,
     observed,
 ):
-    step_count, _, rows, _ = frames.shape
+    step_count, channels, rows, _ = frames.shape
     place = lax.axis_index("tm").astype(jnp.int32)[None]
     flags = history(observed[None], "tm")
     tops = frames[:, :, :EDGE].transpose(0, 2, 1, 3)
@@ -778,19 +812,27 @@
     span = 2 if step_count % 2 == 0 else 1
     part, stats = frame_sums(taps, observed, frames, pooling)
     gain_part = gain_sums(observed, above, below, part, taps, pooling, gain)
-    shifts = total(gain_part, "chan")
     gradient = tap_sums(observed, tops, bottoms, above, below, stats, taps, rows)
-    shifts = total(shifts, "space")
     map_high, map_low, span_high, span_low, span_gram, first_gram = prepare(
         span, transition, update_map, quiet_root, observed_root, init_root
     )
-    held = history(shifts[None], "tm")
-    gradient_beside = partner(gradient, "space")
+    if lax.axis_size("chan") == 2 and step_count <= TAP_ROW:
+        both = packed(gain_part, partner(gain_part, "chan"), gradient)
+        both_beside = partner(both, "space")
+        shifts = first_sum(both, both_beside, step_count)
+    else:
+        both = jnp.pad(
+            gradient,
+            ((TAP_ROW, 2 * GROUP - len(TAPS)), (0, gain.shape[1] - channels)),
+        )
+        shifts = total(total(gain_part, "chan"), "space")[None]
+        both_beside = partner(both, "space")
+    held = history(shifts, "tm")
     gram = recursion(place, flags, step_count, span, span_high, span_low, span_gram, first_gram)
     tops = factor_top(gram)
     root, filtered_means, gradient = factor(
         place, flags, step_count, span, gram, tops,
-        map_high, map_low, span_high, span_low, held, init_mean, gradient, gradient_beside,
+        map_high, map_low, span_high, span_low, held, init_mean, both, both_beside, channels,
     )
     return (filtered_means, root[None], gradient.transpose(1, 2, 0))
 

time: 45 us -> 43.4 us (0.964)
  waiting for transfers between devices: 10.9 us -> 9.81 us
    ppermute x3 -> x2, waiting for transfers between devices: 4.72 us -> 3.63 us  [partner(): return lax.ppermute(value, axis, [(0, 1), (1, 0)])]
  transfers between devices with their start and end apart: 8 -> 7, of which waited for: 4 -> 3; matrix products, arithmetic and copies ran while one was open for 0% -> 0% of each run, Pallas kernels for 33% -> 34%
where the time goes in v6:
time: 43.4 us; the launch traced here: 43.3 us
  Pallas kernels  21.5 us (50%)
  waiting for transfers between devices  9.81 us (23%)
  starting transfers between devices  9.44 us (22%)
  local copies, waits for them, and re-layouts  1.61 us (4%)
  between operations  0.87 us (2%)
    ppermute x4, waiting for transfers between devices, history(): lax.ppermute(sent, axis, [(i, i ^ reach) for i in range(count)])  6.17 us
    ppermute x4, starting transfers between devices, history(): lax.ppermute(sent, axis, [(i, i ^ reach) for i in range(count)])  6.14 us
    pallas_call x1, Pallas kernels, factor(): pl.pallas_call(kernel, out_shape=(jax.ShapeDtypeStruct((size, size), F32)...  5.68 us
    pallas_call x1, Pallas kernels, frame_sums(): pl.pallas_call(kernel, out_shape=(pltpu.VMEM((steps, channels, LANES), F3...  5 us
    pallas_call x1, Pallas kernels, factor_top(): pl.pallas_call(factor_top_kernel, out_shape=(pltpu.VMEM((rows, size), F32...  4.03 us
    ppermute x2, waiting for transfers between devices, partner(): return lax.ppermute(value, axis, [(0, 1), (1, 0)])  3.63 us
    ppermute x1, starting transfers between devices, beside(): got = lax.ppermute(sent, axis, [(0, 1), (1, 0)])  3.03 us
    pallas_call x1, Pallas kernels, prepare(): pl.pallas_call(kernel, out_shape=(pltpu.VMEM((2, size, size), BF16), pltp...  2.37 us
  transfers between devices with their start and end apart: 7, of which 3 were waited for; matrix products, arithmetic and copies ran while one was open for 0% of the time, Pallas kernels for 34%

profile of v6, /device:TPU:0, one launch (start us, length us, event | category | flops | bytes accessed | tf_op | source)
XLA Modules:
  0.0 43.3 jit_solution(7539949712895402091)
XLA Ops:
  0.6 0.0 copy-start.9
  0.6 0.0 copy-start.7
  0.7 0.0 copy-start.6
  0.7 0.0 copy-start.8
  0.7 1.4 %fusion = (bf16[4,32,4,256]{3,2,1,0:T(4,128)(2,1)S(1)}, bf16[4,32,4,256]{3,2,1,0:T(4,128)(2,1)S(1)}) fusion(bf16[4,32,32,256]{3,2,1,0:T(8,128)(2,1)} %refs_2_.3), kind=kLoop, calls=%fused_computation.3 | loop fusion | bytes 1048576 | tf_op jit(solution)/shard_map/slice | solution.py:809
  2.1 0.0 copy-start
  2.1 0.0 copy-start.10
  2.1 0.1 copy_bitcast_fusion
  2.2 0.0 copy-start.1
  2.3 0.0 copy-start.2
  2.3 0.0 copy-start.3
  2.3 0.0 copy-start.4
  2.3 0.0 copy-start.5
  2.3 3.0 %collective-permute-start.2 = (bf16[4,2,32,256]{3,2,1,0:T(8,128)(2,1)S(1)}, bf16[4,2,32,256]{3,2,1,0:T(8,128)(2,1)S(1)}, u32[]{:S(2)}, u32[]{:S(2)}) collective-permute-start(bf16[4,2,32,256]{3,2,1,0:T(8,128)(2,1)S(1)} %slice_select_fusion), channel_id=1, source_target_pairs={{0,2},{2,0},{1,3},{3,1},{4,6},{6,4},{5,7},{7,5},{8,10},{10,8},{9,1... | collective-permute-start | bytes 393224 | tf_op jit(solution)/shard_map/ppermute | solution.py:773
  5.4 0.0 copy-done.9
  5.4 0.0 copy-done.7
  5.4 0.0 copy-done.6
  5.4 5.0 %frame_sums.1 = (f32[4,32,128]{2,1,0:T(8,128)S(1)}, f32[32,1024]{1,0:T(8,128)S(1)}) custom-call(f32[9,32]{1,0:T(8,128)S(1)} %bitcast.11, s32[4]{0:T(128)S(1)} %copy-done.9, bf16[4,32,32,256]{3,2,1,0:T(8,128)(2,1)} %refs_2_.3, f32[32,256]{1,0:T(8,128)S(1)} %copy-done.6), custom_call_target="tpu_custom_call" | custom-call | tf_op jit(solution)/shard_map/frame_sums/pallas_call | solution.py:582
  10.4 0.0 collective-permute-done.2.above.below.refs_3_.refs_4_
  10.4 0.0 copy-done.8
  10.4 1.2 %gain_sums.1.mine = f32[4,256]{1,0:T(4,128)S(1)} custom-call(s32[4]{0:T(128)S(1)} %copy-done.9, bf16[4,2,32,256]{3,2,1,0:T(8,128)(2,1)S(1)} %collective-permute-done.2.above.below.refs_3_.refs_4_, bf16[4,2,32,256]{3,2,1,0:T(8,128)(2,1)S(1)} %collective-permute-done.2.above.below.refs_3_.refs_4_, f32[4,32,128]{2,1,0:T(8,128)S(1)} %get-tuple-element.26.part, ...), custom_call_target="tpu_custom_call" | custom-call | tf_op jit(solution)/shard_map/gain_sums/pallas_call | solution.py:687
  11.6 0.0 collective-permute-start.3
  11.6 0.0 copy-done
  11.6 0.0 copy-done.10
  11.7 1.5 %tap_sums.1.gradient = f32[9,32]{1,0:T(8,128)S(1)} custom-call(s32[4]{0:T(128)S(1)} %copy-done.9, bf16[4,4,32,256]{3,2,1,0:T(8,128)(2,1)S(1)} %get-tuple-element.33.refs_1_, bf16[4,4,32,256]{3,2,1,0:T(8,128)(2,1)S(1)} %get-tuple-element.34.refs_2_, bf16[4,2,32,256]{3,2,1,0:T(8,128)(2,1)S(1)} %collective-permute-done.2.above.below.refs_3_.refs_4_, ...), custom_call_target="tpu_custom_call" | custom-call | tf_op jit(solution)/shard_map/tap_sums/pallas_call | solution.py:758
  13.1 0.0 collective-permute-done.3.got
  13.1 0.1 packed.1.mine.refs_13_
  13.2 0.3 collective-permute-start.4
  13.5 3.6 %collective-permute-done.4.got.refs_14_ = f32[24,256]{1,0:T(8,128)S(1)} collective-permute-done((f32[24,256]{1,0:T(8,128)S(1)}, f32[24,256]{1,0:T(8,128)S(1)}, u32[]{:S(2)}, u32[]{:S(2)}) %collective-permute-start.4) | collective-permute-done | bytes 24608 | tf_op jit(solution)/shard_map/ppermute | solution.py:782
  17.1 1.6 %collective-permute-start.5 = (f32[1,4,256]{2,1,0:T(4,128)S(1)}, f32[1,4,256]{2,1,0:T(4,128)S(1)}, u32[]{:S(2)}, u32[]{:S(2)}) collective-permute-start(f32[1,4,256]{2,1,0:T(4,128)S(1)} %first_sum.1.a.refs_15_), channel_id=1, source_target_pairs={{0,4},{4,0},{8,12},{12,8},{1,5},{5,1},{9,13},{13,9},{2,6},{6,2},{1... | collective-permute-start | bytes 12296 | tf_op jit(solution)/shard_map/ppermute | solution.py:101
  18.7 2.0 %collective-permute-done.5.b.refs_16_ = f32[1,4,256]{2,1,0:T(4,128)S(1)} collective-permute-done((f32[1,4,256]{2,1,0:T(4,128)S(1)}, f32[1,4,256]{2,1,0:T(4,128)S(1)}, u32[]{:S(2)}, u32[]{:S(2)}) %collective-permute-start.5) | collective-permute-done | bytes 4128 | tf_op jit(solution)/shard_map/ppermute | solution.py:101
  20.7 2.6 %collective-permute-start.6 = (f32[2,4,256]{2,1,0:T(4,128)S(1)}, f32[2,4,256]{2,1,0:T(4,128)S(1)}, u32[]{:S(2)}, u32[]{:S(2)}) collective-permute-start(f32[2,4,256]{2,1,0:T(4,128)S(1)} %joined.3), channel_id=1, source_target_pairs={{0,8},{4,12},{8,0},{12,4},{1,9},{5,13},{9,1},{13,5},{2,10},{6,14},... | collective-permute-start | bytes 24584 | tf_op jit(solution)/shard_map/ppermute | solution.py:101
  23.3 1.6 %collective-permute-start = (s32[1,4]{1,0:T(1,128)S(1)}, s32[1,4]{1,0:T(1,128)S(1)}, u32[]{:S(2)}, u32[]{:S(2)}) collective-permute-start(s32[1,4]{1,0:T(1,128)S(1)} %bitcast.15), channel_id=1, source_target_pairs={{0,4},{4,0},{8,12},{12,8},{1,5},{5,1},{9,13},{13,9},{2,6},{6,2},{1... | collective-permute-start | bytes 56 | tf_op jit(solution)/shard_map/ppermute | solution.py:101
  24.9 0.0 copy-done.1
  24.9 0.0 copy-done.2
  24.9 0.0 copy-done.3
  24.9 0.0 copy-done.4
  24.9 0.0 copy-done.5
  24.9 0.0 copy-start.11
  24.9 2.4 %prepare.1 = (bf16[2,256,256]{2,1,0:T(8,128)(2,1)S(1)}, bf16[2,256,256]{2,1,0:T(8,128)(2,1)S(1)}, bf16[4,256,256]{2,1,0:T(8,128)(2,1)S(1)}, bf16[4,256,256]{2,1,...) custom-call(f32[256,256]{1,0:T(8,128)S(1)} %copy-done.1, f32[256,256]{1,0:T(8,128)S(1)} %copy-done.2, ...), custom_call_target="tpu_custom_call" | custom-call | tf_op jit(solution)/shard_map/prepare/pallas_call | solution.py:175
  27.3 0.0 collective-permute-done.b.refs_2_
  27.3 0.4 collective-permute-start.1
  27.7 4.1 %collective-permute-done.1.refs_3_ = s32[2,4]{1,0:T(2,128)S(1)} collective-permute-done((s32[2,4]{1,0:T(2,128)S(1)}, s32[2,4]{1,0:T(2,128)S(1)}, u32[]{:S(2)}, u32[]{:S(2)}) %collective-permute-start.1) | collective-permute-done | bytes 64 | tf_op jit(solution)/shard_map/ppermute | solution.py:101
  31.8 1.7 %recursion.1.gram.refs_4_ = f32[256,256]{1,0:T(8,128)S(1)} custom-call(s32[1]{0:T(128)} %bitcast.refs_0_, s32[1,4]{1,0:T(1,128)S(1)} %bitcast.17, s32[1,4]{1,0:T(1,128)S(1)} %collective-permute-done.b.refs_2_, s32[2,4]{1,0:T(2,128)S(1)} %collective-permute-done.1.refs_3_, bf16[4,256,256]{2,1,0:T(8,128)(2,1)S(1)} %get-tuple-element.17.refs_4_.refs_10_, ...), custom_call_target="tpu_custom_call" | custom-call | tf_op jit(solution)/shard_map/recursion/pallas_call | solution.py:331
  33.5 4.0 %factor_top.1 = (f32[128,256]{1,0:T(8,128)S(1)}, bf16[128,256]{1,0:T(8,128)(2,1)S(1)}, bf16[128,256]{1,0:T(8,128)(2,1)S(1)}) custom-call(f32[256,256]{1,0:T(8,128)S(1)} %recursion.1.gram.refs_4_), custom_call_target="tpu_custom_call" | custom-call | tf_op jit(solution)/shard_map/factor_top/pallas_call | solution.py:349
  37.6 0.0 collective-permute-done.6.refs_17_
  37.6 0.0 copy-done.11
  37.6 5.7 %factor.1 = (f32[256,256]{1,0:T(8,128)}, f32[4,256]{1,0:T(4,128)}, f32[9,1,32]{2,1,0:T(1,128)}) custom-call(s32[1]{0:T(128)} %bitcast.refs_0_, s32[1,4]{1,0:T(1,128)S(1)} %bitcast.18, s32[1,4]{1,0:T(1,128)S(1)} %collective-permute-done.b.refs_2_, s32[2,4]{1,0:T(2,128)S(1)} %collective-permute-done.1.refs_3_, f32[256,256]{1,0:T(8,128)S(1)} %recursion.1.gram.refs_4_, ...), custom_call_target="tpu_custom_call" | custom-call | tf_op jit(solution)/shard_map/factor/pallas_call | solution.py:442
  (4 shorter events, 0.0 us)
Async XLA Ops:
  0.6 4.7 %copy-start.9 = (s32[4]{0:T(128)S(1)}, s32[4]{0:T(128)}, u32[]{:S(2)}) copy-start(s32[4]{0:T(128)} %refs_0_.3) | copy-start | bytes 52
  0.6 4.7 %copy-start.7 = (f32[32,9]{0,1:T(8,128)S(1)}, f32[32,9]{0,1:T(8,128)}, u32[]{:S(2)}) copy-start(f32[32,9]{0,1:T(8,128)} %param.14) | copy-start | bytes 3460
  0.7 4.7 %copy-start.6 = (f32[32,256]{1,0:T(8,128)S(1)}, f32[32,256]{1,0:T(8,128)}, u32[]{:S(2)}) copy-start(f32[32,256]{1,0:T(8,128)} %pooling.1) | copy-start | bytes 98308
  0.7 9.7 %copy-start.8 = (f32[256,32]{0,1:T(8,128)S(1)}, f32[256,32]{0,1:T(8,128)}, u32[]{:S(2)}) copy-start(f32[256,32]{0,1:T(8,128)} %param.16) | copy-start | bytes 98308
  2.1 9.5 %copy-start = (bf16[1280,128]{1,0:T(8,128)(2,1)S(1)}, bf16[1280,128]{1,0:T(8,128)(2,1)}, u32[]{:S(2)}) copy-start(bf16[1280,128]{1,0:T(8,128)(2,1)} %constant.15.clone.refs_7_) | copy-start | bytes 983044
  2.1 9.5 %copy-start.10 = (f32[16,128]{1,0:T(8,128)S(1)}, f32[16,128]{1,0:T(8,128)}, u32[]{:S(2)}) copy-start(f32[16,128]{1,0:T(8,128)} %constant.16.clone.refs_8_) | copy-start | bytes 24580
  2.2 22.6 %copy-start.1 = (f32[256,256]{1,0:T(8,128)S(1)}, f32[256,256]{1,0:T(8,128)}, u32[]{:S(2)}) copy-start(f32[256,256]{1,0:T(8,128)} %refs_0_.2) | copy-start | bytes 786436
  2.3 22.6 %copy-start.2 = (f32[256,256]{1,0:T(8,128)S(1)}, f32[256,256]{1,0:T(8,128)}, u32[]{:S(2)}) copy-start(f32[256,256]{1,0:T(8,128)} %refs_1_.2) | copy-start | bytes 786436
  2.3 22.6 %copy-start.3 = (f32[256,256]{1,0:T(8,128)S(1)}, f32[256,256]{1,0:T(8,128)}, u32[]{:S(2)}) copy-start(f32[256,256]{1,0:T(8,128)} %refs_2_.2) | copy-start | bytes 786436
  2.3 22.6 %copy-start.4 = (f32[256,256]{1,0:T(8,128)S(1)}, f32[256,256]{1,0:T(8,128)}, u32[]{:S(2)}) copy-start(f32[256,256]{1,0:T(8,128)} %refs_3_.2) | copy-start | bytes 786436
  2.3 22.6 %copy-start.5 = (f32[256,256]{1,0:T(8,128)S(1)}, f32[256,256]{1,0:T(8,128)}, u32[]{:S(2)}) copy-start(f32[256,256]{1,0:T(8,128)} %refs_4_.1) | copy-start | bytes 786436
  2.3 8.1 %collective-permute-start.2 = (bf16[4,2,32,256]{3,2,1,0:T(8,128)(2,1)S(1)}, bf16[4,2,32,256]{3,2,1,0:T(8,128)(2,1)S(1)}, u32[]{:S(2)}, u32[]{:S(2)}) collective-permute-start(bf16[4,2,32,256]{3,2,1,0:T(8,128)(2,1)S(1)} %slice_select_fusion), channel_id=1, source_target_pairs={{0,2},{2,0},{1,3},{3,1},{4,6},{6,4},{5,7},{7,5},{8,10},{10,8},{9,1... | collective-permute-start | bytes 393224 | tf_op jit(solution)/shard_map/ppermute | solution.py:773
  11.6 1.5 %collective-permute-start.3 = (f32[4,256]{1,0:T(4,128)S(1)}, f32[4,256]{1,0:T(4,128)S(1)}, u32[]{:S(2)}, u32[]{:S(2)}) collective-permute-start(f32[4,256]{1,0:T(4,128)S(1)} %gain_sums.1.mine), channel_id=1, source_target_pairs={{0,1},{1,0},{2,3},{3,2},{4,5},{5,4},{6,7},{7,6},{8,9},{9,8},{10,11... | collective-permute-start | bytes 12296 | tf_op jit(solution)/shard_map/ppermute | solution.py:782
  13.2 3.9 %collective-permute-start.4 = (f32[24,256]{1,0:T(8,128)S(1)}, f32[24,256]{1,0:T(8,128)S(1)}, u32[]{:S(2)}, u32[]{:S(2)}) collective-permute-start(f32[24,256]{1,0:T(8,128)S(1)} %packed.1.mine.refs_13_), channel_id=1, source_target_pairs={{0,2},{2,0},{1,3},{3,1},{4,6},{6,4},{5,7},{7,5},{8,10},{10,8},{9,1... | collective-permute-start | bytes 73736 | tf_op jit(solution)/shard_map/ppermute | solution.py:782
  17.1 3.6 %collective-permute-start.5 = (f32[1,4,256]{2,1,0:T(4,128)S(1)}, f32[1,4,256]{2,1,0:T(4,128)S(1)}, u32[]{:S(2)}, u32[]{:S(2)}) collective-permute-start(f32[1,4,256]{2,1,0:T(4,128)S(1)} %first_sum.1.a.refs_15_), channel_id=1, source_target_pairs={{0,4},{4,0},{8,12},{12,8},{1,5},{5,1},{9,13},{13,9},{2,6},{6,2},{1... | collective-permute-start | bytes 12296 | tf_op jit(solution)/shard_map/ppermute | solution.py:101
  20.7 16.9 %collective-permute-start.6 = (f32[2,4,256]{2,1,0:T(4,128)S(1)}, f32[2,4,256]{2,1,0:T(4,128)S(1)}, u32[]{:S(2)}, u32[]{:S(2)}) collective-permute-start(f32[2,4,256]{2,1,0:T(4,128)S(1)} %joined.3), channel_id=1, source_target_pairs={{0,8},{4,12},{8,0},{12,4},{1,9},{5,13},{9,1},{13,5},{2,10},{6,14},... | collective-permute-start | bytes 24584 | tf_op jit(solution)/shard_map/ppermute | solution.py:101
  23.3 4.0 %collective-permute-start = (s32[1,4]{1,0:T(1,128)S(1)}, s32[1,4]{1,0:T(1,128)S(1)}, u32[]{:S(2)}, u32[]{:S(2)}) collective-permute-start(s32[1,4]{1,0:T(1,128)S(1)} %bitcast.15), channel_id=1, source_target_pairs={{0,4},{4,0},{8,12},{12,8},{1,5},{5,1},{9,13},{13,9},{2,6},{6,2},{1... | collective-permute-start | bytes 56 | tf_op jit(solution)/shard_map/ppermute | solution.py:101
  24.9 12.7 %copy-start.11 = (f32[256]{0:T(256)S(1)}, f32[256]{0:T(256)}, u32[]{:S(2)}) copy-start(f32[256]{0:T(256)} %param.21) | copy-start | bytes 3076
  27.3 4.5 %collective-permute-start.1 = (s32[2,4]{1,0:T(2,128)S(1)}, s32[2,4]{1,0:T(2,128)S(1)}, u32[]{:S(2)}, u32[]{:S(2)}) collective-permute-start(s32[2,4]{1,0:T(2,128)S(1)} %joined.2), channel_id=1, source_target_pairs={{0,8},{4,12},{8,0},{12,4},{1,9},{5,13},{9,1},{13,5},{2,10},{6,14},... | collective-permute-start | bytes 104 | tf_op jit(solution)/shard_map/ppermute | solution.py:101

commit v7 on v6

--- a/solution.py
+++ b/solution.py
@@ -201,8 +201,11 @@
         start = first * LANES
         panel = gram[top : top + PANEL, start:]
         if top:
-            left = (high[:top, top : top + PANEL], low[:top, top : top + PANEL])
-            panel = panel - three_pass(left, (high[:top, start:], low[:top, start:]), TN)
+            for rows in (slice(0, top - PANEL), slice(top - PANEL, top)):
+                if rows.stop:
+                    left = (high[rows, top : top + PANEL], low[rows, top : top + PANEL])
+                    right = (high[rows, start:], low[rows, start:])
+                    panel = panel - three_pass(left, right, TN)
         places = range(halves - first)
         part = [
             [

time: 43.4 us -> 43.4 us (level)
  no operation moved by 1% of the time
where the time goes in v7:
time: 43.4 us; the launch traced here: 43.2 us
  Pallas kernels  21.4 us (49%)
  waiting for transfers between devices  9.81 us (23%)
  starting transfers between devices  9.44 us (22%)
  local copies, waits for them, and re-layouts  1.61 us (4%)
  between operations  0.87 us (2%)
    ppermute x4, waiting for transfers between devices, history(): lax.ppermute(sent, axis, [(i, i ^ reach) for i in range(count)])  6.17 us
    ppermute x4, starting transfers between devices, history(): lax.ppermute(sent, axis, [(i, i ^ reach) for i in range(count)])  6.14 us
    pallas_call x1, Pallas kernels, factor(): pl.pallas_call(kernel, out_shape=(jax.ShapeDtypeStruct((size, size), F32)...  5.58 us
    pallas_call x1, Pallas kernels, frame_sums(): pl.pallas_call(kernel, out_shape=(pltpu.VMEM((steps, channels, LANES), F3...  5 us
    pallas_call x1, Pallas kernels, factor_top(): pl.pallas_call(factor_top_kernel, out_shape=(pltpu.VMEM((rows, size), F32...  4.04 us
    ppermute x2, waiting for transfers between devices, partner(): return lax.ppermute(value, axis, [(0, 1), (1, 0)])  3.63 us
    ppermute x1, starting transfers between devices, beside(): got = lax.ppermute(sent, axis, [(0, 1), (1, 0)])  3.03 us
    pallas_call x1, Pallas kernels, prepare(): pl.pallas_call(kernel, out_shape=(pltpu.VMEM((2, size, size), BF16), pltp...  2.37 us
  transfers between devices with their start and end apart: 7, of which 3 were waited for; matrix products, arithmetic and copies ran while one was open for 0% of the time, Pallas kernels for 34%

profile of v7, /device:TPU:0, one launch (start us, length us, event | category | flops | bytes accessed | tf_op | source)
XLA Modules:
  0.0 43.2 jit_solution(6617828402775715717)
XLA Ops:
  0.6 0.0 copy-start.9
  0.6 0.0 copy-start.7
  0.7 0.0 copy-start.6
  0.7 0.0 copy-start.8
  0.7 1.4 %fusion = (bf16[4,32,4,256]{3,2,1,0:T(4,128)(2,1)S(1)}, bf16[4,32,4,256]{3,2,1,0:T(4,128)(2,1)S(1)}) fusion(bf16[4,32,32,256]{3,2,1,0:T(8,128)(2,1)} %refs_2_.3), kind=kLoop, calls=%fused_computation.3 | loop fusion | bytes 1048576 | tf_op jit(solution)/shard_map/slice | solution.py:812
  2.1 0.0 copy-start
  2.1 0.0 copy-start.10
  2.1 0.1 copy_bitcast_fusion
  2.2 0.0 copy-start.1
  2.3 0.0 copy-start.2
  2.3 0.0 copy-start.3
  2.3 0.0 copy-start.4
  2.3 0.0 copy-start.5
  2.3 3.0 %collective-permute-start.2 = (bf16[4,2,32,256]{3,2,1,0:T(8,128)(2,1)S(1)}, bf16[4,2,32,256]{3,2,1,0:T(8,128)(2,1)S(1)}, u32[]{:S(2)}, u32[]{:S(2)}) collective-permute-start(bf16[4,2,32,256]{3,2,1,0:T(8,128)(2,1)S(1)} %slice_select_fusion), channel_id=1, source_target_pairs={{0,2},{2,0},{1,3},{3,1},{4,6},{6,4},{5,7},{7,5},{8,10},{10,8},{9,1... | collective-permute-start | bytes 393224 | tf_op jit(solution)/shard_map/ppermute | solution.py:776
  5.4 0.0 copy-done.9
  5.4 0.0 copy-done.7
  5.4 0.0 copy-done.6
  5.4 5.0 %frame_sums.1 = (f32[4,32,128]{2,1,0:T(8,128)S(1)}, f32[32,1024]{1,0:T(8,128)S(1)}) custom-call(f32[9,32]{1,0:T(8,128)S(1)} %bitcast.11, s32[4]{0:T(128)S(1)} %copy-done.9, bf16[4,32,32,256]{3,2,1,0:T(8,128)(2,1)} %refs_2_.3, f32[32,256]{1,0:T(8,128)S(1)} %copy-done.6), custom_call_target="tpu_custom_call" | custom-call | tf_op jit(solution)/shard_map/frame_sums/pallas_call | solution.py:585
  10.4 0.0 collective-permute-done.2.above.below.refs_3_.refs_4_
  10.4 0.0 copy-done.8
  10.4 1.2 %gain_sums.1.mine = f32[4,256]{1,0:T(4,128)S(1)} custom-call(s32[4]{0:T(128)S(1)} %copy-done.9, bf16[4,2,32,256]{3,2,1,0:T(8,128)(2,1)S(1)} %collective-permute-done.2.above.below.refs_3_.refs_4_, bf16[4,2,32,256]{3,2,1,0:T(8,128)(2,1)S(1)} %collective-permute-done.2.above.below.refs_3_.refs_4_, f32[4,32,128]{2,1,0:T(8,128)S(1)} %get-tuple-element.26.part, ...), custom_call_target="tpu_custom_call" | custom-call | tf_op jit(solution)/shard_map/gain_sums/pallas_call | solution.py:690
  11.6 0.0 collective-permute-start.3
  11.6 0.0 copy-done
  11.6 0.0 copy-done.10
  11.7 1.5 %tap_sums.1.gradient = f32[9,32]{1,0:T(8,128)S(1)} custom-call(s32[4]{0:T(128)S(1)} %copy-done.9, bf16[4,4,32,256]{3,2,1,0:T(8,128)(2,1)S(1)} %get-tuple-element.33.refs_1_, bf16[4,4,32,256]{3,2,1,0:T(8,128)(2,1)S(1)} %get-tuple-element.34.refs_2_, bf16[4,2,32,256]{3,2,1,0:T(8,128)(2,1)S(1)} %collective-permute-done.2.above.below.refs_3_.refs_4_, ...), custom_call_target="tpu_custom_call" | custom-call | tf_op jit(solution)/shard_map/tap_sums/pallas_call | solution.py:761
  13.1 0.0 collective-permute-done.3.got
  13.1 0.1 packed.1.mine.refs_13_
  13.2 0.3 collective-permute-start.4
  13.5 3.6 %collective-permute-done.4.got.refs_14_ = f32[24,256]{1,0:T(8,128)S(1)} collective-permute-done((f32[24,256]{1,0:T(8,128)S(1)}, f32[24,256]{1,0:T(8,128)S(1)}, u32[]{:S(2)}, u32[]{:S(2)}) %collective-permute-start.4) | collective-permute-done | bytes 24608 | tf_op jit(solution)/shard_map/ppermute | solution.py:785
  17.1 1.6 %collective-permute-start.5 = (f32[1,4,256]{2,1,0:T(4,128)S(1)}, f32[1,4,256]{2,1,0:T(4,128)S(1)}, u32[]{:S(2)}, u32[]{:S(2)}) collective-permute-start(f32[1,4,256]{2,1,0:T(4,128)S(1)} %first_sum.1.a.refs_15_), channel_id=1, source_target_pairs={{0,4},{4,0},{8,12},{12,8},{1,5},{5,1},{9,13},{13,9},{2,6},{6,2},{1... | collective-permute-start | bytes 12296 | tf_op jit(solution)/shard_map/ppermute | solution.py:101
  18.7 2.0 %collective-permute-done.5.b.refs_16_ = f32[1,4,256]{2,1,0:T(4,128)S(1)} collective-permute-done((f32[1,4,256]{2,1,0:T(4,128)S(1)}, f32[1,4,256]{2,1,0:T(4,128)S(1)}, u32[]{:S(2)}, u32[]{:S(2)}) %collective-permute-start.5) | collective-permute-done | bytes 4128 | tf_op jit(solution)/shard_map/ppermute | solution.py:101
  20.7 2.6 %collective-permute-start.6 = (f32[2,4,256]{2,1,0:T(4,128)S(1)}, f32[2,4,256]{2,1,0:T(4,128)S(1)}, u32[]{:S(2)}, u32[]{:S(2)}) collective-permute-start(f32[2,4,256]{2,1,0:T(4,128)S(1)} %joined.3), channel_id=1, source_target_pairs={{0,8},{4,12},{8,0},{12,4},{1,9},{5,13},{9,1},{13,5},{2,10},{6,14},... | collective-permute-start | bytes 24584 | tf_op jit(solution)/shard_map/ppermute | solution.py:101
  23.3 1.6 %collective-permute-start = (s32[1,4]{1,0:T(1,128)S(1)}, s32[1,4]{1,0:T(1,128)S(1)}, u32[]{:S(2)}, u32[]{:S(2)}) collective-permute-start(s32[1,4]{1,0:T(1,128)S(1)} %bitcast.15), channel_id=1, source_target_pairs={{0,4},{4,0},{8,12},{12,8},{1,5},{5,1},{9,13},{13,9},{2,6},{6,2},{1... | collective-permute-start | bytes 56 | tf_op jit(solution)/shard_map/ppermute | solution.py:101
  24.9 0.0 copy-done.1
  24.9 0.0 copy-done.2
  24.9 0.0 copy-done.3
  24.9 0.0 copy-done.4
  24.9 0.0 copy-done.5
  24.9 0.0 copy-start.11
  24.9 2.4 %prepare.1 = (bf16[2,256,256]{2,1,0:T(8,128)(2,1)S(1)}, bf16[2,256,256]{2,1,0:T(8,128)(2,1)S(1)}, bf16[4,256,256]{2,1,0:T(8,128)(2,1)S(1)}, bf16[4,256,256]{2,1,...) custom-call(f32[256,256]{1,0:T(8,128)S(1)} %copy-done.1, f32[256,256]{1,0:T(8,128)S(1)} %copy-done.2, ...), custom_call_target="tpu_custom_call" | custom-call | tf_op jit(solution)/shard_map/prepare/pallas_call | solution.py:175
  27.3 0.0 collective-permute-done.b.refs_2_
  27.3 0.4 collective-permute-start.1
  27.7 4.1 %collective-permute-done.1.refs_3_ = s32[2,4]{1,0:T(2,128)S(1)} collective-permute-done((s32[2,4]{1,0:T(2,128)S(1)}, s32[2,4]{1,0:T(2,128)S(1)}, u32[]{:S(2)}, u32[]{:S(2)}) %collective-permute-start.1) | collective-permute-done | bytes 64 | tf_op jit(solution)/shard_map/ppermute | solution.py:101
  31.8 1.7 %recursion.1.gram.refs_4_ = f32[256,256]{1,0:T(8,128)S(1)} custom-call(s32[1]{0:T(128)} %bitcast.refs_0_, s32[1,4]{1,0:T(1,128)S(1)} %bitcast.17, s32[1,4]{1,0:T(1,128)S(1)} %collective-permute-done.b.refs_2_, s32[2,4]{1,0:T(2,128)S(1)} %collective-permute-done.1.refs_3_, bf16[4,256,256]{2,1,0:T(8,128)(2,1)S(1)} %get-tuple-element.17.refs_4_.refs_10_, ...), custom_call_target="tpu_custom_call" | custom-call | tf_op jit(solution)/shard_map/recursion/pallas_call | solution.py:334
  33.5 4.0 %factor_top.1 = (f32[128,256]{1,0:T(8,128)S(1)}, bf16[128,256]{1,0:T(8,128)(2,1)S(1)}, bf16[128,256]{1,0:T(8,128)(2,1)S(1)}) custom-call(f32[256,256]{1,0:T(8,128)S(1)} %recursion.1.gram.refs_4_), custom_call_target="tpu_custom_call" | custom-call | tf_op jit(solution)/shard_map/factor_top/pallas_call | solution.py:352
  37.6 0.0 collective-permute-done.6.refs_17_
  37.6 0.0 copy-done.11
  37.6 5.6 %factor.1 = (f32[256,256]{1,0:T(8,128)}, f32[4,256]{1,0:T(4,128)}, f32[9,1,32]{2,1,0:T(1,128)}) custom-call(s32[1]{0:T(128)} %bitcast.refs_0_, s32[1,4]{1,0:T(1,128)S(1)} %bitcast.18, s32[1,4]{1,0:T(1,128)S(1)} %collective-permute-done.b.refs_2_, s32[2,4]{1,0:T(2,128)S(1)} %collective-permute-done.1.refs_3_, f32[256,256]{1,0:T(8,128)S(1)} %recursion.1.gram.refs_4_, ...), custom_call_target="tpu_custom_call" | custom-call | tf_op jit(solution)/shard_map/factor/pallas_call | solution.py:445
  (4 shorter events, 0.0 us)
Async XLA Ops:
  0.6 4.7 %copy-start.9 = (s32[4]{0:T(128)S(1)}, s32[4]{0:T(128)}, u32[]{:S(2)}) copy-start(s32[4]{0:T(128)} %refs_0_.3) | copy-start | bytes 52
  0.6 4.7 %copy-start.7 = (f32[32,9]{0,1:T(8,128)S(1)}, f32[32,9]{0,1:T(8,128)}, u32[]{:S(2)}) copy-start(f32[32,9]{0,1:T(8,128)} %param.14) | copy-start | bytes 3460
  0.7 4.7 %copy-start.6 = (f32[32,256]{1,0:T(8,128)S(1)}, f32[32,256]{1,0:T(8,128)}, u32[]{:S(2)}) copy-start(f32[32,256]{1,0:T(8,128)} %pooling.1) | copy-start | bytes 98308
  0.7 9.7 %copy-start.8 = (f32[256,32]{0,1:T(8,128)S(1)}, f32[256,32]{0,1:T(8,128)}, u32[]{:S(2)}) copy-start(f32[256,32]{0,1:T(8,128)} %param.16) | copy-start | bytes 98308
  2.1 9.5 %copy-start = (bf16[1280,128]{1,0:T(8,128)(2,1)S(1)}, bf16[1280,128]{1,0:T(8,128)(2,1)}, u32[]{:S(2)}) copy-start(bf16[1280,128]{1,0:T(8,128)(2,1)} %constant.15.clone.refs_7_) | copy-start | bytes 983044
  2.1 9.5 %copy-start.10 = (f32[16,128]{1,0:T(8,128)S(1)}, f32[16,128]{1,0:T(8,128)}, u32[]{:S(2)}) copy-start(f32[16,128]{1,0:T(8,128)} %constant.16.clone.refs_8_) | copy-start | bytes 24580
  2.2 22.6 %copy-start.1 = (f32[256,256]{1,0:T(8,128)S(1)}, f32[256,256]{1,0:T(8,128)}, u32[]{:S(2)}) copy-start(f32[256,256]{1,0:T(8,128)} %refs_0_.2) | copy-start | bytes 786436
  2.3 22.6 %copy-start.2 = (f32[256,256]{1,0:T(8,128)S(1)}, f32[256,256]{1,0:T(8,128)}, u32[]{:S(2)}) copy-start(f32[256,256]{1,0:T(8,128)} %refs_1_.2) | copy-start | bytes 786436
  2.3 22.6 %copy-start.3 = (f32[256,256]{1,0:T(8,128)S(1)}, f32[256,256]{1,0:T(8,128)}, u32[]{:S(2)}) copy-start(f32[256,256]{1,0:T(8,128)} %refs_2_.2) | copy-start | bytes 786436
  2.3 22.6 %copy-start.4 = (f32[256,256]{1,0:T(8,128)S(1)}, f32[256,256]{1,0:T(8,128)}, u32[]{:S(2)}) copy-start(f32[256,256]{1,0:T(8,128)} %refs_3_.2) | copy-start | bytes 786436
  2.3 22.6 %copy-start.5 = (f32[256,256]{1,0:T(8,128)S(1)}, f32[256,256]{1,0:T(8,128)}, u32[]{:S(2)}) copy-start(f32[256,256]{1,0:T(8,128)} %refs_4_.1) | copy-start | bytes 786436
  2.3 8.1 %collective-permute-start.2 = (bf16[4,2,32,256]{3,2,1,0:T(8,128)(2,1)S(1)}, bf16[4,2,32,256]{3,2,1,0:T(8,128)(2,1)S(1)}, u32[]{:S(2)}, u32[]{:S(2)}) collective-permute-start(bf16[4,2,32,256]{3,2,1,0:T(8,128)(2,1)S(1)} %slice_select_fusion), channel_id=1, source_target_pairs={{0,2},{2,0},{1,3},{3,1},{4,6},{6,4},{5,7},{7,5},{8,10},{10,8},{9,1... | collective-permute-start | bytes 393224 | tf_op jit(solution)/shard_map/ppermute | solution.py:776
  11.6 1.5 %collective-permute-start.3 = (f32[4,256]{1,0:T(4,128)S(1)}, f32[4,256]{1,0:T(4,128)S(1)}, u32[]{:S(2)}, u32[]{:S(2)}) collective-permute-start(f32[4,256]{1,0:T(4,128)S(1)} %gain_sums.1.mine), channel_id=1, source_target_pairs={{0,1},{1,0},{2,3},{3,2},{4,5},{5,4},{6,7},{7,6},{8,9},{9,8},{10,11... | collective-permute-start | bytes 12296 | tf_op jit(solution)/shard_map/ppermute | solution.py:785
  13.2 3.9 %collective-permute-start.4 = (f32[24,256]{1,0:T(8,128)S(1)}, f32[24,256]{1,0:T(8,128)S(1)}, u32[]{:S(2)}, u32[]{:S(2)}) collective-permute-start(f32[24,256]{1,0:T(8,128)S(1)} %packed.1.mine.refs_13_), channel_id=1, source_target_pairs={{0,2},{2,0},{1,3},{3,1},{4,6},{6,4},{5,7},{7,5},{8,10},{10,8},{9,1... | collective-permute-start | bytes 73736 | tf_op jit(solution)/shard_map/ppermute | solution.py:785
  17.1 3.6 %collective-permute-start.5 = (f32[1,4,256]{2,1,0:T(4,128)S(1)}, f32[1,4,256]{2,1,0:T(4,128)S(1)}, u32[]{:S(2)}, u32[]{:S(2)}) collective-permute-start(f32[1,4,256]{2,1,0:T(4,128)S(1)} %first_sum.1.a.refs_15_), channel_id=1, source_target_pairs={{0,4},{4,0},{8,12},{12,8},{1,5},{5,1},{9,13},{13,9},{2,6},{6,2},{1... | collective-permute-start | bytes 12296 | tf_op jit(solution)/shard_map/ppermute | solution.py:101
  20.7 16.9 %collective-permute-start.6 = (f32[2,4,256]{2,1,0:T(4,128)S(1)}, f32[2,4,256]{2,1,0:T(4,128)S(1)}, u32[]{:S(2)}, u32[]{:S(2)}) collective-permute-start(f32[2,4,256]{2,1,0:T(4,128)S(1)} %joined.3), channel_id=1, source_target_pairs={{0,8},{4,12},{8,0},{12,4},{1,9},{5,13},{9,1},{13,5},{2,10},{6,14},... | collective-permute-start | bytes 24584 | tf_op jit(solution)/shard_map/ppermute | solution.py:101
  23.3 4.0 %collective-permute-start = (s32[1,4]{1,0:T(1,128)S(1)}, s32[1,4]{1,0:T(1,128)S(1)}, u32[]{:S(2)}, u32[]{:S(2)}) collective-permute-start(s32[1,4]{1,0:T(1,128)S(1)} %bitcast.15), channel_id=1, source_target_pairs={{0,4},{4,0},{8,12},{12,8},{1,5},{5,1},{9,13},{13,9},{2,6},{6,2},{1... | collective-permute-start | bytes 56 | tf_op jit(solution)/shard_map/ppermute | solution.py:101
  24.9 12.7 %copy-start.11 = (f32[256]{0:T(256)S(1)}, f32[256]{0:T(256)}, u32[]{:S(2)}) copy-start(f32[256]{0:T(256)} %param.21) | copy-start | bytes 3076
  27.3 4.5 %collective-permute-start.1 = (s32[2,4]{1,0:T(2,128)S(1)}, s32[2,4]{1,0:T(2,128)S(1)}, u32[]{:S(2)}, u32[]{:S(2)}) collective-permute-start(s32[2,4]{1,0:T(2,128)S(1)} %joined.2), channel_id=1, source_target_pairs={{0,8},{4,12},{8,0},{12,4},{1,9},{5,13},{9,1},{13,5},{2,10},{6,14},... | collective-permute-start | bytes 104 | tf_op jit(solution)/shard_map/ppermute | solution.py:101
